TPU v7x, 32 devices: a whole 2x2x4 slice. The times are simulated.
32 devices in a mesh: dp: 8 (over z, x), tensor: 4 (over y, core).
Axes of the slice: x: 2, y: 2, z: 4, core: 2. Of those that a mesh axis runs over, the one named last changes fastest.
Arguments:
- hidden_in: bfloat16 [32768, 768], P(('dp', 'tensor')), may hold values from -6 to 6
- teacher: float32 [32768, 768], P(('dp', 'tensor')), may hold values from -6 to 6
- valid_mask: int32 [32768], P(('dp', 'tensor')), may hold values from 0 to 1
- random_blocks: int32 [12, 32, 3, 32], replicated, may hold values from 0 to 1, as said below
- w_qkv: bfloat16 [3, 768, 768], P(None, 'dp', 'tensor'), may hold values from -0.21875 to 0.21875
- b_qv: bfloat16 [2, 12, 64], P(None, 'tensor', 'dp'), may hold values from -3 to 3
- w_out: bfloat16 [768, 768], P('tensor', 'dp'), may hold values from -3 to 3
- w_in: bfloat16 [768, 3072], P('dp', 'tensor'), may hold values from -0.21875 to 0.21875
- b_in: bfloat16 [48, 64], P('tensor', 'dp'), may hold values from -3 to 3
- w_back: bfloat16 [3072, 768], P('tensor', 'dp'), may hold values from -0.109375 to 0.109375
- ln_gains: bfloat16 [2, 768], P(None, 'dp'), may hold values from 0.25 to 1.75
- row_biases: bfloat16 [4, 768], P(None, 'dp'), may hold values from -2 to 2
Outputs:
- loss: float32 [], replicated
- encoded: float32 [32768, 768], P(('dp', 'tensor'))
- grad_in: float32 [32768, 768], P(('dp', 'tensor'))
- grad_qkv: float32 [3, 768, 768], P(None, 'dp', 'tensor')
- grad_qv_bias: float32 [2, 12, 64], P(None, 'tensor', 'dp')
- grad_out: float32 [768, 768], P('tensor', 'dp')
- grad_w_in: float32 [768, 3072], P('dp', 'tensor')
- grad_b_in: float32 [48, 64], P('tensor', 'dp')
- grad_w_back: float32 [3072, 768], P('tensor', 'dp')
- grad_gains: float32 [2, 768], P(None, ('dp', 'tensor'))
- grad_biases: float32 [4, 768], P(None, ('dp', 'tensor'))
Inputs may be any that keep to these rules, and one draw needn't show every extreme that they name: `random_blocks`: each [h, j, r, :] holds a single 1; the 3 blocks chosen for one h and j are different, and none of them is block 0, block 31, or within one block of j.
All inputs are finite; a program needn't handle non-finite values.
Results may differ from a plain program's by a relative error of at most 0.015.
Values may be sent and summed in bfloat16 or wider, within the bound.
A program may use at most 192 MiB of HBM per device.

v0:
```python
import jax
import jax.numpy as jnp
from jax import lax
from jax.sharding import PartitionSpec as P

D = 768
HD = 64
BLK = 64
SEQ_LEN = 2048


epsilon = 1e-06
masked_score = -1e30
exact_precision = lax.Precision.HIGHEST


def layer_norm(values, gain, shift):
    centred = values - jnp.mean(values, axis=-1, keepdims=True)
    variance = jnp.mean(centred * centred, axis=-1, keepdims=True)
    return centred * lax.rsqrt(variance + epsilon) * gain + shift


def gelu_tanh(values):
    return (
        0.5
        * values
        * (1.0 + jnp.tanh(0.7978845608028654 * (values + 0.044715 * values * values * values)))
    )


def fetch_weights(w_qkv, b_qv, w_out, w_in, b_in, w_back, ln_gains, row_biases):
    return (
        lax.all_gather(w_qkv, "dp", axis=1, tiled=True),
        lax.all_gather(b_qv, "dp", axis=2, tiled=True),
        lax.all_gather(w_out, "dp", axis=1, tiled=True),
        lax.all_gather(w_in, "dp", axis=0, tiled=True),
        lax.all_gather(b_in, "dp", axis=1, tiled=True),
        lax.all_gather(w_back, "dp", axis=1, tiled=True),
        lax.all_gather(ln_gains, "dp", axis=1, tiled=True),
        lax.all_gather(row_biases, "dp", axis=1, tiled=True),
    )


def widen_units(in_weight, in_bias, back_weight):
    return (
        lax.all_gather(in_weight, "tensor", axis=1, tiled=True),
        lax.all_gather(in_bias, "tensor", axis=0, tiled=True),
        lax.all_gather(back_weight, "tensor", axis=0, tiled=True),
    )


def gather_slots(blocks, one_hot):
    middle = one_hot.shape[0]
    nearby = jnp.stack([blocks[0:middle], blocks[1 : middle + 1], blocks[2 : middle + 2]], axis=1)
    edges = jnp.broadcast_to(
        jnp.stack([blocks[0], blocks[-1]])[None], (middle, 2) + blocks.shape[1:]
    )
    distant = jnp.einsum(
        "mrn,nbd->mrbd", one_hot, blocks, preferred_element_type=jnp.float32
    ).astype(jnp.bfloat16)
    slots = jnp.concatenate([nearby, edges, distant], axis=1)
    return slots.reshape(middle, -1, blocks.shape[-1])


def slot_valid(middle, width):
    slot_ids = jnp.arange(width) // BLK
    row_ids = jnp.arange(middle)[:, None]
    first_double = (slot_ids[None, :] == 3) & (row_ids == 0)
    last_double = (slot_ids[None, :] == 4) & (row_ids == middle - 1)
    return jnp.logical_not(first_double | last_double)[:, None, :]


def spread_slots(slot_grads, one_hot):
    middle = slot_grads.shape[0]
    parts_grad = slot_grads.reshape(middle, -1, BLK, slot_grads.shape[-1])
    nearby = (
        jnp.pad(parts_grad[:, 0], ((0, 2), (0, 0), (0, 0)))
        + jnp.pad(parts_grad[:, 1], ((1, 1), (0, 0), (0, 0)))
        + jnp.pad(parts_grad[:, 2], ((2, 0), (0, 0), (0, 0)))
    )
    edges = jnp.concatenate(
        [
            jnp.sum(parts_grad[:, 3], axis=0)[None],
            jnp.zeros((middle,) + parts_grad.shape[2:], jnp.float32),
            jnp.sum(parts_grad[:, 4], axis=0)[None],
        ],
        axis=0,
    )
    distant = jnp.einsum(
        "mrn,mrbd->nbd", one_hot.astype(jnp.float32), parts_grad[:, 5:], precision=exact_precision
    )
    return nearby + edges + distant


def log_total(scores):
    peak = jnp.max(scores, axis=-1, keepdims=True)
    return peak + jnp.log(jnp.sum(jnp.exp(scores - peak), axis=-1, keepdims=True))


def middle_scores(stack, chosen):
    queries, keys, values = (stack[0], stack[1], stack[2])
    scale = queries.shape[-1] ** (-0.5)
    one_hot = chosen[1:-1].astype(jnp.bfloat16)
    mid_queries = queries[1:-1]
    key_slots = gather_slots(keys, one_hot)
    value_slots = gather_slots(values, one_hot)
    scores = (
        jnp.einsum("mqd,mkd->mqk", mid_queries, key_slots, preferred_element_type=jnp.float32)
        * scale
    )
    scores = jnp.where(slot_valid(mid_queries.shape[0], key_slots.shape[1]), scores, masked_score)
    return (mid_queries, key_slots, value_slots, scores)


def edge_scores_of(stack):
    queries, keys, values = (stack[0], stack[1], stack[2])
    head_dim = queries.shape[-1]
    edge_queries = jnp.concatenate([queries[0], queries[-1]], axis=0)
    flat_keys = keys.reshape(-1, head_dim)
    flat_values = values.reshape(-1, head_dim)
    scores = jnp.einsum(
        "qd,kd->qk", edge_queries, flat_keys, preferred_element_type=jnp.float32
    ) * head_dim ** (-0.5)
    return (edge_queries, flat_keys, flat_values, scores)


def item_forward(stack, chosen):
    mid_queries, key_slots, value_slots, scores = middle_scores(stack, chosen)
    log_middle = log_total(scores)
    shares = jnp.exp(scores - log_middle).astype(jnp.bfloat16)
    context_mid = jnp.einsum(
        "mqk,mkd->mqd", shares, value_slots, preferred_element_type=jnp.float32
    )
    edge_queries, flat_keys, flat_values, edge_scores = edge_scores_of(stack)
    log_edge = log_total(edge_scores)
    edge_shares = jnp.exp(edge_scores - log_edge).astype(jnp.bfloat16)
    context_edge = jnp.dot(edge_shares, flat_values, preferred_element_type=jnp.float32)
    block = stack.shape[2]
    context = jnp.concatenate(
        [context_edge[:block][None], context_mid, context_edge[block:][None]], axis=0
    )
    return (context.astype(jnp.bfloat16), log_middle[..., 0], log_edge[:, 0])


def item_backward(stack, chosen, grad_context, log_middle, log_edge):
    scale = stack.shape[-1] ** (-0.5)
    block = stack.shape[2]
    mid_queries, key_slots, value_slots, scores = middle_scores(stack, chosen)
    shares = jnp.exp(scores - log_middle[..., None])
    grad_mid = grad_context[1:-1]
    grad_shares = jnp.einsum(
        "mqd,mkd->mqk", grad_mid, value_slots, preferred_element_type=jnp.float32
    )
    inner = jnp.sum(shares * grad_shares, axis=-1, keepdims=True)
    grad_scores = (shares * (grad_shares - inner)).astype(jnp.bfloat16)
    grad_query_mid = (
        jnp.einsum("mqk,mkd->mqd", grad_scores, key_slots, preferred_element_type=jnp.float32)
        * scale
    )
    grad_key_slots = (
        jnp.einsum("mqk,mqd->mkd", grad_scores, mid_queries, preferred_element_type=jnp.float32)
        * scale
    )
    grad_value_slots = jnp.einsum(
        "mqk,mqd->mkd", shares.astype(jnp.bfloat16), grad_mid, preferred_element_type=jnp.float32
    )
    edge_queries, flat_keys, flat_values, edge_scores = edge_scores_of(stack)
    edge_shares = jnp.exp(edge_scores - log_edge[:, None])
    grad_edge = jnp.concatenate([grad_context[0], grad_context[-1]], axis=0)
    grad_edge_shares = jnp.einsum(
        "qd,kd->qk", grad_edge, flat_values, preferred_element_type=jnp.float32
    )
    edge_inner = jnp.sum(edge_shares * grad_edge_shares, axis=-1, keepdims=True)
    grad_edge_scores = (edge_shares * (grad_edge_shares - edge_inner)).astype(jnp.bfloat16)
    grad_query_edge = (
        jnp.dot(grad_edge_scores, flat_keys, preferred_element_type=jnp.float32) * scale
    )
    grad_key_edge = (
        jnp.einsum("qk,qd->kd", grad_edge_scores, edge_queries, preferred_element_type=jnp.float32)
        * scale
    )
    grad_value_edge = jnp.einsum(
        "qk,qd->kd", edge_shares.astype(jnp.bfloat16), grad_edge, preferred_element_type=jnp.float32
    )
    one_hot = chosen[1:-1]
    grad_queries = jnp.concatenate(
        [grad_query_edge[:block][None], grad_query_mid, grad_query_edge[block:][None]], axis=0
    )
    grad_keys = spread_slots(grad_key_slots, one_hot) + grad_key_edge.reshape(stack.shape[1:])
    grad_values = spread_slots(grad_value_slots, one_hot) + grad_value_edge.reshape(stack.shape[1:])
    return jnp.stack([grad_queries, grad_keys, grad_values]).astype(jnp.bfloat16)


def run_forward(pair):
    return item_forward(pair[0], pair[1])


def run_backward(group_items):
    return item_backward(
        group_items[0], group_items[1], group_items[2], group_items[3], group_items[4]
    )


def per_device(
    hidden_in,
    teacher,
    valid_mask,
    random_blocks,
    w_qkv,
    b_qv,
    w_out,
    w_in,
    b_in,
    w_back,
    ln_gains,
    row_biases,
):
    local_rows = hidden_in.shape[0]
    tensor_count = lax.axis_size("tensor")
    tokens_total = local_rows * tensor_count * lax.axis_size("dp")
    group_rows = local_rows * tensor_count
    seq_count = group_rows // SEQ_LEN
    blocks_count = SEQ_LEN // BLK
    fetched = fetch_weights(w_qkv, b_qv, w_out, w_in, b_in, w_back, ln_gains, row_biases)
    qkv_weight, bias_pair, out_weight, in_weight, in_bias, back_weight, gains, biases = fetched
    full_in, full_bias, full_back = widen_units(in_weight, in_bias, back_weight)
    head_local = qkv_weight.shape[2] // HD
    chosen_local = lax.dynamic_slice_in_dim(
        random_blocks, lax.axis_index("tensor") * head_local, head_local, 0
    )
    whole_in = lax.all_gather(hidden_in, "tensor", axis=0, tiled=True)
    projected = jnp.einsum("nd,kde->kne", whole_in, qkv_weight, preferred_element_type=jnp.float32)
    bias_flat = bias_pair.astype(jnp.float32).reshape(2, -1)
    bias_rows = jnp.stack([bias_flat[0], jnp.zeros_like(bias_flat[0]), bias_flat[1]])
    projected = (projected + bias_rows[:, None, :]).astype(jnp.bfloat16)
    items = projected.reshape(3, seq_count, blocks_count, BLK, head_local, HD).transpose(
        1, 4, 0, 2, 3, 5
    )
    items = items.reshape(seq_count * head_local, 3, blocks_count, BLK, HD)
    chosen_all = jnp.tile(chosen_local, (seq_count, 1, 1, 1))
    context_items, log_middle, log_edge = lax.map(run_forward, (items, chosen_all))
    context = context_items.reshape(seq_count, head_local, blocks_count, BLK, HD).transpose(
        0, 2, 3, 1, 4
    )
    context = context.reshape(group_rows, head_local * HD)
    piece = context
    attention = lax.psum_scatter(
        jnp.dot(piece, out_weight, preferred_element_type=jnp.float32).astype(jnp.bfloat16),
        "tensor",
        scatter_dimension=0,
        tiled=True,
    ).astype(jnp.float32)
    gain_values = gains.astype(jnp.float32)
    bias_values = biases.astype(jnp.float32)
    mixed = hidden_in.astype(jnp.float32) + attention + bias_values[0]
    normed, first_back = jax.vjp(layer_norm, mixed, gain_values[0], bias_values[1])
    normed_low = normed.astype(jnp.bfloat16)
    inner = jnp.dot(normed_low, full_in, preferred_element_type=jnp.float32) + full_bias.astype(
        jnp.float32
    ).reshape(-1)
    active_float, gelu_back = jax.vjp(gelu_tanh, inner)
    active = active_float.astype(jnp.bfloat16)
    feed = jnp.dot(active, full_back, preferred_element_type=jnp.float32)
    second = normed + feed + bias_values[2]
    encoded, final_back = jax.vjp(layer_norm, second, gain_values[1], bias_values[3])
    mask_rows = valid_mask.astype(jnp.float32)
    error = encoded - teacher
    sum_sq, valid_total = lax.psum(
        (jnp.sum(mask_rows[:, None] * error * error), jnp.sum(mask_rows)), ("dp", "tensor")
    )
    loss = sum_sq / (D * valid_total)
    grad_encoded = mask_rows[:, None] * error * (tokens_total / valid_total)
    grad_second, grad_gain_two, grad_shift_two = final_back(grad_encoded)
    second_low = grad_second.astype(jnp.bfloat16)
    fetched = fetch_weights(w_qkv, b_qv, w_out, w_in, b_in, w_back, ln_gains, row_biases)
    qkv_weight, bias_pair, out_weight, in_weight, in_bias, back_weight, gains, biases = fetched
    full_in, full_bias, full_back = widen_units(in_weight, in_bias, back_weight)
    grad_active = jnp.einsum("nd,fd->nf", second_low, full_back, preferred_element_type=jnp.float32)
    grad_inner = gelu_back(grad_active)[0].astype(jnp.bfloat16)
    grad_in_full = jnp.einsum(
        "nd,nf->df", normed_low, grad_inner, preferred_element_type=jnp.float32
    )
    grad_back_full = jnp.einsum("nf,nd->fd", active, second_low, preferred_element_type=jnp.float32)
    grad_bias_full = jnp.sum(grad_inner, axis=0, dtype=jnp.float32).reshape(-1, 64)
    grad_in_weight, grad_in_bias, grad_back_weight = (
        lax.psum_scatter(
            grad_in_full.astype(jnp.bfloat16), "tensor", scatter_dimension=1, tiled=True
        ).astype(jnp.float32),
        lax.psum_scatter(
            grad_bias_full.astype(jnp.bfloat16), "tensor", scatter_dimension=0, tiled=True
        ).astype(jnp.float32),
        lax.psum_scatter(
            grad_back_full.astype(jnp.bfloat16), "tensor", scatter_dimension=0, tiled=True
        ).astype(jnp.float32),
    )
    grad_feed = jnp.einsum("nf,df->nd", grad_inner, full_in, preferred_element_type=jnp.float32)
    grad_normed = grad_second + grad_feed
    grad_mixed, grad_gain_one, grad_shift_one = first_back(grad_normed)
    mixed_low = grad_mixed.astype(jnp.bfloat16)
    whole_grad_mixer = lax.all_gather(mixed_low, "tensor", axis=0, tiled=True)
    grad_context = jnp.einsum(
        "nd,ed->ne", whole_grad_mixer, out_weight, preferred_element_type=jnp.float32
    ).astype(jnp.bfloat16)
    grad_out_weight = jnp.einsum(
        "ne,nd->ed", context, whole_grad_mixer, preferred_element_type=jnp.float32
    )
    grad_items = grad_context.reshape(seq_count, blocks_count, BLK, head_local, HD).transpose(
        0, 3, 1, 2, 4
    )
    grad_items = grad_items.reshape(seq_count * head_local, blocks_count, BLK, HD)
    grad_stack = lax.map(run_backward, (items, chosen_all, grad_items, log_middle, log_edge))
    grad_projected = grad_stack.reshape(seq_count, head_local, 3, blocks_count, BLK, HD).transpose(
        2, 0, 3, 4, 1, 5
    )
    grad_projected = grad_projected.reshape(3, group_rows, head_local * HD)
    grad_bias_pair = jnp.stack(
        [
            jnp.sum(grad_projected[0], axis=0, dtype=jnp.float32),
            jnp.sum(grad_projected[2], axis=0, dtype=jnp.float32),
        ]
    ).reshape(2, head_local, HD)
    grad_qkv_weight = jnp.einsum(
        "nd,kne->kde", whole_in, grad_projected, preferred_element_type=jnp.float32
    )
    piece = grad_projected
    grad_tokens = grad_mixed + lax.psum_scatter(
        jnp.einsum("kne,kde->nd", piece, qkv_weight, preferred_element_type=jnp.float32).astype(
            jnp.bfloat16
        ),
        "tensor",
        scatter_dimension=0,
        tiled=True,
    ).astype(jnp.float32)
    grads = (
        lax.psum_scatter(grad_qkv_weight, "dp", scatter_dimension=1, tiled=True),
        lax.psum_scatter(grad_bias_pair, "dp", scatter_dimension=2, tiled=True),
        lax.psum_scatter(grad_out_weight, "dp", scatter_dimension=1, tiled=True),
        lax.psum_scatter(grad_in_weight, "dp", scatter_dimension=0, tiled=True),
        lax.psum_scatter(grad_in_bias, "dp", scatter_dimension=1, tiled=True),
        lax.psum_scatter(grad_back_weight, "dp", scatter_dimension=1, tiled=True),
    )
    gain_terms = jnp.stack([grad_gain_one, grad_gain_two])
    bias_terms = jnp.stack(
        [jnp.sum(grad_mixed, axis=0), grad_shift_one, jnp.sum(grad_second, axis=0), grad_shift_two]
    )
    vectors = (
        lax.psum_scatter(gain_terms, ("dp", "tensor"), scatter_dimension=1, tiled=True),
        lax.psum_scatter(bias_terms, ("dp", "tensor"), scatter_dimension=1, tiled=True),
    )
    return (
        loss,
        encoded,
        grad_tokens,
        grads[0],
        grads[1],
        grads[2],
        grads[3],
        grads[4],
        grads[5],
        vectors[0],
        vectors[1],
    )


def solution(mesh):
    in_specs = (
        P(("dp", "tensor"), None),
        P(("dp", "tensor"), None),
        P(("dp", "tensor")),
        P(),
        P(None, "dp", "tensor"),
        P(None, "tensor", "dp"),
        P("tensor", "dp"),
        P("dp", "tensor"),
        P("tensor", "dp"),
        P("tensor", "dp"),
        P(None, "dp"),
        P(None, "dp"),
    )
    out_specs = (
        P(),
        P(("dp", "tensor"), None),
        P(("dp", "tensor"), None),
        P(None, "dp", "tensor"),
        P(None, "tensor", "dp"),
        P("tensor", "dp"),
        P("dp", "tensor"),
        P("tensor", "dp"),
        P("tensor", "dp"),
        P(None, ("dp", "tensor")),
        P(None, ("dp", "tensor")),
    )
    return jax.shard_map(
        per_device, mesh=mesh, in_specs=in_specs, out_specs=out_specs, check_vma=False
    )
```

profile of v0, /device:TPU:0, one launch (start us, length us, event | category | flops | bytes accessed | tf_op | source)
XLA Modules:
  0.0 1814.6 jit_solution(15611825318617754182)
XLA Ops:
  10.3 32.2 %all_gather.47 = bf16[2,3,64]{1,0,2:T(2,128)(2,1)S(1)} all-gather(bf16[2,3,8]{1,0,2:T(2,128)(2,1)S(1)} %copy.288), channel_id=1, replica_groups=mesh['dp'=8,'tensor'=4] {'dp'}, dimensions={2}, use_global_device_ids=true | all-gather | bytes 864 | tf_op jit(solution)/shard_map/all_gather | solution.py:34
  44.8 31.3 %all_gather.48 = bf16[192,768]{0,1:T(8,128)(2,1)S(1)} all-gather(bf16[192,96]{0,1:T(8,128)(2,1)S(1)} %copy.293), channel_id=1, replica_groups=mesh['dp'=8,'tensor'=4] {'dp'}, dimensions={1}, use_global_device_ids=true | all-gather | bytes 331776 | tf_op jit(solution)/shard_map/all_gather | solution.py:35
  76.1 42.3 %all_gather.45 = bf16[3,768,192]{2,0,1:T(4,128)(2,1)S(1)} all-gather(bf16[3,96,192]{2,0,1:T(4,128)(2,1)S(1)} %copy.286), channel_id=1, replica_groups=mesh['dp'=8,'tensor'=4] {'dp'}, dimensions={1}, use_global_device_ids=true | all-gather | bytes 995328 | tf_op jit(solution)/shard_map/all_gather | solution.py:33
  143.8 17.0 copy.291
  161.6 175.6 %while.28 = (s32[]{:T(128)}, bf16[6,32,64,64]{3,2,1,0:T(8,128)(2,1)}, f32[6,30,64]{2,1,0:T(8,128)S(1)}, f32[6,128]{1,0:T(8,128)S(1)}, bf16[6,3,32,64,64]{4,2,3,1...) while((s32[]{:T(128)}, ...), condition=%wide.region_5.6_spmd, body=%wide.region_0.5_spmd.sunk | while | flops 380113600 | bytes 35916652 | solution.py:241
  353.1 37.5 %psum.15 = f32[]{:T(128)} all-reduce(f32[]{:T(128)} %convert_reduce_fusion.2), channel_id=1, replica_groups=mesh['dp'=8,'tensor'=4] {'dp','tensor'}, use_global_device_ids=true, to_apply=%region_14.15 | all-reduce | flops 1 | bytes 8 | tf_op jit(solution)/shard_map/psum | solution.py:268
  390.6 20.0 %all-gather.1 = bf16[8,96,2]{1,2,0:T(2,128)(2,1)S(1)} all-gather(bf16[1,96,2]{1,2,0:T(2,128)(2,1)S(1)} %bitcast.468), channel_id=1, replica_groups=mesh['dp'=8,'tensor'=4] {'dp'}, dimensions={0}, use_global_device_ids=true | all-gather | bytes 3456 | tf_op jit(solution)/shard_map/all_gather | solution.py:39
  427.1 26.0 %all_gather.53 = bf16[12,64]{0,1:T(8,128)(2,1)S(1)} all-gather(bf16[12,8]{0,1:T(8,128)(2,1)S(1)} %copy-done.28), channel_id=1, replica_groups=mesh['dp'=8,'tensor'=4] {'dp'}, dimensions={1}, use_global_device_ids=true | all-gather | bytes 1728 | tf_op jit(solution)/shard_map/all_gather | solution.py:37
  507.9 20.5 %fusion.135 = (bf16[3072]{0:T(1024)(128)(2,1)}, bf16[1024,3072]{1,0:T(8,128)(2,1)}) fusion(bf16[3072,768]{0,1:T(8,128)(2,1)S(1)} %bitcast.472, f32[1024,768]{1,0:T(8,128)S(1)} %get-tuple-element.307, f32[1024]{0:T(1024)S(1)} %negate_multiply_fusion.1, f32[1024,3072]{1,0:T(8,128)} %fusion.126, f32[3072]{0:T(1024)S(1)} %reshape.666), kind=kOutput, calls=%fused_computation.289 | convolution fusion | flops 4915196928 | bytes 26761216 | tf_op jit(solution)/shard_map/nd,fd->nf/dot_general | solution.py:278
  566.0 22.7 %all-gather.20.cloned.1.call-done = bf16[4096,768]{1,0:T(8,128)(2,1)} async-done(((bf16[1024,768]{1,0:T(8,128)(2,1)}), bf16[4096,768]{1,0:T(8,128)(2,1)}) %all-gather.20.cloned.1.call-update) | async-done | bytes 6291472 | tf_op jit(solution)/shard_map/all_gather | solution.py:300
  610.3 881.7 %while.29 = (s32[]{:T(128)}, bf16[6,3,32,64,64]{4,3,2,1,0:T(8,128)(2,1)}, bf16[6,3,32,64,64]{4,2,3,1,0:T(8,128)(2,1)}, f32[6,128]{1,0:T(8,128)S(1)}, bf16[6,32,6...) while((s32[]{:T(128)}, ...), condition=%wide.region_26.27_spmd, body=%wide.region_19.26_spmd.sunk | while | flops 1145694464 | bytes 190884928 | solution.py:311
  686.3 16.3 slice_reduce_fusion.12
  729.1 16.4 slice_reduce_fusion.13
  828.5 16.3 slice_reduce_fusion.12
  871.2 16.4 slice_reduce_fusion.13
  1013.3 16.4 slice_reduce_fusion.13
  1155.3 16.4 slice_reduce_fusion.13
  1297.4 16.4 slice_reduce_fusion.13
  1439.4 16.4 slice_reduce_fusion.13
  1568.7 37.2 %all-reduce.13 = (f32[2,3,64]{2,1,0:T(4,128)S(1)}, f32[12,64]{1,0:T(8,128)S(1)}) all-reduce(f32[2,3,64]{2,1,0:T(4,128)S(1)} %pad_maximum_fusion.13, f32[12,64]{1,0:T(8,128)S(1)} %dynamic-slice_convert_fusion.2), channel_id=5, replica_groups=mesh['dp'=8,'tensor'=4] {'dp'}, use_global_device_ids=true, to_apply=%region_31.32.clone | all-reduce | flops 1152 | bytes 9216
  1610.9 50.1 %reduce-scatter.23.cloned.1.call-done = bf16[1024,768]{1,0:T(8,128)(2,1)} async-done(((bf16[4096,768]{1,0:T(8,128)(2,1)}), bf16[1024,768]{1,0:T(8,128)(2,1)}) %reduce-scatter.23.cloned.1.call-update) | async-done | bytes 1572880 | tf_op jit(solution)/shard_map/reduce_scatter | solution.py:326
  1665.5 40.4 %all-reduce.12 = (f32[]{:T(128)}, f32[2,768]{1,0:T(2,128)S(1)}, f32[4,768]{1,0:T(4,128)S(1)}) all-reduce(f32[]{:T(128)} %get-tuple-element.263, f32[2,768]{1,0:T(2,128)S(1)} %pad_maximum_fusion.11, f32[4,768]{1,0:T(4,128)S(1)} %pad_maximum_fusion.10), channel_id=1, replica_groups=mesh['dp'=8,'tensor'=4] {'dp','tensor'}, use_global_device_ids=true, to_apply=%region_12.13 | all-reduce | flops 4609 | bytes 36872 | tf_op jit(solution)/shard_map/psum | solution.py:268
  1707.9 26.9 %reduce-scatter.35.cloned.1.call-done = f32[96,768]{1,0:T(8,128)} async-done(((f32[768,768]{1,0:T(8,128)}), f32[96,768]{1,0:T(8,128)}) %reduce-scatter.35.cloned.1.call-update) | async-done | bytes 294928
  1734.8 72.0 %reduce-scatter.27.cloned.1.call-done = f32[96,768]{1,0:T(8,128)} async-done(((f32[768,768]{1,0:T(8,128)}), f32[96,768]{1,0:T(8,128)}) %reduce-scatter.27.cloned.1.call-update) | async-done | bytes 294928 | tf_op jit(solution)/shard_map/reduce_scatter | solution.py:338
  (878 shorter events, 1156.1 us)
Async XLA Ops:
  7.2 111.4 %copy-start = (s32[12,32,3,32]{3,1,2,0:T(8,128)S(1)}, s32[12,32,3,32]{3,1,2,0:T(8,128)}, u32[]{:S(2)}) copy-start(s32[12,32,3,32]{3,1,2,0:T(8,128)} %param.19) | copy-start | bytes 442372
  7.2 111.4 %all-gather.10.cloned.1.call-start = ((), (), s32[]{:S(2)}) async-start(), calls=%async_computation.8 | async-start | bytes 7864320 | tf_op jit(solution)/shard_map/all_gather | solution.py:231
  7.9 343.5 %all-gather.12.cloned.1.call-start = ((), (), s32[]{:S(2)}) async-start(), calls=%async_computation.10 | async-start | bytes 1327104 | tf_op jit(solution)/shard_map/all_gather | solution.py:36
  8.7 343.3 %all-gather.16.cloned.1.call-start = ((), (), s32[]{:S(2)}) async-start(), calls=%async_computation.12 | async-start | bytes 1327104 | tf_op jit(solution)/shard_map/all_gather | solution.py:38
  9.4 449.8 %reduce-scatter.21.cloned.1.call-start = ((), (), s32[]{:S(2)}) async-start(), calls=%async_computation.9 | async-start | bytes 7864320 | tf_op jit(solution)/shard_map/reduce_scatter | solution.py:247
  351.3 39.3 %copy-start.30 = (bf16[2,96]{1,0:T(2,128)(2,1)S(1)}, bf16[2,96]{1,0:T(2,128)(2,1)}, u32[]{:S(2)}) copy-start(bf16[2,96]{1,0:T(2,128)(2,1)} %param.26) | copy-start | bytes 1156
  351.3 59.5 %copy-start.29 = (bf16[4,96]{1,0:T(4,128)(2,1)S(1)}, bf16[4,96]{1,0:T(4,128)(2,1)}, u32[]{:S(2)}) copy-start(bf16[4,96]{1,0:T(4,128)(2,1)} %param.27) | copy-start | bytes 2308
  351.3 75.8 %copy-start.28 = (bf16[12,8]{0,1:T(8,128)(2,1)S(1)}, bf16[12,8]{0,1:T(8,128)(2,1)}, u32[]{:S(2)}) copy-start(bf16[12,8]{0,1:T(8,128)(2,1)} %param.24) | copy-start | bytes 580
  351.3 107.9 %copy-start.9 = (bf16[1024,768]{1,0:T(8,128)(2,1)S(1)}, bf16[1024,768]{1,0:T(8,128)(2,1)}, u32[]{:S(2)}) copy-start(bf16[1024,768]{1,0:T(8,128)(2,1)} %param.16) | copy-start | bytes 4718596
  351.3 111.0 %all-gather.14.cloned.1.call-start = ((), (), s32[]{:S(2)}) async-start(), calls=%async_computation.11 | async-start | bytes 5898240 | tf_op jit(solution)/shard_map/all_gather | solution.py:46
  351.9 135.0 %all-gather.18.cloned.1.call-start = ((), (), s32[]{:S(2)}) async-start(), calls=%async_computation.13 | async-start | bytes 5898240 | tf_op jit(solution)/shard_map/all_gather | solution.py:48
  352.5 236.3 %all-gather.20.cloned.1.call-start = ((), (), s32[]{:S(2)}) async-start(), calls=%async_computation.14 | async-start | bytes 7864320 | tf_op jit(solution)/shard_map/all_gather | solution.py:300
  506.2 22.3 %slice-start = ((s8[4718592]{0:T(1024)(128)(4,1)}), s8[524288]{0:T(1024)(128)(4,1)S(1)}, s32[]{:S(2)}) async-start(s8[4718592]{0:T(1024)(128)(4,1)} %bitcast.469), calls=%async_computation.22 | async-start | bytes 1048576
  507.9 34.4 %copy-start.22 = (f32[1024]{0:T(1024)}, f32[1024]{0:T(1024)S(1)}, u32[]{:S(2)}) copy-start(f32[1024]{0:T(1024)S(1)} %negate_multiply_fusion.1) | copy-start | bytes 12292
  542.2 1001.3 %reduce-scatter.29.cloned.1.call-start = ((), (), s32[]{:S(2)}) async-start(), calls=%async_computation.18 | async-start | bytes 5898240 | tf_op jit(solution)/shard_map/reduce_scatter | solution.py:292
  555.6 990.8 %reduce-scatter.25.cloned.1.call-start = ((), (), s32[]{:S(2)}) async-start(), calls=%async_computation.16 | async-start | bytes 5898240 | tf_op jit(solution)/shard_map/reduce_scatter | solution.py:286
  566.0 1041.4 %reduce-scatter.33.cloned.1.call-start = ((), (), s32[]{:S(2)}) async-start(), calls=%async_computation.20 | async-start | bytes 884736
  610.3 998.8 %reduce-scatter.31.cloned.1.call-start = ((), (), s32[]{:S(2)}) async-start(), calls=%async_computation.19 | async-start | bytes 2211840
  1533.8 127.2 %reduce-scatter.23.cloned.1.call-start = ((), (), s32[]{:S(2)}) async-start(), calls=%async_computation.15 | async-start | bytes 7864320 | tf_op jit(solution)/shard_map/reduce_scatter | solution.py:326
  1543.5 191.3 %reduce-scatter.35.cloned.1.call-start = ((), (), s32[]{:S(2)}) async-start(), calls=%async_computation.21 | async-start | bytes 2654208
  1546.3 260.4 %reduce-scatter.27.cloned.1.call-start = ((), (), s32[]{:S(2)}) async-start(), calls=%async_computation.17 | async-start | bytes 2654208 | tf_op jit(solution)/shard_map/reduce_scatter | solution.py:338
  1560.5 3.6 collective-permute-start
  1564.3 96.7 %copy-start.19 = (f32[1024]{0:T(1024)S(1)}, f32[1024]{0:T(1024)}, u32[]{:S(2)}) copy-start(f32[1024]{0:T(1024)} %copy-done.18) | copy-start | bytes 12292
  1610.2 196.6 %copy-start.1 = (s32[12,32,3,32]{3,1,2,0:T(8,128)S(1)}, s32[12,32,3,32]{3,1,2,0:T(8,128)}, u32[]{:S(2)}) copy-start(s32[12,32,3,32]{3,1,2,0:T(8,128)} %param.19) | copy-start | bytes 442372
  (58 other events, 525.1 us)
Sparse Core Ops, SparseCore 0:
  9.6 49.0 all-gather.9
  60.9 50.5 all-gather.11
  113.6 40.8 all-gather.15
  351.4 57.4 reduce-scatter.20
  410.4 37.4 all-gather.13
  449.4 37.4 all-gather.17
  542.3 46.3 all-gather.19
  591.4 47.8 reduce-scatter.28
  641.9 47.8 reduce-scatter.24
  693.2 62.4 reduce-scatter.32
  1533.9 67.1 reduce-scatter.30
  1603.6 57.3 reduce-scatter.22
  1665.1 69.6 reduce-scatter.34
  1738.7 67.9 reduce-scatter.26
where the time goes:
time: 1830 us; the launch traced here: 1810 us
  local copies, waits for them, and re-layouts  596 us (33%)
  matrix products  389 us (21%)
  blocking collectives  296 us (16%)
  other arithmetic  291 us (16%)
  waiting for transfers between devices  188 us (10%)
  loops' own time  32 us (2%)
  between operations  19.2 us (1%)
    while x216, local copies, waits for them, and re-layouts  240 us
    reduce_sum x12, other arithmetic, spread_slots(): jnp.sum(parts_grad[:, 3], axis=0)[None]  196 us
    reshape x12, local copies, waits for them, and re-layouts, spread_slots(): parts_grad = slot_grads.reshape(middle, -1, BLK, slot_grads.shape[-1])  80 us
    psum x2, blocking collectives, per_device(): lax.psum((jnp.sum(mask_rows[:, None] * error * error), jnp.sum(mask_rows)...  77.9 us
    reduce_scatter x1, waiting for transfers between devices, per_device(): lax.psum_scatter(grad_in_weight, 'dp', scatter_dimension=0, tiled=True)  72 us
    reduce_scatter x1, waiting for transfers between devices, per_device(): lax.psum_scatter(jnp.einsum('kne,kde->nd', piece, qkv_weight, preferred_e...  50.1 us
    dot_general x12, matrix products, middle_scores(): jnp.einsum('mqd,mkd->mqk', mid_queries, key_slots, preferred_element_type...  47.5 us
    unnamed x2, blocking collectives  45.1 us
  transfers between devices with their start and end apart: 15, of which 5 were waited for; matrix products, arithmetic and copies ran while one was open for 67% of the time, Pallas kernels for 0%

commit v1 on v0

v1 whole, which is shorter than its diff:
```python
import functools

import jax
import jax.numpy as jnp
from jax import lax
from jax.experimental import pallas as pl
from jax.experimental.pallas import tpu as pltpu
from jax.sharding import PartitionSpec as P

D = 768
HD = 64
BLK = 64
SEQ_LEN = 2048
epsilon = 1e-06
NEG = -1e30
F32 = jnp.float32
BF = jnp.bfloat16
MESH = pl.DeviceIdType.MESH
NT = (((1,), (1,)), ((), ()))
NN = (((1,), (0,)), ((), ()))
TN = (((0,), (0,)), ((), ()))
VM = pl.BlockSpec(memory_space=pltpu.VMEM)
SM = pl.BlockSpec(memory_space=pltpu.SMEM)
ANY = pl.BlockSpec(memory_space=pl.ANY)
SDS = jax.ShapeDtypeStruct


def dot(a, b, dims):
    return lax.dot_general(a, b, dims, preferred_element_type=F32)


def params(mib, cid=None):
    if cid is None:
        return pltpu.CompilerParams(vmem_limit_bytes=mib << 20)
    return pltpu.CompilerParams(vmem_limit_bytes=mib << 20, collective_id=cid, has_side_effects=True)


class Place:
    def __init__(self):
        self.zn = lax.axis_size("dp") // 2
        dp, t = lax.axis_index("dp"), lax.axis_index("tensor")
        self.z, self.x, self.y, self.c = dp // 2, dp % 2, t // 2, t % 2

    def at(self, z=None, x=None, y=None, c=None):
        z = self.z if z is None else z
        x = self.x if x is None else x
        y = self.y if y is None else y
        c = self.c if c is None else c
        return (z * 2 + x, y * 2 + c)

    def peer(self, axis, k=1):
        if axis == "z":
            return self.at(z=(self.z + k) % self.zn)
        return {
            "x": self.at(x=1 - self.x),
            "y": self.at(y=1 - self.y),
            "c": self.at(c=1 - self.c),
        }[axis]

    def peers(self, axes):
        out = []
        for axis in axes:
            for k in range(1, self.zn if axis == "z" else 2):
                out.append(self.peer(axis, k))
        return out


def greet(place, axes):
    barrier = pltpu.get_barrier_semaphore()
    peers = place.peers(axes)
    for peer in peers:
        pl.semaphore_signal(barrier, inc=1, device_id=peer, device_id_type=MESH)
    pl.semaphore_wait(barrier, len(peers))


class Sems:
    def __init__(self, send, recv):
        self.send, self.recv, self.used = send, recv, 0

    def copy(self, src, dst, device):
        i = self.used
        self.used += 1
        return pltpu.make_async_remote_copy(
            src_ref=src,
            dst_ref=dst,
            send_sem=self.send.at[i],
            recv_sem=self.recv.at[i],
            device_id=device,
            device_id_type=MESH,
        )
class Gather:
    def __init__(self, place, sems, shard, out, spec):
        self.place, self.sems, self.shard, self.out = place, sems, shard, out
        self.order, self.pre, self.axes, self.lanes = spec
        self.live = []

    def piece(self, whole):
        p = self.place
        own = {"y": p.y, "c": p.c, "z": p.z, "x": p.x}
        idx = (slice(None),) * self.pre
        idx += tuple(slice(None) if a in whole else own[a] for a in self.axes)
        if self.lanes is not None:
            idx += (slice(None),) * (len(self.out.shape) - len(idx) - 1) + (self.lanes,)
        return self.out.at[idx]

    def mine(self):
        ref = self.shard
        if self.lanes is None:
            return ref
        return ref.at[(slice(None),) * (len(ref.shape) - 1) + (self.lanes,)]

    def local(self, sem):
        return pltpu.make_async_copy(self.mine(), self.piece(""), sem)

    def start(self, stage):
        axis = self.order[stage]
        if stage == 0:
            src, dst = self.mine(), self.piece("")
        else:
            src = dst = self.piece(self.order[:stage])
        for k in range(1, self.place.zn if axis == "z" else 2):
            copy = self.sems.copy(src, dst, self.place.peer(axis, k))
            copy.start()
            self.live.append(copy)

    def wait(self):
        for copy in self.live:
            copy.wait()
        self.live = []


def gather_kernel(plan, n_in, *refs):
    ins, outs = refs[:n_in], refs[n_in : 2 * n_in]
    send, recv, here = refs[2 * n_in :]
    place = Place()
    greet(place, "zxyc")
    sems = Sems(send, recv)
    chunks = [Gather(place, sems, ins[i], outs[i], spec) for i, spec in plan]
    locals_ = []
    for n, chunk in enumerate(chunks):
        chunk.start(0)
        copy = chunk.local(here.at[n])
        copy.start()
        locals_.append(copy)
    for copy in locals_:
        copy.wait()
    for stage in range(1, 5):
        for chunk in chunks:
            if stage <= len(chunk.order):
                chunk.wait()
            if stage < len(chunk.order):
                chunk.start(stage)


def copies_of(order, zn):
    return sum(zn - 1 if a == "z" else 1 for a in order)


def gathered_shape(a, spec, zn):
    size = {"y": 2, "c": 2, "z": zn, "x": 2}
    pre = spec[1]
    return SDS(a.shape[:pre] + tuple(size[s] for s in spec[2]) + a.shape[pre:], a.dtype)


def gather_all(shards, plan, zn, cid):
    spec_of = {i: spec for i, spec in plan}
    copies = sum(copies_of(spec[0], zn) for _, spec in plan)
    n = len(shards)
    return pl.pallas_call(
        functools.partial(gather_kernel, plan, n),
        out_shape=tuple(gathered_shape(a, spec_of[i], zn) for i, a in enumerate(shards)),
        in_specs=[ANY] * n,
        out_specs=(ANY,) * n,
        scratch_shapes=[
            pltpu.SemaphoreType.DMA((copies,)),
            pltpu.SemaphoreType.DMA((copies,)),
            pltpu.SemaphoreType.DMA((len(plan),)),
        ],
        compiler_params=params(16, cid),
        name="gather_weights",
    )(*shards)


def swap_kernel(x_ref, o_ref, send, recv):
    place = Place()
    greet(place, "c")
    copy = pltpu.make_async_remote_copy(
        src_ref=x_ref.at[1 - place.c],
        dst_ref=o_ref,
        send_sem=send,
        recv_sem=recv,
        device_id=place.peer("c"),
        device_id_type=MESH,
    )
    copy.start()
    copy.wait()


def swap_cores(x, cid):
    return pl.pallas_call(
        swap_kernel,
        out_shape=SDS(x.shape[1:], x.dtype),
        in_specs=[ANY],
        out_specs=ANY,
        scratch_shapes=[pltpu.SemaphoreType.DMA, pltpu.SemaphoreType.DMA],
        compiler_params=params(16, cid),
        name="swap_cores",
    )(x)


class Scatter:
    def __init__(self, place, sems, grad, out, spec, bufs):
        self.place, self.sems, self.grad, self.out, self.bufs = place, sems, grad, out, bufs
        self.order, self.pre, self.axes = spec
        self.live = []

    @staticmethod
    def buffers(a, spec, zn):
        order, pre, axes = spec
        size = {"y": 2, "c": 2, "z": zn, "x": 2}
        lead, tail = a.shape[:pre], a.shape[pre + len(axes) :]
        left = list(axes)
        out = []
        for n, axis in enumerate(order):
            before = tuple(size[s] for s in left)
            left.remove(axis)
            after = tuple(size[s] for s in left)
            if axis == "z":
                recv = (zn - 1,) + lead + after + tail
            else:
                recv = lead + after + tail
            if n == 0:
                out.append((pltpu.VMEM(recv, BF), pltpu.VMEM(lead + after + tail, BF)))
            else:
                send = ((zn,) + lead + tail) if axis == "z" else lead + after + tail
                out.append((pltpu.VMEM(recv, BF), pltpu.VMEM(send, BF), pltpu.VMEM(lead + after + tail, F32)))
        return [b for group in out for b in group]

    def groups(self):
        out, rest = [], list(self.bufs)
        for n in range(len(self.order)):
            take = 2 if n == 0 else 3
            out.append(rest[:take])
            rest = rest[take:]
        return out

    def own(self, axis):
        p = self.place
        return {"y": p.y, "c": p.c, "z": p.z, "x": p.x}[axis]

    def begin(self, here):
        axis = self.order[0]
        at = self.pre + self.axes.index(axis)
        recv, keep = self.groups()[0]

        def half(i):
            return self.grad.at[(slice(None),) * at + (i,)]

        copy = self.sems.copy(half(1 - self.own(axis)), recv, self.place.peer(axis))
        copy.start()
        self.live = [copy]
        self.mine = pltpu.make_async_copy(half(self.own(axis)), keep, here)
        self.mine.start()
        self.left = [a for a in self.axes if a != axis]
        self.stage = 0

    def wait(self):
        for copy in self.live:
            copy.wait()
        self.live = []
        if self.stage == 0:
            self.mine.wait()

    def add(self):
        p, n = self.place, self.stage
        axis = self.order[n]
        group = self.groups()[n]
        recv, keep = group[0], group[-1]
        size = {"y": 2, "c": 2, "z": p.zn, "x": 2}
        lead = [range(s) for s in self.grad.shape[: self.pre]]

        def total(idx):
            if axis == "z":
                t = keep[idx]
                for k in range(p.zn - 1):
                    t = t + recv[(k,) + idx].astype(F32)
                return t
            return keep[idx].astype(F32) + recv[idx].astype(F32)

        def each(ranges, fn):
            if not ranges:
                fn(())
                return
            if isinstance(ranges[0], range):
                for i in ranges[0]:
                    each(ranges[1:], lambda rest, i=i: fn((i,) + rest))
            else:

                def body(i, carry):
                    each(ranges[1:], lambda rest: fn((i,) + rest))
                    return carry

                lax.fori_loop(0, ranges[0], body, 0)

        if n == len(self.order) - 1:

            def last(idx):
                self.out[idx] = total(idx)

            each(lead, last)
            return
        nxt = self.order[n + 1]
        recv2, send2, keep2 = self.groups()[n + 1]
        pos = self.left.index(nxt)
        own = self.own(nxt)
        rest_axes = [a for a in self.left if a != nxt]
        rest = lead + [size[a] if a == "z" else range(size[a]) for a in rest_axes]

        def place_of(idx, i):
            cut = self.pre + pos
            return idx[:cut] + (i,) + idx[cut:]

        def keep_one(idx):
            keep2[idx] = total(place_of(idx, own))

        if nxt == "z":
            for k in range(1, p.zn):
                i = (p.z + k) % p.zn

                def send_one(idx, i=i, k=k):
                    send2[(k,) + idx] = total(place_of(idx, i)).astype(BF)

                each(rest, send_one)
                copy = self.sems.copy(send2.at[k], recv2.at[k - 1], p.peer("z", k))
                copy.start()
                self.live.append(copy)
        else:

            def send_other(idx):
                send2[idx] = total(place_of(idx, 1 - own)).astype(BF)

            each(rest, send_other)
            copy = self.sems.copy(send2, recv2, p.peer(nxt))
            copy.start()
            self.live.append(copy)
        each(rest, keep_one)
        self.left = rest_axes
        self.stage = n + 1


class SumAll:
    order = "cyxz"

    def __init__(self, place, sems, value, out, recv, held):
        self.place, self.sems, self.value, self.out, self.recv, self.held = place, sems, value, out, recv, held
        self.live = []

    @staticmethod
    def buffers(a, zn):
        return [pltpu.VMEM((2 + zn,) + a.shape, F32), pltpu.VMEM((3,) + a.shape, F32)]

    def begin(self):
        self.stage = 0
        self.send(self.value)

    def send(self, src):
        p, n = self.place, self.stage
        axis = self.order[n]
        for k in range(1, p.zn if axis == "z" else 2):
            copy = self.sems.copy(src, self.recv.at[n + k - 1], p.peer(axis, k))
            copy.start()
            self.live.append(copy)

    def wait(self):
        for copy in self.live:
            copy.wait()
        self.live = []

    def add(self):
        n = self.stage
        mine = self.value[...] if n == 0 else self.held[n - 1]
        if n == 3:
            for k in range(self.place.zn - 1):
                mine = mine + self.recv[n + k]
            self.out[...] = mine
            return
        self.held[n] = mine + self.recv[n]
        self.stage = n + 1
        self.send(self.held.at[n])


def scatter_kernel(plan, shapes, zn, n_in, *refs):
    ins, outs, rest = refs[:n_in], refs[n_in : 2 * n_in], list(refs[2 * n_in :])
    send, recv, here = rest[:3]
    rest = rest[3:]
    place = Place()
    greet(place, "zxyc")
    sems = Sems(send, recv)
    chunks = []
    for n, spec in enumerate(plan):
        count = len(Scatter.buffers(shapes[n], spec, zn))
        chunks.append(Scatter(place, sems, ins[n], outs[n], spec, rest[:count]))
        rest = rest[count:]
    small = SumAll(place, sems, ins[-1], outs[-1], *rest)
    for n, chunk in enumerate(chunks):
        chunk.begin(here.at[n])
    small.begin()
    for stage in range(4):
        for chunk in chunks + [small]:
            if stage < len(chunk.order):
                chunk.wait()
                chunk.add()


def scatter_all(grads, plan, vector, zn, cid):
    shapes = tuple(SDS(g.shape, g.dtype) for g in grads)
    bufs = []
    for g, spec in zip(shapes, plan):
        bufs += Scatter.buffers(g, spec, zn)
    bufs += SumAll.buffers(vector, zn)
    copies = sum(copies_of(spec[0], zn) for spec in plan) + copies_of("cyxz", zn)
    out = [SDS(g.shape[: s[1]] + g.shape[s[1] + len(s[2]) :], F32) for g, s in zip(shapes, plan)]
    n = len(grads) + 1
    return pl.pallas_call(
        functools.partial(scatter_kernel, plan, shapes, zn, n),
        out_shape=tuple(out) + (SDS(vector.shape, F32),),
        in_specs=[ANY] * len(grads) + [VM],
        out_specs=(VM,) * n,
        scratch_shapes=[
            pltpu.SemaphoreType.DMA((copies,)),
            pltpu.SemaphoreType.DMA((copies,)),
            pltpu.SemaphoreType.DMA((len(grads),)),
        ]
        + bufs,
        compiler_params=params(56, cid),
        name="sum_gradients",
    )(*grads, vector)
def stack_heads(q):
    lo=lax.broadcasted_iota(jnp.int32,q.shape,1)<64
    z=jnp.zeros_like(q)
    return jnp.concatenate([jnp.where(lo,q,z),jnp.where(lo,z,q)],axis=0)

def slots_of(ref, j, picks, lanes, nb):
    lo=lax.broadcasted_iota(jnp.int32,(BLK,128),1)<64
    parts=[ref[0:BLK,lanes],ref[(nb-1)*BLK:nb*BLK,lanes],ref[pl.ds(pl.multiple_of((j-1)*BLK,BLK),3*BLK),lanes]]
    for a,b in picks:
        parts.append(jnp.where(lo,ref[pl.ds(pl.multiple_of(a*BLK,BLK),BLK),lanes],ref[pl.ds(pl.multiple_of(b*BLK,BLK),BLK),lanes]))
    return jnp.concatenate(parts,axis=0)

def picks_of(idx_ref,p,j):
    return [(idx_ref[2*p,j*3+r],idx_ref[2*p+1,j*3+r]) for r in range(3)]

def fwd_pair(p, idx_ref, q_ref, k_ref, v_ref, ctx_ref, lse_ref, lse_t, unroll=2):
    lanes=slice(p*128,(p+1)*128)
    nb=q_ref.shape[0]//BLK
    lo=lax.broadcasted_iota(jnp.int32,(BLK,128),1)<64
    col=lax.broadcasted_iota(jnp.int32,(128,128),1)
    def finish(o,l,m,j):
        inv=1.0/l
        o=o*inv
        ctx_ref[pl.ds(pl.multiple_of(j*BLK,BLK),BLK),lanes]=jnp.where(lo,o[:BLK],o[BLK:]).astype(BF)
        lse=m+jnp.log(l)
        lse_t[...]=jnp.where(col==j,lse,lse_t[...])
    def tile(j):
        picks=picks_of(idx_ref,p,j)
        q=stack_heads(q_ref[pl.ds(pl.multiple_of(j*BLK,BLK),BLK),lanes])
        ks=slots_of(k_ref,j,picks,lanes,nb); vs=slots_of(v_ref,j,picks,lanes,nb)
        s=dot(q,ks,NT)
        dup=((col<BLK)&(j==1))|((col>=BLK)&(j==nb-2))
        s=jnp.concatenate([jnp.where(dup,NEG,s[:,:128]),s[:,128:]],axis=1)
        m=jnp.max(s,axis=1,keepdims=True)
        e=jnp.exp(s-m)
        l=jnp.sum(e,axis=1,keepdims=True)
        o=dot(e.astype(BF),vs,NN)
        finish(o,l,m,j)
    def body(i,c):
        for u in range(unroll): tile(1+i*unroll+u)
        return c
    for j in (0,nb-1):
        q=stack_heads(q_ref[j*BLK:(j+1)*BLK,lanes])
        s=dot(q,k_ref[:,lanes],NT)
        m=jnp.max(s,axis=1,keepdims=True)
        e=jnp.exp(s-m)
        l=jnp.sum(e,axis=1,keepdims=True)
        o=dot(e.astype(BF),v_ref[:,lanes],NN)
        finish(o,l,m,j)
    lax.fori_loop(0,(nb-2)//unroll,body,0)
    lse_ref[p]=jnp.transpose(lse_t[...])[:nb]

def delta_row(do,ctx):
    d=jnp.transpose(do.astype(F32)*ctx.astype(F32))
    a=jnp.sum(d[:64],axis=0,keepdims=True); b=jnp.sum(d[64:],axis=0,keepdims=True)
    return jnp.concatenate([a,b],axis=1)

def bwd_pair(p, idx_ref, q_ref, k_ref, v_ref, ctx_ref, do_ref, lse_ref, dq_ref, dk_acc, dv_acc, unroll=1):
    lanes=slice(p*128,(p+1)*128)
    nb=q_ref.shape[0]//BLK
    lo=lax.broadcasted_iota(jnp.int32,(BLK,128),1)<64
    row=lax.broadcasted_iota(jnp.int32,(128,128),0)
    def core_math(q,do,ks,vs,lse,delta,dup=None):
        st=dot(ks,q,NT)
        pt=jnp.exp(st-lse)
        if dup is not None:
            pt=jnp.concatenate([jnp.where(dup,0.0,pt[:128]),pt[128:]],axis=0)
        dpt=dot(vs,do,NT)
        dst=(pt*(dpt-delta)).astype(BF)
        dv=dot(pt.astype(BF),do,NN)
        dk=dot(dst,q,NN)
        dq=dot(dst,ks,TN)
        return dq,dk,dv
    qs=[];dos=[];ls=[];ds=[]
    for j in (0,nb-1):
        rows=slice(j*BLK,(j+1)*BLK)
        qs.append(stack_heads(q_ref[rows,lanes])); dos.append(stack_heads(do_ref[rows,lanes]))
        ls.append(lse_ref[p,j:j+1,:]); ds.append(delta_row(do_ref[rows,lanes],ctx_ref[rows,lanes]))
    q=jnp.concatenate(qs,axis=0);do=jnp.concatenate(dos,axis=0);lse=jnp.concatenate(ls,axis=1);delta=jnp.concatenate(ds,axis=1)
    dqe=jnp.zeros((256,128),F32)
    ck=512
    for c in range(nb*BLK//ck):
        r=slice(c*ck,(c+1)*ck)
        dq,dk,dv=core_math(q,do,k_ref[r,lanes],v_ref[r,lanes],lse,delta)
        dqe=dqe+dq; dk_acc[r,:]=dk; dv_acc[r,:]=dv
    dqe=dqe*0.125
    dq_ref[0:BLK,lanes]=jnp.where(lo,dqe[0:64],dqe[64:128]).astype(BF)
    dq_ref[(nb-1)*BLK:nb*BLK,lanes]=jnp.where(lo,dqe[128:192],dqe[192:256]).astype(BF)
    def tile(j):
        picks=picks_of(idx_ref,p,j)
        rows=pl.ds(pl.multiple_of(j*BLK,BLK),BLK)
        qb=q_ref[rows,lanes]; dob=do_ref[rows,lanes]
        delta=delta_row(dob,ctx_ref[rows,lanes])
        ks=slots_of(k_ref,j,picks,lanes,nb); vs=slots_of(v_ref,j,picks,lanes,nb)
        dup=((row<BLK)&(j==1))|((row>=BLK)&(j==nb-2))
        dq,dk,dv=core_math(stack_heads(qb),stack_heads(dob),ks,vs,lse_ref[p,pl.ds(j,1),:],delta,dup)
        dq_ref[rows,lanes]=(jnp.where(lo,dq[:64],dq[64:])*0.125).astype(BF)
        win=pl.ds(pl.multiple_of((j-1)*BLK,BLK),3*BLK)
        for acc,g in ((dk_acc,dk),(dv_acc,dv)):
            acc[0:BLK,:]+=g[0:64]; acc[(nb-1)*BLK:nb*BLK,:]+=g[64:128]
            acc[win,:]+=g[128:320]
            for r,(a,b) in enumerate(picks):
                t=g[320+64*r:384+64*r]
                acc[pl.ds(pl.multiple_of(a*BLK,BLK),BLK),:]+=jnp.where(lo,t,0.0)
                acc[pl.ds(pl.multiple_of(b*BLK,BLK),BLK),:]+=jnp.where(lo,0.0,t)
    def body(i,c):
        for u in range(unroll): tile(1+i*unroll+u)
        return c
    lax.fori_loop(0,(nb-2)//unroll,body,0)

def concat_lanes(parts):
    return jnp.concatenate(parts, axis=1)


def project_kernel(unroll, idx_ref, h_ref, w_ref, b_ref, q_ref, k_ref, v_ref, ctx_ref, lse_ref, lse_t):
    rows = h_ref.shape[0]
    for k, out in enumerate((q_ref, k_ref, v_ref)):
        w = concat_lanes([w_ref[k, 0], w_ref[k, 1]])

        def some(i, carry, k=k, out=out, w=w):
            r = pl.ds(pl.multiple_of(i * 512, 512), 512)
            t = dot(h_ref[r, :], w, NN)
            if k != 1:
                t = t + b_ref[k // 2 : k // 2 + 1, :]
            t = t.astype(BF)
            if k == 0:
                t = (t.astype(F32) * 0.125).astype(BF)
            out[r, :] = t
            return carry

        lax.fori_loop(0, rows // 512, some, 0)
    for p in range(q_ref.shape[1] // 128):
        fwd_pair(p, idx_ref, q_ref, k_ref, v_ref, ctx_ref, lse_ref, lse_t, unroll)


def project_attend(idx, hidden, w, bias, unroll):
    n = hidden.shape[0]
    e = 2 * w.shape[-1]
    s = SDS((n, e), BF)
    return pl.pallas_call(
        functools.partial(project_kernel, unroll),
        out_shape=(s, s, s, s, SDS((e // 128, n // BLK, 128), F32)),
        in_specs=[SM, VM, VM, VM],
        out_specs=(VM,) * 5,
        scratch_shapes=[pltpu.VMEM((128, 128), F32)],
        compiler_params=params(56),
        name="project_attend",
    )(idx, hidden, w, bias)


def attend_back_kernel(unroll, idx_ref, q_ref, k_ref, v_ref, c_ref, do_ref, lse_ref, dq_ref, dk_ref, dv_ref, dka, dva):
    for p in range(q_ref.shape[1] // 128):
        bwd_pair(p, idx_ref, q_ref, k_ref, v_ref, c_ref, do_ref, lse_ref, dq_ref, dka, dva, unroll)
        lanes = slice(p * 128, (p + 1) * 128)
        dk_ref[:, lanes] = dka[...].astype(BF)
        dv_ref[:, lanes] = dva[...].astype(BF)


def attend_back(idx, q, k, v, ctx, do, lse, unroll):
    n, e = q.shape
    s = SDS((n, e), BF)
    return pl.pallas_call(
        functools.partial(attend_back_kernel, unroll),
        out_shape=(s, s, s),
        in_specs=[SM] + [VM] * 6,
        out_specs=(VM,) * 3,
        scratch_shapes=[pltpu.VMEM((n, 128), F32)] * 2,
        compiler_params=params(56),
        name="attend_back",
    )(idx, q, k, v, ctx, do, lse)


def norm(v):
    centred = v - jnp.mean(v, axis=-1, keepdims=True)
    rs = lax.rsqrt(jnp.mean(centred * centred, axis=-1, keepdims=True) + epsilon)
    return centred * rs, rs


def norm_back(g, gain, xhat, rs):
    gx = gain * g
    return rs * (gx - jnp.mean(gx, axis=-1, keepdims=True) - xhat * jnp.mean(gx * xhat, axis=-1, keepdims=True))


def gelu_both(v):
    k, a = 0.7978845608028654, 0.044715
    v2 = v * v
    th = jnp.tanh(k * v * (1.0 + a * v2))
    half = 0.5 * (1.0 + th)
    slope = half + (0.5 * k) * v * (1.0 - th * th) * (1.0 + (3.0 * a) * v2)
    return v * half, slope


def rows_kernel(
    scale_ref,
    ctx_ref,
    h_ref,
    t_ref,
    m_ref,
    w_in,
    w_bt,
    w_ot,
    b_in,
    gains,
    biases,
    enc_ref,
    gmix_ref,
    gctx_ref,
    gin_ref,
    gbt_ref,
    got_ref,
    vec_ref,
    gbin_ref,
    sq_ref,
    slope,
    act,
    ginner,
    nlow_t,
    slow_t,
    mlow_t,
):
    step = pl.program_id(0)
    tile = h_ref.shape[0]
    units = w_in.shape[0]
    r = pl.ds(pl.multiple_of(step * tile, tile), tile)

    @pl.when(step == 0)
    def _():
        vec_ref[...] = jnp.zeros_like(vec_ref)
        gbin_ref[...] = jnp.zeros_like(gbin_ref)
        sq_ref[...] = jnp.zeros_like(sq_ref)

    w_o = concat_lanes([w_ot[0, 0], w_ot[1, 0], w_ot[0, 1], w_ot[1, 1]])
    ctx = concat_lanes([ctx_ref[0], ctx_ref[1]])
    mixed = h_ref[...].astype(F32) + dot(ctx, w_o, NT) + biases[0:1, :]
    xhat1, rs1 = norm(mixed)
    normed = xhat1 * gains[0:1, :] + biases[1:2, :]
    nlow = normed.astype(BF)
    nlow_t[:, r] = nlow.T
    second = normed + biases[2:3, :]
    for u in range(units):
        inner = dot(nlow, w_in[u], NN) + b_in[u : u + 1, :]
        a, s = gelu_both(inner)
        a = a.astype(BF)
        act[u, r, :] = a
        slope[u] = s
        second = second + dot(a, w_bt[u], NT)
    xhat2, rs2 = norm(second)
    encoded = xhat2 * gains[1:2, :] + biases[3:4, :]
    enc_ref[...] = encoded
    error = encoded - t_ref[...]
    merr = m_ref[...] * error
    sq_ref[...] += jnp.sum(merr * error, axis=0, keepdims=True)
    genc = merr * scale_ref[0, 0]
    gsec = norm_back(genc, gains[1:2, :], xhat2, rs2)
    slow = gsec.astype(BF)
    slow_t[:, r] = slow.T
    gnorm = gsec
    for u in range(units):
        gi = (dot(slow, w_bt[u], NN) * slope[u]).astype(BF)
        ginner[u, r, :] = gi
        gbin_ref[u : u + 1, :] += jnp.sum(gi.astype(F32), axis=0, keepdims=True)
        gnorm = gnorm + dot(gi, w_in[u], NT)
    gmix = norm_back(gnorm, gains[0:1, :], xhat1, rs1)
    gmix_ref[...] = gmix
    mlow = gmix.astype(BF)
    mlow_t[:, r] = mlow.T
    gctx = dot(mlow, w_o, NN).astype(BF)
    gctx_ref[0] = gctx[:, : D // 2]
    gctx_ref[1] = gctx[:, D // 2 :]
    for n, value in enumerate((gnorm * xhat1, genc * xhat2, gmix, gnorm, gsec, genc)):
        vec_ref[n : n + 1, :] += jnp.sum(value, axis=0, keepdims=True)
    part = dot(mlow_t[:, r], ctx, NN)

    @pl.when(step == 0)
    def _():
        got_ref[...] = part

    @pl.when(step > 0)
    def _():
        got_ref[...] += part

    @pl.when(step == pl.num_programs(0) - 1)
    def _():
        for u in range(units):
            gin_ref[u] = dot(nlow_t[...], ginner[u], NN).astype(BF)
            gbt_ref[u] = dot(slow_t[...], act[u], NN).astype(BF)


def row_pass(scale, ctx, hidden, teacher, mask, w_in, w_bt, w_ot, b_in, gains, biases, tile):
    n = hidden.shape[0]
    units, _, wide = w_in.shape
    once = pl.Buffered(1)

    def whole(a):
        return pl.BlockSpec(a.shape, lambda i, nd=len(a.shape): (0,) * nd, pipeline_mode=once)

    def rows(width):
        return pl.BlockSpec((tile, width), lambda i: (i, 0))

    pair = pl.BlockSpec((2, tile, D // 2), lambda i: (0, i, 0))
    outs = (
        SDS((n, D), F32),
        SDS((n, D), F32),
        SDS((2, n, D // 2), BF),
        SDS(w_in.shape, BF),
        SDS(w_in.shape, BF),
        SDS((D, D), F32),
        SDS((6, D), F32),
        SDS((units, wide), F32),
        SDS((1, D), F32),
    )
    return pl.pallas_call(
        rows_kernel,
        grid=(n // tile,),
        out_shape=outs,
        in_specs=[SM, pair, rows(D), rows(D), rows(1)] + [whole(a) for a in (w_in, w_bt, w_ot, b_in, gains, biases)],
        out_specs=(rows(D), rows(D), pair) + tuple(whole(a) for a in outs[3:]),
        scratch_shapes=[
            pltpu.VMEM((units, tile, wide), F32),
            pltpu.VMEM((units, n, wide), BF),
            pltpu.VMEM((units, n, wide), BF),
            pltpu.VMEM((D, n), BF),
            pltpu.VMEM((D, n), BF),
            pltpu.VMEM((D, n), BF),
        ],
        compiler_params=params(62),
        name="row_pass",
    )(scale, ctx, hidden, teacher, mask, w_in, w_bt, w_ot, b_in, gains, biases)


def project_back_kernel(h_ref, dq_ref, dk_ref, dv_ref, w_ref, gw_ref, gh_ref, gb_ref):
    e = dq_ref.shape[1]
    half = e // 2
    hidden_t = h_ref[...].T
    for k, g in enumerate((dq_ref, dk_ref, dv_ref)):
        t = dot(hidden_t, g[...], NN).astype(BF)
        gw_ref[k, 0] = t[:, :half]
        gw_ref[k, 1] = t[:, half:]
        if k != 1:
            gb_ref[k // 2 : k // 2 + 1, :] = jnp.sum(g[...].astype(F32), axis=0, keepdims=True)
    w = [concat_lanes([w_ref[k, 0], w_ref[k, 1]]) for k in range(3)]

    def some(i, carry):
        r = pl.ds(pl.multiple_of(i * 256, 256), 256)
        t = dot(dq_ref[r, :], w[0], NT) + dot(dk_ref[r, :], w[1], NT) + dot(dv_ref[r, :], w[2], NT)
        gh_ref[r, :] = t.astype(BF)
        return carry

    lax.fori_loop(0, h_ref.shape[0] // 256, some, 0)


def project_back(hidden, dq, dk, dv, w):
    n = hidden.shape[0]
    return pl.pallas_call(
        project_back_kernel,
        out_shape=(SDS(w.shape, BF), SDS((n, D), BF), SDS((2, dq.shape[1]), F32)),
        in_specs=[VM] * 5,
        out_specs=(VM,) * 3,
        compiler_params=params(56),
        name="project_back",
    )(hidden, dq, dk, dv, w)
def per_device(
    hidden_in, teacher, valid_mask, random_blocks, w_qkv, b_qv, w_out, w_in, b_in, w_back, ln_gains, row_biases
):
    local = hidden_in.shape[0]
    dp, tensor = lax.axis_size("dp"), lax.axis_size("tensor")
    zn = dp // 2
    tokens_total = local * tensor * dp
    dpi, ti = lax.axis_index("dp"), lax.axis_index("tensor")
    y, c = ti // 2, ti % 2
    share = ln_gains.shape[1]
    heads = b_qv.shape[1]
    hd = b_qv.shape[2]
    mask = valid_mask.astype(F32)
    small = jnp.concatenate(
        [a.astype(F32).reshape(-1) for a in (b_qv, b_in, ln_gains, row_biases)] + [jnp.sum(mask).reshape(1)]
    )
    rows8 = -(-small.shape[0] // 1024) * 8
    small_pad = jnp.pad(small, (0, rows8 * 128 - small.shape[0])).reshape(rows8, 128)
    w_bt, w_ot = w_back.T, w_out.T
    half = w_in.shape[1] // 2
    lo, hi = slice(0, half), slice(half, 2 * half)
    full_qkv, whole_in, full_small, full_in, full_bt, full_ot = gather_all(
        (w_qkv, hidden_in, small_pad, w_in, w_bt, w_ot),
        [
            (0, ("zxy", 1, "yzx", None)),
            (1, ("c", 0, "c", None)),
            (2, ("zyxc", 0, "yczx", None)),
            (3, ("zxyc", 0, "yczx", lo)),
            (4, ("zyxc", 0, "yczx", lo)),
            (3, ("zxyc", 0, "yczx", hi)),
            (4, ("zyxc", 0, "yczx", hi)),
            (5, ("zyxc", 0, "yczx", None)),
        ],
        zn,
        0,
    )
    whole_in = whole_in.reshape(2 * local, D)
    full_qkv = full_qkv.reshape(3, 2, D, w_qkv.shape[2])
    full_in = full_in.reshape(4, D, w_in.shape[1])
    full_bt = full_bt.reshape(4, D, w_in.shape[1])
    full_ot = full_ot.reshape(2, 2, D, w_out.shape[0])
    flat = full_small.reshape(2, 2, dp, rows8 * 128)
    n0 = 2 * heads * hd
    n1 = n0 + b_in.size
    n2 = n1 + 2 * share
    n3 = n2 + 4 * share
    bias_qv = lax.dynamic_index_in_dim(flat, c, 1, False)[:, :, :n0].reshape(2, dp, 2, heads, hd)
    bias_qv = bias_qv.transpose(2, 0, 3, 1, 4).reshape(2, 2 * heads * hd * dp)
    bias_in = flat[..., n0:n1].reshape(4, dp, b_in.shape[0], hd).transpose(0, 2, 1, 3).reshape(4, -1)
    gains = flat[0, 0, :, n1:n2].reshape(dp, 2, share).transpose(1, 0, 2).reshape(2, D)
    biases = flat[0, 0, :, n2:n3].reshape(dp, 4, share).transpose(1, 0, 2).reshape(4, D)
    valid_total = jnp.sum(flat[..., n3])
    scale = (tokens_total / valid_total).reshape(1, 1)

    blocks = random_blocks.shape[1]
    idx = jnp.sum(random_blocks * jnp.arange(blocks, dtype=jnp.int32), axis=-1)
    idx = lax.dynamic_index_in_dim(idx.reshape(2, 2, heads, blocks * 3), c, 1, False).reshape(2 * heads, blocks * 3)

    q, k, v, ctx, lse = project_attend(idx, whole_in, full_qkv, bias_qv, 5)
    ctx_by_core = ctx.reshape(2, local, -1)
    ctx_there = swap_cores(ctx_by_core, 1)
    ctx_here = lax.dynamic_index_in_dim(ctx_by_core, c, 0, False)
    first = c == 0
    ctx_rows = jnp.stack([jnp.where(first, ctx_here, ctx_there), jnp.where(first, ctx_there, ctx_here)])
    encoded, gmix, gctx, g_in, g_bt, g_ot, vec, g_bin, sq = row_pass(
        scale, ctx_rows, hidden_in, teacher, mask[:, None], full_in, full_bt, full_ot, bias_in, gains, biases, 256
    )
    gctx_there = swap_cores(gctx, 2)
    gctx_here = lax.dynamic_index_in_dim(gctx, c, 0, False)
    gctx_seq = jnp.concatenate([jnp.where(first, gctx_here, gctx_there), jnp.where(first, gctx_there, gctx_here)])
    dq, dk, dv = attend_back(idx, q, k, v, ctx, gctx_seq, lse, 5)
    g_qkv, g_hidden, g_bias = project_back(whole_in, dq, dk, dv, full_qkv)
    g_hidden = g_hidden.reshape(2, local, D)
    there = swap_cores(g_hidden, 3)
    grad_in = gmix + lax.dynamic_index_in_dim(g_hidden, c, 0, False).astype(F32) + there.astype(F32)

    g_ot = g_ot.astype(BF).reshape(D, 2, 2, -1).transpose(2, 1, 0, 3)
    g_bias_all = lax.dynamic_update_index_in_dim(
        jnp.zeros((2, 2, 2, g_bias.shape[1] // 2), F32), g_bias.reshape(2, 2, -1), c, 2
    )
    vector = jnp.concatenate([vec.reshape(-1), g_bin.reshape(-1), g_bias_all.reshape(-1), jnp.sum(sq).reshape(1)])
    vrows = -(-vector.shape[0] // 1024) * 8
    vector = jnp.pad(vector, (0, vrows * 128 - vector.shape[0])).reshape(vrows, 128)
    s_in, s_bt, s_ot, s_qkv, vector = scatter_all(
        (
            g_in.reshape(2, 2, zn, 2, share, -1),
            g_bt.reshape(2, 2, zn, 2, share, -1),
            g_ot.reshape(2, 2, zn, 2, share, -1),
            g_qkv.reshape(3, 2, zn, 2, share, -1),
        ),
        [("cyxz", 0, "yczx"), ("cxyz", 0, "yczx"), ("cxyz", 0, "yczx"), ("yxz", 1, "yzx")],
        vector,
        zn,
        4,
    )
    vector = vector.reshape(-1)
    m0 = 6 * D
    m1 = m0 + g_bin.size
    m2 = m1 + g_bias_all.size
    part = dpi * tensor + ti
    cols = D // (dp * tensor)
    gains_biases = lax.dynamic_slice_in_dim(vector[:m0].reshape(6, D), part * cols, cols, 1)
    grad_b_in = lax.dynamic_index_in_dim(vector[m0:m1].reshape(tensor, b_in.shape[0], dp, hd), ti, 0, False)
    grad_b_in = lax.dynamic_index_in_dim(grad_b_in, dpi, 1, False)
    grad_qv = lax.dynamic_index_in_dim(vector[m1:m2].reshape(2, tensor, heads, dp, hd), ti, 1, False)
    grad_qv = lax.dynamic_index_in_dim(grad_qv, dpi, 2, False)
    loss = vector[m2] / (D * valid_total)
    return (
        loss,
        encoded,
        grad_in,
        s_qkv,
        grad_qv,
        s_ot.T,
        s_in,
        grad_b_in,
        s_bt.T,
        gains_biases[:2],
        gains_biases[2:],
    )


def solution(mesh):
    rows = P(("dp", "tensor"), None)
    in_specs = (
        rows,
        rows,
        P(("dp", "tensor")),
        P(),
        P(None, "dp", "tensor"),
        P(None, "tensor", "dp"),
        P("tensor", "dp"),
        P("dp", "tensor"),
        P("tensor", "dp"),
        P("tensor", "dp"),
        P(None, "dp"),
        P(None, "dp"),
    )
    out_specs = (
        P(),
        rows,
        rows,
        P(None, "dp", "tensor"),
        P(None, "tensor", "dp"),
        P("tensor", "dp"),
        P("dp", "tensor"),
        P("tensor", "dp"),
        P("tensor", "dp"),
        P(None, ("dp", "tensor")),
        P(None, ("dp", "tensor")),
    )
    return jax.shard_map(per_device, mesh=mesh, in_specs=in_specs, out_specs=out_specs, check_vma=False)
```

time: 1830 us -> 451 us (0.25)
  local copies, waits for them, and re-layouts: 596 us -> 42 us
  matrix products: 389 us -> 0 us
  Pallas kernels: 0 us -> 387 us
  blocking collectives: 296 us -> 0 us
  other arithmetic: 291 us -> 9.65 us
  waiting for transfers between devices: 188 us -> 0 us
  loops' own time: 32 us -> 0 us
    pallas_call x0 -> x9, Pallas kernels: none -> 387 us  [the longest x1 113 us: gather_all(): pl.pallas_call(functools.partial(gather_kernel, plan, n), out_shape=tuple...]
    dot_general x131 -> x0, matrix products: 383 us -> none  [the longest x12 47.5 us: middle_scores(): jnp.einsum('mqd,mkd->mqk', mid_queries, key_slots, preferred_element_type...]
    while x216 -> x0, local copies, waits for them, and re-layouts: 240 us -> none
    reduce_sum x33 -> x4, other arithmetic: 224 us -> 3.27 us  [the longest x1 1.29 us: per_device(): jnp.sum(mask).reshape(1)]
    all_gather x7 -> x0, blocking collectives: 173 us -> none  [the longest x1 42.3 us: fetch_weights(): lax.all_gather(w_qkv, 'dp', axis=1, tiled=True)]
    reshape x27 -> x22, local copies, waits for them, and re-layouts: 154 us -> 7.25 us  [the longest x6 3.13 us: per_device(): a.astype(F32).reshape(-1)]
    reduce_scatter x5 -> x0, waiting for transfers between devices: 122 us -> none  [the longest x1 72 us: per_device(): lax.psum_scatter(grad_in_weight, 'dp', scatter_dimension=0, tiled=True)]
    slice x84 -> x10, local copies, waits for them, and re-layouts: 112 us -> 4.76 us  [the longest x1 1.19 us: per_device(): loss = vector[m2] / (D * valid_total)]
  transfers between devices with their start and end apart: 15 -> 0, of which waited for: 5 -> 0; matrix products, arithmetic and copies ran while one was open for 67% -> 0% of each run, Pallas kernels for 0% -> 0%
where the time goes in v1:
time: 451 us; the launch traced here: 443 us
  Pallas kernels  387 us (86%)
  local copies, waits for them, and re-layouts  42 us (9%)
  other arithmetic  9.65 us (2%)
  between operations  4.59 us (1%)
    pallas_call x1, Pallas kernels, gather_all(): pl.pallas_call(functools.partial(gather_kernel, plan, n), out_shape=tuple...  113 us
    pallas_call x1, Pallas kernels, scatter_all(): pl.pallas_call(functools.partial(scatter_kernel, plan, shapes, zn, n), ou...  110 us
    pallas_call x1, Pallas kernels, row_pass(): pl.pallas_call(rows_kernel, grid=(n // tile,), out_shape=outs, in_specs=[...  55.7 us
    pallas_call x1, Pallas kernels, project_attend(): pl.pallas_call(functools.partial(project_kernel, unroll), out_shape=(s, s...  42.3 us
    pallas_call x1, Pallas kernels, attend_back(): pl.pallas_call(functools.partial(attend_back_kernel, unroll), out_shape=(...  39.9 us
    unnamed x54, local copies, waits for them, and re-layouts  24.7 us
    pallas_call x1, Pallas kernels, project_back(): pl.pallas_call(project_back_kernel, out_shape=(SDS(w.shape, BF), SDS((n,...  17.2 us

profile of v1, /device:TPU:0, one launch (start us, length us, event | category | flops | bytes accessed | tf_op | source)
XLA Modules:
  0.0 442.7 jit_solution(9792429460336244001)
XLA Ops:
  4.7 1.3 convert_reduce_fusion
  6.7 1.4 copy-done.6
  10.9 113.2 %gather_weights.1 = (bf16[3,2,4,2,96,192]{5,4,3,2,1,0:T(8,128)(2,1)S(1)}, bf16[2,1024,768]{2,1,0:T(8,128)(2,1)S(1)}, f32[2,2,4,2,8,128]{5,4,3,2,1,0:T(8,128)S(1)...) custom-call(bf16[3,96,192]{2,1,0:T(8,128)(2,1)S(1)} %copy-done.12, ...), custom_call_target="tpu_custom_call" | custom-call | tf_op jit(solution)/shard_map/gather_weights/pallas_call | solution.py:169
  124.1 1.7 copy-done
  125.7 1.4 copy-done.3
  127.1 2.2 copy-done.7
  129.4 2.1 copy-done.8
  135.2 42.3 %project_attend.1 = (bf16[2048,384]{1,0:T(8,128)(2,1)}, bf16[2048,384]{1,0:T(8,128)(2,1)}, bf16[2048,384]{1,0:T(8,128)(2,1)}, bf16[2048,384]{1,0:T(8,128)(2,1)}, f32[3,32,128]{2,1,0:T(8,128)}) custom-call(s32[6,96]{1,0:T(8,128)} %reshape.173.idx_ref, bf16[2048,768]{1,0:T(8,128)(2,1)} %bitcast.67, bf16[3,2,768,192]{3,2,1,0:T(8,128)(2,1)} %bitcast.71, ...), custom_call_target="tpu_custom_call" | custom-call | tf_op jit(solution)/shard_map/project_attend/pallas_call | solution.py:577
  177.5 1.4 copy-done.1
  178.9 2.3 swap_cores.3
  181.4 1.3 pad_maximum_fusion.ctx_ref
  187.8 55.7 %row_pass.1 = (f32[1024,768]{1,0:T(8,128)}, f32[1024,768]{1,0:T(8,128)}, bf16[2,1024,384]{2,1,0:T(8,128)(2,1)}, bf16[4,768,768]{2,1,0:T(8,128)(2,1)}, bf16[4,768...) custom-call(f32[1,1]{1,0:T(1,128)} %bitcast.4.scale_ref, ...), custom_call_target="tpu_custom_call" | custom-call | tf_op jit(solution)/shard_map/row_pass/pallas_call | solution.py:749
  243.5 1.4 copy-done.9
  244.9 2.4 swap_cores.4
  248.8 39.9 %attend_back.1 = (bf16[2048,384]{1,0:T(8,128)(2,1)}, bf16[2048,384]{1,0:T(8,128)(2,1)}, bf16[2048,384]{1,0:T(8,128)(2,1)}) custom-call(s32[6,96]{1,0:T(8,128)} %reshape.173.idx_ref, bf16[2048,384]{1,0:T(8,128)(2,1)} %get-tuple-element.52.q_ref, bf16[2048,384]{1,0:T(8,128)(2,1)} %get-tuple-element.53.k_ref, bf16[2048,384]{1,0:T(8,128)(2,1)} %get-tuple-element.54.v_ref, ...), custom_call_target="tpu_custom_call" | custom-call | tf_op jit(solution)/shard_map/attend_back/pallas_call | solution.py:599
  288.7 17.2 %project_back.1 = (bf16[3,2,768,192]{3,2,1,0:T(8,128)(2,1)}, bf16[2048,768]{1,0:T(8,128)(2,1)}, f32[2,384]{1,0:T(2,128)}) custom-call(bf16[2048,768]{1,0:T(8,128)(2,1)} %bitcast.68, bf16[2048,384]{1,0:T(8,128)(2,1)} %get-tuple-element.57.dq_ref, bf16[2048,384]{1,0:T(8,128)(2,1)} %get-tuple-element.58.dk_ref, bf16[2048,384]{1,0:T(8,128)(2,1)} %get-tuple-element.59.dv_ref, ...), custom_call_target="tpu_custom_call" | custom-call | tf_op jit(solution)/shard_map/project_back/pallas_call | solution.py:791
  305.9 1.9 copy-done.4
  307.8 3.4 swap_cores.5
  311.3 2.1 fusion
  316.3 1.5 copy.54
  317.9 110.0 %sum_gradients.1 = (f32[96,768]{1,0:T(8,128)}, f32[96,768]{1,0:T(8,128)}, f32[96,192]{1,0:T(8,128)}, f32[3,96,192]{2,1,0:T(8,128)}, f32[80,128]{1,0:T(8,128)}) custom-call(bf16[2,2,4,2,96,768]{5,4,3,2,1,0:T(8,128)(2,1)} %bitcast.82, bf16[2,2,4,2,96,768]{5,4,3,2,1,0:T(8,128)(2,1)} %bitcast.83, bf16[2,2,4,2,96,192]{5,4,3,2,1,0:T(8,128)(2,1)} %bitcast.80, ...), custom_call_target="tpu_custom_call" | custom-call | tf_op jit(solution)/shard_map/sum_gradients/pallas_call | solution.py:424
  430.9 1.6 copy.58
  437.0 1.7 copy.66
  438.7 1.7 copy.67
  (103 shorter events, 26.8 us)
Async XLA Ops:
  6.7 1.4 copy-start.6
  8.1 0.9 copy-start.12
  9.0 0.9 copy-start.13
  9.9 0.9 copy-start.14
  10.9 122.7 %copy-start.17 = (s32[12,32,3,32]{3,1,2,0:T(8,128)S(1)}, s32[12,32,3,32]{3,1,2,0:T(8,128)}, u32[]{:S(2)}) copy-start(s32[12,32,3,32]{3,1,2,0:T(8,128)} %param.15) | copy-start | bytes 442372
  124.1 1.7 copy-start
  125.7 1.4 copy-start.3
  127.1 2.2 copy-start.7
  129.4 2.1 copy-start.8
  131.5 1.2 copy-start.11
  177.5 1.4 copy-start.1
  178.9 2.3 copy-start.2
  181.4 5.4 %copy-start.20 = (s32[1024]{0:T(1024)S(1)}, s32[1024]{0:T(1024)}, u32[]{:S(2)}) copy-start(s32[1024]{0:T(1024)} %param.14) | copy-start | bytes 12292
  243.5 1.4 copy-start.9
  244.9 2.4 copy-start.10
  288.7 22.5 %copy-start.15 = (f32[1024,768]{1,0:T(8,128)S(1)}, f32[1024,768]{1,0:T(8,128)}, u32[]{:S(2)}) copy-start(f32[1024,768]{1,0:T(8,128)} %get-tuple-element.67) | copy-start | bytes 9437188
  305.9 1.9 copy-start.4
  307.8 3.4 copy-start.5
  311.3 2.1 copy-start.22
  311.3 2.3 copy-start.19
  311.3 2.3 copy-start.21
  311.3 2.4 copy-start.23
  311.3 4.2 copy-start.16
  427.9 12.5 %copy-start.18 = (f32[96,768]{1,0:T(8,128)S(1)}, f32[96,768]{1,0:T(8,128)}, u32[]{:S(2)}) copy-start(f32[96,768]{1,0:T(8,128)} %get-tuple-element.72) | copy-start | bytes 884740

commit v2 on v1

v2 whole, which is shorter than its diff:
```python
import functools

import jax
import jax.numpy as jnp
from jax import lax
from jax.experimental import pallas as pl
from jax.experimental.pallas import tpu as pltpu
from jax.sharding import PartitionSpec as P

D = 768
HD = 64
BLK = 64
SEQ_LEN = 2048
epsilon = 1e-06
NEG = -1e30
F32 = jnp.float32
BF = jnp.bfloat16
MESH = pl.DeviceIdType.MESH
NT = (((1,), (1,)), ((), ()))
NN = (((1,), (0,)), ((), ()))
TN = (((0,), (0,)), ((), ()))
VM = pl.BlockSpec(memory_space=pltpu.VMEM)
SM = pl.BlockSpec(memory_space=pltpu.SMEM)
ANY = pl.BlockSpec(memory_space=pl.ANY)
SDS = jax.ShapeDtypeStruct


def dot(a, b, dims):
    return lax.dot_general(a, b, dims, preferred_element_type=F32)


def params(mib, cid=None):
    if cid is None:
        return pltpu.CompilerParams(vmem_limit_bytes=mib << 20)
    return pltpu.CompilerParams(vmem_limit_bytes=mib << 20, collective_id=cid, has_side_effects=True)


class Place:
    def __init__(self):
        self.zn = lax.axis_size("dp") // 2
        dp, t = lax.axis_index("dp"), lax.axis_index("tensor")
        self.z, self.x, self.y, self.c = dp // 2, dp % 2, t // 2, t % 2

    def at(self, z=None, x=None, y=None, c=None):
        z = self.z if z is None else z
        x = self.x if x is None else x
        y = self.y if y is None else y
        c = self.c if c is None else c
        return (z * 2 + x, y * 2 + c)

    def peer(self, axis, k=1):
        if axis == "z":
            return self.at(z=(self.z + k) % self.zn)
        return {
            "x": self.at(x=1 - self.x),
            "y": self.at(y=1 - self.y),
            "c": self.at(c=1 - self.c),
        }[axis]

    def peers(self, axes):
        out = []
        for axis in axes:
            for k in range(1, self.zn if axis == "z" else 2):
                out.append(self.peer(axis, k))
        return out


def greet(place, axes):
    barrier = pltpu.get_barrier_semaphore()
    peers = place.peers(axes)
    for peer in peers:
        pl.semaphore_signal(barrier, inc=1, device_id=peer, device_id_type=MESH)
    pl.semaphore_wait(barrier, len(peers))


class Sems:
    def __init__(self, send, recv):
        self.send, self.recv, self.used = send, recv, 0

    def take(self, count):
        at = self.used
        self.used += count
        return at

    def copy(self, i, src, dst, device):
        return pltpu.make_async_remote_copy(
            src_ref=src,
            dst_ref=dst,
            send_sem=self.send.at[i],
            recv_sem=self.recv.at[i],
            device_id=device,
            device_id_type=MESH,
        )


def copies_of(order, zn):
    return sum(zn - 1 if a == "z" else 1 for a in order)


def concat_lanes(parts):
    return jnp.concatenate(parts, axis=1)


class Gather:
    def __init__(self, place, sems, shard, out, spec):
        self.place, self.shard, self.out = place, shard, out
        self.order, self.pre, self.axes, self.lanes = spec
        self.sems = sems
        self.base = sems.take(copies_of(self.order, place.zn))

    def piece(self, whole):
        p = self.place
        own = {"y": p.y, "c": p.c, "z": p.z, "x": p.x}
        idx = (slice(None),) * self.pre
        idx += tuple(slice(None) if a in whole else own[a] for a in self.axes)
        if self.lanes is not None:
            idx += (slice(None),) * (len(self.out.shape) - len(idx) - 1) + (self.lanes,)
        return self.out.at[idx]

    def mine(self):
        ref = self.shard
        if self.lanes is None:
            return ref
        return ref.at[(slice(None),) * (len(ref.shape) - 1) + (self.lanes,)]

    def local(self, sem):
        return pltpu.make_async_copy(self.mine(), self.piece(""), sem)

    def copies(self, stage):
        axis, zn = self.order[stage], self.place.zn
        if stage == 0:
            src, dst = self.mine(), self.piece("")
        else:
            src = dst = self.piece(self.order[:stage])
        at = self.base + copies_of(self.order[:stage], zn)
        return [
            self.sems.copy(at + k - 1, src, dst, self.place.peer(axis, k))
            for k in range(1, zn if axis == "z" else 2)
        ]

    def start(self, stage):
        for copy in self.copies(stage):
            copy.start()

    def wait(self, stage):
        for copy in self.copies(stage):
            copy.wait()


class Scatter:
    def __init__(self, place, sems, grad, out, spec, bufs):
        self.place, self.sems, self.grad, self.out = place, sems, grad, out
        self.order, self.pre, self.axes, self.lanes = spec
        self.base = sems.take(copies_of(self.order, place.zn))
        self.keep, self.recv, self.send = bufs[0], [bufs[1]] + list(bufs[2::2]), [None] + list(bufs[3::2])
        self.own = {"y": place.y, "c": place.c, "z": place.z, "x": place.x}
        self.size = {"y": 2, "c": 2, "z": place.zn, "x": 2}

    @staticmethod
    def buffers(a, spec, zn):
        order, pre, axes, lanes = spec
        size = {"y": 2, "c": 2, "z": zn, "x": 2}
        lead, tail = a.shape[:pre], a.shape[pre + len(axes) :]
        if lanes is not None:
            tail = tail[:-1] + (lanes.stop - lanes.start,)
        out = []
        for n, axis in enumerate(order):
            after = tuple(size[s] for s in axes if s not in order[: n + 1])
            one = lead + after + tail
            if n == 0:
                out.append(pltpu.VMEM(one, BF))
            out.append(pltpu.VMEM(((zn - 1,) if axis == "z" else ()) + one, BF))
            if n > 0:
                out.append(pltpu.VMEM(((zn,) if axis == "z" else ()) + one, BF))
        return out

    def copies(self, stage, only=None):
        p, axis = self.place, self.order[stage]
        at = self.base + copies_of(self.order[:stage], p.zn)
        recv, send = self.recv[stage], self.send[stage]
        if axis == "z":
            return [
                self.sems.copy(at + k - 1, send.at[k], recv.at[k - 1], p.peer("z", k))
                for k in (range(1, p.zn) if only is None else (only,))
            ]
        return [self.sems.copy(at, self.half(1 - self.own[axis]) if stage == 0 else send, recv, p.peer(axis))]

    def half(self, i):
        idx = (slice(None),) * (self.pre + self.axes.index(self.order[0])) + (i,)
        if self.lanes is not None:
            idx += (slice(None),) * (len(self.grad.shape) - len(idx) - 1) + (self.lanes,)
        return self.grad.at[idx]

    def kept(self, here):
        return pltpu.make_async_copy(self.half(self.own[self.order[0]]), self.keep, here)

    def begin(self, here):
        self.copies(0)[0].start()
        self.kept(here).start()

    def wait(self, stage, here=None):
        for copy in self.copies(stage):
            copy.wait()
        if stage == 0:
            self.kept(here).wait()

    def total(self, n, lead, coords):
        def at(done):
            return lead + tuple(coords.get(a, self.own[a]) for a in self.axes if a not in done)

        t = self.keep[at(self.order[:1])].astype(F32)
        for m in range(n + 1):
            idx = at(self.order[: m + 1])
            if self.order[m] == "z":
                for k in range(self.place.zn - 1):
                    t = t + self.recv[m][(k,) + idx].astype(F32)
            else:
                t = t + self.recv[m][idx].astype(F32)
        return t

    def each(self, axes, fn, coords=None, lead=()):
        coords = coords or {}
        if len(lead) < self.pre:
            for i in range(self.grad.shape[len(lead)]):
                self.each(axes, fn, coords, lead + (i,))
        elif not axes:
            fn(lead, coords)
        elif axes[0] == "z":

            def body(i, carry):
                self.each(axes[1:], fn, {**coords, "z": i}, lead)
                return carry

            lax.fori_loop(0, self.size["z"], body, 0)
        else:
            for i in range(2):
                self.each(axes[1:], fn, {**coords, axes[0]: i}, lead)

    def add(self, n):
        p = self.place
        if n == len(self.order) - 1:

            def last(lead, coords):
                if self.lanes is None:
                    self.out[lead] = self.total(n, lead, coords)
                else:
                    self.out[lead + (slice(None), self.lanes)] = self.total(n, lead, coords)

            self.each("", last)
            return
        nxt = self.order[n + 1]
        send = self.send[n + 1]
        left = [a for a in self.axes if a not in self.order[: n + 2]]
        if nxt == "z":
            for k in range(1, p.zn):
                to = (p.z + k) % p.zn

                def put(lead, coords, k=k, to=to):
                    send[(k,) + lead] = self.total(n, lead, {**coords, "z": to}).astype(BF)

                self.each(left, put)
                self.copies(n + 1, k)[0].start()
        else:

            def put(lead, coords):
                idx = lead + tuple(coords[a] for a in left)
                send[idx] = self.total(n, lead, {**coords, nxt: 1 - self.own[nxt]}).astype(BF)

            self.each(left, put)
            self.copies(n + 1)[0].start()


class SumAll:
    order = "cyxz"

    def __init__(self, place, sems, value, out, recv, held):
        self.place, self.sems, self.value, self.out, self.recv, self.held = place, sems, value, out, recv, held
        self.base = sems.take(copies_of(self.order, place.zn))

    @staticmethod
    def buffers(a, zn):
        return [pltpu.VMEM((2 + zn,) + a.shape, F32), pltpu.VMEM((3,) + a.shape, F32)]

    def copies(self, n):
        p = self.place
        axis = self.order[n]
        src = self.value if n == 0 else self.held.at[n - 1]
        at = self.base + n
        return [
            self.sems.copy(at + k - 1, src, self.recv.at[n + k - 1], p.peer(axis, k))
            for k in range(1, p.zn if axis == "z" else 2)
        ]

    def begin(self):
        self.copies(0)[0].start()

    def wait(self, n):
        for copy in self.copies(n):
            copy.wait()

    def add(self, n):
        mine = self.value[...] if n == 0 else self.held[n - 1]
        if n == 3:
            for k in range(self.place.zn - 1):
                mine = mine + self.recv[n + k]
            self.out[...] = mine
            return
        self.held[n] = mine + self.recv[n]
        for copy in self.copies(n + 1):
            copy.start()


UNROLL = 5


def stack_heads(q):
    lo = lax.broadcasted_iota(jnp.int32, q.shape, 1) < HD
    z = jnp.zeros_like(q)
    return jnp.concatenate([jnp.where(lo, q, z), jnp.where(lo, z, q)], axis=0)


def block_rows(j, count=1):
    return pl.ds(pl.multiple_of(j * BLK, BLK), count * BLK)


def flat_rows(t):
    return t.reshape(t.shape[0] * t.shape[1], t.shape[2])


def picks_of(idx_ref, p, j):
    pairs = idx_ref.shape[0] // 2
    return [(idx_ref[p, j * 3 + r], idx_ref[pairs + p, j * 3 + r]) for r in range(3)]


def slots_of(ref, p, j, picks, nb):
    lo = lax.broadcasted_iota(jnp.int32, (BLK, 2 * HD), 1) < HD
    parts = [ref[p, 0], ref[p, nb - 1], flat_rows(ref[p, pl.ds(j - 1, 3)])]
    for a, b in picks:
        parts.append(jnp.where(lo, ref[p, a], ref[p, b]))
    return jnp.concatenate(parts, axis=0)


class Forward:
    def __init__(self, idx_ref, q_ref, k_ref, v_ref, ctx_ref, lse_ref, lse_t):
        self.idx, self.q, self.k, self.v, self.ctx, self.lse, self.lse_t = (
            idx_ref,
            q_ref,
            k_ref,
            v_ref,
            ctx_ref,
            lse_ref,
            lse_t,
        )
        self.nb = q_ref.shape[1] // BLK
        self.steps = (self.nb - 2) // UNROLL

    def close(self, p, j, s, v):
        lo = lax.broadcasted_iota(jnp.int32, (BLK, 2 * HD), 1) < HD
        col = lax.broadcasted_iota(jnp.int32, (2 * BLK, 128), 1)
        m = jnp.max(s, axis=1, keepdims=True)
        e = jnp.exp(s - m)
        total = jnp.sum(e, axis=1, keepdims=True)
        o = dot(e.astype(BF), v, NN) * (1.0 / total)
        self.ctx[p, block_rows(j), :] = jnp.where(lo, o[:BLK], o[BLK:]).astype(BF)
        self.lse_t[...] = jnp.where(col == j, m + jnp.log(total), self.lse_t[...])

    def edges(self, p):
        for j in (0, self.nb - 1):
            q = stack_heads(self.q[p, j * BLK : (j + 1) * BLK, :])
            self.close(p, j, dot(q, flat_rows(self.k[p]), NT), flat_rows(self.v[p]))

    def tile(self, p, j):
        picks = picks_of(self.idx, p, j)
        q = stack_heads(self.q[p, block_rows(j), :])
        ks = slots_of(self.k, p, j, picks, self.nb)
        vs = slots_of(self.v, p, j, picks, self.nb)
        s = dot(q, ks, NT)
        col = lax.broadcasted_iota(jnp.int32, (2 * BLK, 128), 1)
        double = ((col < BLK) & (j == 1)) | ((col >= BLK) & (j == self.nb - 2))
        s = jnp.concatenate([jnp.where(double, NEG, s[:, :128]), s[:, 128:]], axis=1)
        self.close(p, j, s, vs)

    def step(self, p, i):
        for u in range(UNROLL):
            self.tile(p, 1 + i * UNROLL + u)

    def finish(self, p):
        self.lse[p] = jnp.transpose(self.lse_t[...])[: self.nb]

    def run(self, pairs, at=None):
        def body(g, carry):
            p, i = g // self.steps, g % self.steps
            if at is not None:
                at(g)

            @pl.when(i == 0)
            def _():
                self.edges(p)

            self.step(p, i)

            @pl.when(i == self.steps - 1)
            def _():
                self.finish(p)

            return carry

        lax.fori_loop(0, pairs * self.steps, body, 0)


def delta_row(do, ctx):
    d = jnp.transpose(do.astype(F32) * ctx.astype(F32))
    a = jnp.sum(d[:HD], axis=0, keepdims=True)
    b = jnp.sum(d[HD:], axis=0, keepdims=True)
    return jnp.concatenate([a, b], axis=1)


class Backward:
    def __init__(self, idx_ref, prev_ref, last_ref, q, k, v, ctx, do, lse, dq, dk, dv, dk_acc, dv_acc, dk_run, dv_run):
        self.idx, self.prev, self.last = idx_ref, prev_ref, last_ref
        self.q, self.k, self.v, self.ctx, self.do, self.lse = q, k, v, ctx, do, lse
        self.dq, self.dk, self.dv = dq, dk, dv
        self.accs = ((dk_acc, dk_run), (dv_acc, dv_run))
        self.nb = q.shape[1] // BLK
        self.steps = (self.nb - 2) // UNROLL

    def math(self, q, do, ks, vs, lse, delta, double=None):
        st = dot(ks, q, NT)
        pt = jnp.exp(st - lse)
        if double is not None:
            pt = jnp.concatenate([jnp.where(double, 0.0, pt[:128]), pt[128:]], axis=0)
        dst = (pt * (dot(vs, do, NT) - delta)).astype(BF)
        return dot(dst, ks, TN), dot(dst, q, NN), dot(pt.astype(BF), do, NN)

    def edges(self, p):
        qs, dos, ls, ds = [], [], [], []
        lo = lax.broadcasted_iota(jnp.int32, (BLK, 2 * HD), 1) < HD
        for j in (0, self.nb - 1):
            rows = slice(j * BLK, (j + 1) * BLK)
            do = self.do_block(p, j)
            qs.append(stack_heads(self.q[p, rows, :]))
            dos.append(stack_heads(do))
            ls.append(self.lse[p, j : j + 1, :])
            ds.append(delta_row(do, self.ctx[p, rows, :]))
        q, do = jnp.concatenate(qs, axis=0), jnp.concatenate(dos, axis=0)
        lse, delta = jnp.concatenate(ls, axis=1), jnp.concatenate(ds, axis=1)
        dq_sum = jnp.zeros((4 * BLK, 2 * HD), F32)
        for n in range(self.nb // 8):
            r = slice(n * 8 * BLK, (n + 1) * 8 * BLK)
            ks, vs = flat_rows(self.k[p, n * 8 : (n + 1) * 8]), flat_rows(self.v[p, n * 8 : (n + 1) * 8])
            dq, dk, dv = self.math(q, do, ks, vs, lse, delta)
            dq_sum = dq_sum + dq
            self.accs[0][0][r, :] = dk
            self.accs[1][0][r, :] = dv
        dq_sum = dq_sum * 0.125
        for n, j in enumerate((0, self.nb - 1)):
            part = dq_sum[n * 2 * BLK : (n + 1) * 2 * BLK]
            self.dq[p, j * BLK : (j + 1) * BLK, :] = jnp.where(lo, part[:BLK], part[BLK:]).astype(BF)
        for _, run in self.accs:
            run[0] = jnp.zeros((BLK, 2 * HD), F32)

    def do_block(self, p, j):
        half = self.nb // 2
        if isinstance(j, int):
            return self.do[j // half, p, (j % half) * BLK : (j % half + 1) * BLK, :]
        return self.do[j // half, p, block_rows(j % half), :]

    def tile(self, p, j):
        lo = lax.broadcasted_iota(jnp.int32, (BLK, 2 * HD), 1) < HD
        row = lax.broadcasted_iota(jnp.int32, (2 * BLK, 128), 0)
        nb, pairs = self.nb, self.idx.shape[0] // 2
        picks = picks_of(self.idx, p, j)
        q, do = self.q[p, block_rows(j), :], self.do_block(p, j)
        delta = delta_row(do, self.ctx[p, block_rows(j), :])
        ks = slots_of(self.k, p, j, picks, nb)
        vs = slots_of(self.v, p, j, picks, nb)
        double = ((row < BLK) & (j == 1)) | ((row >= BLK) & (j == nb - 2))
        dq, dk, dv = self.math(
            stack_heads(q), stack_heads(do), ks, vs, self.lse[p, pl.ds(j, 1), :], delta, double
        )
        self.dq[p, block_rows(j), :] = (jnp.where(lo, dq[:BLK], dq[BLK:]) * 0.125).astype(BF)
        for (acc, run), g in zip(self.accs, (dk, dv)):
            acc[0:BLK, :] += g[0:BLK]
            acc[(nb - 1) * BLK : nb * BLK, :] += g[BLK : 2 * BLK]
            acc[block_rows(j - 1, 3), :] += g[2 * BLK : 5 * BLK]
            for r in range(3):
                s = j * 3 + r
                before = jnp.where(lo, run[self.prev[p, s]], run[self.prev[pairs + p, s]])
                run[s - 2] = g[(5 + r) * BLK : (6 + r) * BLK] + before

    def step(self, p, i):
        for u in range(UNROLL):
            self.tile(p, 1 + i * UNROLL + u)

    def finish(self, p):
        lo = lax.broadcasted_iota(jnp.int32, (BLK, 2 * HD), 1) < HD
        pairs = self.idx.shape[0] // 2

        def body(n, carry):
            a, b = self.last[p, n], self.last[pairs + p, n]
            for (acc, run), out in zip(self.accs, (self.dk, self.dv)):
                t = acc[block_rows(n), :] + jnp.where(lo, run[a], run[b])
                out[p, block_rows(n), :] = t.astype(BF)
            return carry

        lax.fori_loop(0, self.nb, body, 0)

    def run(self, pairs, at=None, done=None):
        def body(g, carry):
            p, i = g // self.steps, g % self.steps
            if at is not None:
                at(g)

            @pl.when(i == 0)
            def _():
                self.edges(p)

            self.step(p, i)

            @pl.when(i == self.steps - 1)
            def _():
                self.finish(p)
                if done is not None:
                    done(p)

            return carry

        lax.fori_loop(0, pairs * self.steps, body, 0)


def block_tables(random_blocks, place_c):
    heads, blocks = random_blocks.shape[:2]
    own = lax.dynamic_index_in_dim(
        random_blocks.reshape((2, 2, heads // 4) + random_blocks.shape[1:]), place_c, 1, False
    ).reshape(heads // 2, blocks * 3, blocks)
    idx = jnp.sum(own * jnp.arange(blocks, dtype=jnp.int32), axis=-1)
    slots = blocks * 3
    s = jnp.arange(slots, dtype=jnp.int32)
    middle = (s >= 3) & (s < slots - 3)
    number = jnp.where(middle, s - 2, 0)
    same = (idx[:, :, None] == idx[:, None, :]) & (s[None, None, :] < s[None, :, None])
    prev = jnp.max(jnp.where(same, number[None, None, :], 0), axis=-1)
    last = jnp.max(jnp.where(own > 0, number[None, :, None], 0), axis=1)
    return idx, prev, last
SMALL_ROWS = 16


class Due:
    def __init__(self):
        self.todo = {}

    def add(self, step, fn):
        self.todo.setdefault(step, []).append(fn)

    def __call__(self, g):
        for step, fns in self.todo.items():

            @pl.when(g == step)
            def _(fns=fns):
                for fn in fns:
                    fn()


def assemble_qkv(parts, w, pairs):
    zn, half = parts.shape[1], parts.shape[3]
    wide = parts.shape[4] // 2

    def body(n, carry):
        z, x = n // 2, n % 2
        for h in range(2):
            rows = pl.ds(pl.multiple_of(n * 2 * half + h * half, half), half)
            src = [parts[y, z, x, :, h * wide : (h + 1) * wide] for y in range(2)]
            for kp in range(3 * pairs):
                w[rows, kp * 128 : (kp + 1) * 128] = jnp.concatenate(
                    [s[:, kp * HD : (kp + 1) * HD] for s in src], axis=1
                )
        return carry

    lax.fori_loop(0, zn * 2, body, 0)


def project_rows(i, chunk, hid, w, bias, q, k, v):
    pairs = q.shape[0]
    e = pairs * 128
    per = hid.shape[1] // chunk
    src = hid[i // per, pl.ds(pl.multiple_of(i % per * chunk, chunk), chunk), :]
    rows = pl.ds(pl.multiple_of(i * chunk, chunk), chunk)
    t = dot(src, w[...], NN)
    for n, out in enumerate((q, k, v)):
        part = t[:, n * e : (n + 1) * e]
        if n == 0:
            part = (part + bias[0:1, :]).astype(BF).astype(F32) * 0.125
        if n == 2:
            part = part + bias[1:2, :]
        part = part.astype(BF)
        for p in range(pairs):
            one = part[:, p * 128 : (p + 1) * 128]
            if n == 0:
                out[p, rows, :] = one
            else:
                out[p, pl.ds(i * (chunk // BLK), chunk // BLK)] = one.reshape(chunk // BLK, BLK, 128)


def gather_attend_kernel(
    cuts,
    idx_ref,
    wq_ref,
    h_ref,
    small_ref,
    win_ref,
    wb_ref,
    wo_ref,
    q_ref,
    k_ref,
    v_ref,
    ctx_ref,
    lse_ref,
    rows_ref,
    hid_ref,
    w_ref,
    fin_ref,
    fbt_ref,
    fot_ref,
    par_ref,
    send,
    recv,
    here,
    parts,
    wbt,
    wot,
    s_recv,
    s_held,
    lse_t,
):
    place = Place()
    c = place.c
    local = h_ref.shape[0]
    pairs = q_ref.shape[0]
    greet(place, "zxyc")
    sems = Sems(send, recv)
    qkv = [
        Gather(place, sems, wq_ref, parts, ("zxy" if n % 2 == 0 else "zyx", 0, "yzx", slice(a, b)))
        for n, (a, b) in enumerate(cuts)
    ]
    hid = Gather(place, sems, h_ref, hid_ref, ("c", 0, "c", None))
    small = SumAll(place, sems, small_ref, par_ref, s_recv, s_held)
    half = win_ref.shape[1] // 2
    lo, hi = slice(0, half), slice(half, 2 * half)
    ffn = [
        Gather(place, sems, win_ref, fin_ref, ("zxyc", 0, "yczx", lo)),
        Gather(place, sems, wbt, fbt_ref, ("zyxc", 0, "yczx", lo)),
        Gather(place, sems, win_ref, fin_ref, ("zxyc", 0, "yczx", hi)),
        Gather(place, sems, wbt, fbt_ref, ("zyxc", 0, "yczx", hi)),
        Gather(place, sems, wot, fot_ref, ("zyxc", 0, "yczx", None)),
    ]
    swap_at = sems.take(pairs)
    for chunk in qkv:
        chunk.start(0)
    hid.start(0)
    small.begin()
    own = [pltpu.make_async_copy(wq_ref, parts.at[place.y, place.z, place.x], here.at[0]), hid.local(here.at[1])]
    for copy in own:
        copy.start()
    wbt[...] = wb_ref[...].T
    t = wo_ref[...].T
    hr = wot.shape[0]
    wot[...] = concat_lanes([t[:hr], t[hr:]])
    late = [
        pltpu.make_async_copy(src, out.at[place.y, c, place.z, place.x], here.at[2 + n])
        for n, (src, out) in enumerate(((win_ref, fin_ref), (wbt, fbt_ref), (wot, fot_ref)))
    ]
    for copy in late:
        copy.start()
    for copy in own:
        copy.wait()
    small.wait(0)
    small.add(0)
    for chunk in qkv:
        chunk.wait(0)
        chunk.start(1)
    small.wait(1)
    small.add(1)
    for chunk in ffn:
        chunk.start(0)
    for chunk in qkv:
        chunk.wait(1)
        chunk.start(2)
    small.wait(2)
    small.add(2)
    for copy in late:
        copy.wait()
    hid.wait(0)
    small.wait(3)
    small.add(3)
    for chunk in qkv:
        chunk.wait(2)
    assemble_qkv(parts, w_ref, pairs)

    def pass_on(n, stage):
        def fn():
            ffn[n].wait(stage)
            ffn[n].start(stage + 1)

        return fn

    early, due = Due(), Due()
    for step, n, stage in ((0, 0, 0), (0, 1, 0), (1, 2, 0), (3, 3, 0)):
        early.add(step, pass_on(n, stage))
    for step, n, stage in (
        (0, 4, 0),
        (0, 0, 1),
        (1, 1, 1),
        (3, 2, 1),
        (4, 3, 1),
        (6, 4, 1),
        (6, 0, 2),
        (8, 1, 2),
        (12, 2, 2),
        (15, 3, 2),
        (17, 4, 2),
    ):
        due.add(step, pass_on(n, stage))
    e = pairs * 128
    bias = jnp.where(c == 0, par_ref[11:13, :e], par_ref[11:13, e:])
    chunk_rows = local // 2

    def project(i, carry):
        early(i)
        project_rows(i, chunk_rows, hid_ref, w_ref, bias, q_ref, k_ref, v_ref)
        return carry

    lax.fori_loop(0, 4, project, 0)
    attend = Forward(idx_ref, q_ref, k_ref, v_ref, ctx_ref, lse_ref, lse_t)
    attend.run(pairs, due)

    def there(p):
        rows = pl.ds(pl.multiple_of((1 - c) * local, local), local)
        return sems.copy(swap_at + p, ctx_ref.at[p, rows, :], rows_ref.at[c, p], place.peer("c"))

    for p in range(pairs):
        there(p).start()
    mine = pltpu.make_async_copy(
        ctx_ref.at[:, pl.ds(pl.multiple_of(c * local, local), local), :], rows_ref.at[c], here.at[0]
    )
    mine.start()
    for chunk in ffn:
        chunk.wait(3)
    mine.wait()
    for p in range(pairs):
        there(p).wait()


def gather_attend(idx, wq, hidden, small, w_in, w_back, w_out, pairs, zn, cid):
    local = hidden.shape[0]
    n = 2 * local
    e = pairs * 128
    share, wide = w_in.shape
    width = wq.shape[1]
    step = width // 128 // 4 * 128
    cuts = [(i * step, (i + 1) * step if i < 3 else width) for i in range(4)]
    heads_shape = SDS((pairs, n, 128), BF)
    blocks_shape = SDS((pairs, n // BLK, BLK, 128), BF)
    wot = (share // 2, 2 * w_out.shape[0])
    copies = 4 * copies_of("zxy", zn) + 1 + copies_of("cyxz", zn) + 5 * copies_of("zxyc", zn) + pairs
    return pl.pallas_call(
        functools.partial(gather_attend_kernel, cuts),
        out_shape=(
            heads_shape,
            blocks_shape,
            blocks_shape,
            heads_shape,
            SDS((pairs, n // BLK, 128), F32),
            SDS((2, pairs, local, 128), BF),
            SDS((2, local, D), BF),
            SDS((D, 3 * e), BF),
            SDS((2, 2, zn, 2, share, wide), BF),
            SDS((2, 2, zn, 2, share, wide), BF),
            SDS((2, 2, zn, 2) + wot, BF),
            SDS(small.shape, F32),
        ),
        in_specs=[SM, ANY, ANY, VM, ANY, VM, VM],
        out_specs=(VM,) * 5 + (ANY, VM, VM, ANY, ANY, ANY, VM),
        scratch_shapes=[
            pltpu.SemaphoreType.DMA((copies,)),
            pltpu.SemaphoreType.DMA((copies,)),
            pltpu.SemaphoreType.DMA((5,)),
            pltpu.VMEM((2, zn, 2) + wq.shape, BF),
            pltpu.VMEM((share, wide), BF),
            pltpu.VMEM(wot, BF),
        ]
        + SumAll.buffers(small, zn)
        + [pltpu.VMEM((128, 128), F32)],
        compiler_params=params(56, cid),
        name="gather_attend",
    )(idx, wq, hidden, small, w_in, w_back, w_out)
def norm(v):
    centred = v - jnp.mean(v, axis=-1, keepdims=True)
    rs = lax.rsqrt(jnp.mean(centred * centred, axis=-1, keepdims=True) + epsilon)
    return centred * rs, rs


def norm_back(g, gain, xhat, rs):
    gx = gain * g
    return rs * (gx - jnp.mean(gx, axis=-1, keepdims=True) - xhat * jnp.mean(gx * xhat, axis=-1, keepdims=True))


def gelu_both(v):
    k, a = 0.7978845608028654, 0.044715
    v2 = v * v
    th = jnp.tanh(k * v * (1.0 + a * v2))
    half = 0.5 * (1.0 + th)
    slope = half + (0.5 * k) * v * (1.0 - th * th) * (1.0 + (3.0 * a) * v2)
    return v * half, slope


def assemble_out(parts, w):
    zn, half = parts.shape[2], parts.shape[4]
    wide = parts.shape[5] // 2
    pairs = wide // HD

    def body(n, carry):
        z, x = n // 2, n % 2
        for h in range(2):
            rows = pl.ds(pl.multiple_of(n * 2 * half + h * half, half), half)
            for c in range(2):
                for p in range(pairs):
                    at = h * wide + p * HD
                    w[rows, (c * pairs + p) * 128 : (c * pairs + p + 1) * 128] = concat_lanes(
                        [parts[y, c, z, x, :, at : at + HD] for y in range(2)]
                    )
        return carry

    lax.fori_loop(0, zn * 2, body, 0)


def scatter_out(w, parts):
    zn, half = parts.shape[2], parts.shape[4]
    wide = parts.shape[5] // 2
    pairs = wide // HD

    def body(n, carry):
        z, x = n // 2, n % 2
        src = [w[pl.ds(pl.multiple_of(n * 2 * half + h * half, half), half), :] for h in range(2)]
        for y in range(2):
            for c in range(2):
                cols = [(c * pairs + p) * 128 + y * HD for p in range(pairs)]
                parts[y, c, z, x] = concat_lanes([s[:, a : a + HD] for s in src for a in cols]).astype(BF)
        return carry

    lax.fori_loop(0, zn * 2, body, 0)


def rows_kernel(
    tokens_total,
    packed,
    ctx_ref,
    h_ref,
    t_ref,
    m_ref,
    w_in,
    w_bt,
    w_ot,
    par,
    enc_ref,
    gmix_ref,
    gctx_ref,
    gin_ref,
    gbt_ref,
    got_ref,
    vec_ref,
    slope,
    act,
    ginner,
    nlow_t,
    slow_t,
    w_o,
    got,
):
    step = pl.program_id(0)
    tile = h_ref.shape[0]
    units = w_in.shape[0]
    pairs = ctx_ref.shape[1]
    r = pl.ds(pl.multiple_of(step * tile, tile), tile)

    @pl.when(step == 0)
    def _():
        vec_ref[...] = jnp.zeros_like(vec_ref)
        got[...] = jnp.zeros_like(got)
        if packed:
            assemble_out(w_ot, w_o)
        else:
            w_o[...] = w_ot[...]

    gains, biases = par[4:6, :], par[6:10, :]
    scale = tokens_total / par[10:11, 0:1]
    ctx = concat_lanes([ctx_ref[n, p] for n in range(2) for p in range(pairs)])
    mixed = h_ref[...].astype(F32) + dot(ctx, w_o[...], NT) + biases[0:1, :]
    xhat1, rs1 = norm(mixed)
    normed = xhat1 * gains[0:1, :] + biases[1:2, :]
    nlow = normed.astype(BF)
    nlow_t[:, r] = nlow.T
    second = normed + biases[2:3, :]
    for u in range(units):
        inner = dot(nlow, w_in[u], NN) + par[u : u + 1, :]
        a, s = gelu_both(inner)
        a = a.astype(BF)
        act[u, r, :] = a
        slope[u] = s
        second = second + dot(a, w_bt[u], NT)
    xhat2, rs2 = norm(second)
    encoded = xhat2 * gains[1:2, :] + biases[3:4, :]
    enc_ref[...] = encoded
    error = encoded - t_ref[...]
    merr = m_ref[...] * error
    genc = merr * scale
    gsec = norm_back(genc, gains[1:2, :], xhat2, rs2)
    slow = gsec.astype(BF)
    slow_t[:, r] = slow.T
    gnorm = gsec
    for u in range(units):
        gi = (dot(slow, w_bt[u], NN) * slope[u]).astype(BF)
        ginner[u, r, :] = gi
        vec_ref[6 + u : 7 + u, :] += jnp.sum(gi.astype(F32), axis=0, keepdims=True)
        gnorm = gnorm + dot(gi, w_in[u], NT)
    gmix = norm_back(gnorm, gains[0:1, :], xhat1, rs1)
    gmix_ref[...] = gmix
    mlow = gmix.astype(BF)
    gctx = dot(mlow, w_o[...], NN).astype(BF)
    for n in range(2):
        for p in range(pairs):
            gctx_ref[n, p] = gctx[:, (n * pairs + p) * 128 : (n * pairs + p + 1) * 128]
    sums = (gnorm * xhat1, genc * xhat2, gmix, gnorm, gsec, genc)
    for n, value in enumerate(sums):
        vec_ref[n : n + 1, :] += jnp.sum(value, axis=0, keepdims=True)
    vec_ref[10:11, :] += jnp.sum(merr * error, axis=0, keepdims=True)
    got[...] += dot(mlow.T, ctx, NN)

    @pl.when(step == pl.num_programs(0) - 1)
    def _():
        if packed:
            scatter_out(got, got_ref)
        else:
            got_ref[...] = got[...].astype(BF)
        for u in range(units):
            gin_ref[u] = dot(nlow_t[...], ginner[u], NN).astype(BF)
            gbt_ref[u] = dot(slow_t[...], act[u], NN).astype(BF)


def row_pass(tokens_total, ctx, hidden, teacher, mask, w_in, w_bt, w_ot, par, tile):
    n = hidden.shape[0]
    units, _, wide = w_in.shape
    pairs = ctx.shape[1]
    once = pl.Buffered(1)

    def whole(a):
        return pl.BlockSpec(a.shape, lambda i, nd=len(a.shape): (0,) * nd, pipeline_mode=once)

    def rows(width):
        return pl.BlockSpec((tile, width), lambda i: (i, 0))

    heads = pl.BlockSpec((2, pairs, tile, 128), lambda i: (0, 0, i, 0))
    outs = (
        SDS((n, D), F32),
        SDS((n, D), F32),
        SDS((2, pairs, n, 128), BF),
        SDS(w_in.shape, BF),
        SDS(w_in.shape, BF),
        SDS(w_ot.shape, BF),
        SDS((SMALL_ROWS, D), F32),
    )
    return pl.pallas_call(
        functools.partial(rows_kernel, float(tokens_total), len(w_ot.shape) > 2),
        grid=(n // tile,),
        out_shape=outs,
        in_specs=[heads, rows(D), rows(D), rows(1)] + [whole(a) for a in (w_in, w_bt, w_ot, par)],
        out_specs=(rows(D), rows(D), heads) + tuple(whole(a) for a in outs[3:]),
        scratch_shapes=[
            pltpu.VMEM((units, tile, wide), F32),
            pltpu.VMEM((units, n, wide), BF),
            pltpu.VMEM((units, n, wide), BF),
            pltpu.VMEM((D, n), BF),
            pltpu.VMEM((D, n), BF),
            pltpu.VMEM((D, D), BF),
            pltpu.VMEM((D, D), F32),
        ],
        compiler_params=params(62),
        name="row_pass",
    )(ctx, hidden, teacher, mask, w_in, w_bt, w_ot, par)
QKV_ORDERS = ("yxz", "xyz", "yxz")
FFN_ORDERS = ("cyxz", "cxyz", "cyxz", "cxyz")
OUT_ORDER = "cxyz"


def weight_grad(p, hid_t, dq, dk, dv):
    return dot(hid_t[...], concat_lanes([dq[p], dk[p], dv[p]]), NN)


def hidden_grad(dq, dk, dv, w, rows):
    pairs = dq.shape[0]
    return dot(concat_lanes([g[p, rows, :] for g in (dq, dk, dv) for p in range(pairs)]), w[...], NT)


def attend_sum_kernel(
    idx_ref,
    prev_ref,
    last_ref,
    q_ref,
    k_ref,
    v_ref,
    ctx_ref,
    lse_ref,
    gctx_ref,
    hid_ref,
    w_ref,
    gmix_ref,
    gin_ref,
    gbt_ref,
    got_ref,
    vec_ref,
    out_ref,
    sin_ref,
    sbt_ref,
    sot_ref,
    sq_ref,
    vsum_ref,
    send,
    recv,
    here,
    do_ref,
    dq,
    dk,
    dv,
    dk_acc,
    dv_acc,
    dk_run,
    dv_run,
    hid_t,
    gq,
    gh_send,
    gh_recv,
    v_recv,
    v_held,
    *bufs,
):
    place = Place()
    c = place.c
    pairs = q_ref.shape[0]
    local = gmix_ref.shape[0]
    greet(place, "zxyc")
    sems = Sems(send, recv)
    wide = gin_ref.shape[-1]
    halves = (slice(0, wide // 2), slice(wide // 2, wide))
    jobs = []
    rest = list(bufs)
    for grad, out, order, lanes in (
        (gin_ref, sin_ref, FFN_ORDERS[0], halves[0]),
        (gbt_ref, sbt_ref, FFN_ORDERS[1], halves[0]),
        (gin_ref, sin_ref, FFN_ORDERS[2], halves[1]),
        (gbt_ref, sbt_ref, FFN_ORDERS[3], halves[1]),
        (got_ref, sot_ref, OUT_ORDER, None),
    ):
        spec = (order, 0, "yczx", lanes)
        count = len(Scatter.buffers(grad, spec, place.zn))
        jobs.append(Scatter(place, sems, grad, out, spec, rest[:count]))
        rest = rest[count:]
    for p in range(pairs):
        spec = (QKV_ORDERS[p % 3], 0, "yzx", None)
        count = len(Scatter.buffers(gq.at[p], spec, place.zn))
        jobs.append(Scatter(place, sems, gq.at[p], sq_ref.at[p], spec, rest[:count]))
        rest = rest[count:]
    small = SumAll(place, sems, vec_ref, vsum_ref, v_recv, v_held)
    swaps = sems.take(2)
    first = sems.copy(swaps, gctx_ref.at[1 - c], do_ref.at[c], place.peer("c"))
    first.start()
    mine = pltpu.make_async_copy(gctx_ref.at[c], do_ref.at[c], here.at[len(jobs)])
    mine.start()
    start_out = pltpu.make_async_copy(gmix_ref, out_ref, here.at[len(jobs) + 1])
    start_out.start()
    for n in range(5):
        jobs[n].begin(here.at[n])
    for i in range(2):
        hid_t[:, i * local : (i + 1) * local] = hid_ref[i].T
    mine.wait()
    first.wait()

    def advance(n, stage):
        def fn():
            jobs[n].wait(stage, here.at[n])
            jobs[n].add(stage)

        return fn

    due = Due()
    for step, n, stage in (
        (0, 0, 0),
        (1, 1, 0),
        (2, 2, 0),
        (3, 3, 0),
        (4, 4, 0),
        (6, 0, 1),
        (6, 1, 1),
        (9, 0, 2),
        (9, 1, 2),
        (10, 2, 1),
        (10, 3, 1),
        (11, 4, 1),
        (12, 0, 3),
        (12, 1, 3),
        (12, 5, 0),
        (14, 2, 2),
        (14, 3, 2),
        (14, 5, 1),
        (15, 4, 2),
        (15, 6, 0),
        (16, 5, 2),
        (17, 2, 3),
        (17, 3, 3),
        (17, 6, 1),
    ):
        due.add(step, advance(n, stage))
    attend = Backward(
        idx_ref, prev_ref, last_ref, q_ref, k_ref, v_ref, ctx_ref, do_ref, lse_ref, dq, dk, dv,
        dk_acc, dv_acc, dk_run, dv_run,
    )
    half = gq.shape[4]

    def done(p):
        t = weight_grad(p, hid_t, dq, dk, dv).astype(BF)
        for z in range(place.zn):
            for x in range(2):
                at = (z * 2 + x) * 2 * half
                src = [t[at + h * half : at + (h + 1) * half] for h in range(2)]
                for y in range(2):
                    gq[p, y, z, x] = concat_lanes(
                        [s[:, k * 128 + y * HD : k * 128 + (y + 1) * HD] for s in src for k in range(3)]
                    )
        lanes = pl.ds(pl.multiple_of((c * pairs + p) * 128, 128), 128)
        for row, g in ((11, dq), (12, dv)):
            vec_ref[row : row + 1, lanes] = jnp.sum(g[p].astype(F32), axis=0, keepdims=True)
        for n in range(pairs):

            @pl.when(p == n)
            def _(n=n):
                jobs[5 + n].begin(here.at[5 + n])

    attend.run(pairs, due, done)
    small.begin()
    size = local // 4

    def other(i, carry):
        t = hidden_grad(dq, dk, dv, w_ref, pl.ds(pl.multiple_of((1 - c) * local + i * size, size), size))
        gh_send[pl.ds(pl.multiple_of(i * size, size), size), :] = t.astype(BF)
        return carry

    lax.fori_loop(0, 4, other, 0)
    swap = sems.copy(swaps + 1, gh_send, gh_recv, place.peer("c"))
    swap.start()
    start_out.wait()
    small.wait(0)
    small.add(0)
    advance(7, 0)()

    def own(i, carry):
        rows = pl.ds(pl.multiple_of(i * size, size), size)
        t = hidden_grad(dq, dk, dv, w_ref, pl.ds(pl.multiple_of(c * local + i * size, size), size))
        out_ref[rows, :] += t
        return carry

    lax.fori_loop(0, 4, own, 0)
    for n, stage in ((4, 3), (6, 2)):
        advance(n, stage)()
    small.wait(1)
    small.add(1)
    advance(7, 1)()
    swap.wait()

    def last(i, carry):
        rows = pl.ds(pl.multiple_of(i * size, size), size)
        out_ref[rows, :] += gh_recv[rows, :].astype(F32)
        return carry

    lax.fori_loop(0, 4, last, 0)
    small.wait(2)
    small.add(2)
    advance(7, 2)()
    small.wait(3)
    small.add(3)


def attend_sum(tables, q, k, v, ctx, lse, gctx, hid, w, gmix, g_in, g_bt, g_ot, vec, zn, cid):
    pairs, n, _ = q.shape
    local = gmix.shape[0]
    share, wide = g_in.shape[-2:]
    blocks = n // BLK
    packed = g_ot.shape[-2:]
    gq = (pairs, 2, zn, 2) + packed
    heads = pltpu.VMEM((pairs, n, 128), BF)
    half = slice(0, wide // 2)
    bufs = []
    copies = copies_of("cyxz", zn) + 2
    big = [(g_in, order, "yczx", half) for order in FFN_ORDERS]
    for a, order, axes, lanes in big + [(g_ot, OUT_ORDER, "yczx", None)] + [
        (SDS(gq[1:], BF), QKV_ORDERS[p % 3], "yzx", None) for p in range(pairs)
    ]:
        bufs += Scatter.buffers(a, (order, 0, axes, lanes), zn)
        copies += copies_of(order, zn)
    return pl.pallas_call(
        attend_sum_kernel,
        out_shape=(
            SDS((local, D), F32),
            SDS((share, wide), F32),
            SDS((share, wide), F32),
            SDS(packed, F32),
            SDS((pairs,) + packed, F32),
            SDS(vec.shape, F32),
        ),
        in_specs=[SM] * 3 + [VM] * 5 + [ANY, VM, VM, ANY, ANY, ANY, ANY, VM],
        out_specs=(VM,) * 6,
        scratch_shapes=[
            pltpu.SemaphoreType.DMA((copies,)),
            pltpu.SemaphoreType.DMA((copies,)),
            pltpu.SemaphoreType.DMA((7 + pairs,)),
            pltpu.VMEM(gctx.shape, BF),
            heads,
            heads,
            heads,
            pltpu.VMEM((n, 128), F32),
            pltpu.VMEM((n, 128), F32),
            pltpu.VMEM((3 * (blocks - 2) + 1, BLK, 128), F32),
            pltpu.VMEM((3 * (blocks - 2) + 1, BLK, 128), F32),
            pltpu.VMEM((D, n), BF),
            pltpu.VMEM(gq, BF),
            pltpu.VMEM((local, D), BF),
            pltpu.VMEM((local, D), BF),
        ]
        + SumAll.buffers(vec, zn)
        + bufs,
        compiler_params=params(62, cid),
        name="attend_sum",
    )(*tables, q, k, v, ctx, lse, gctx, hid, w, gmix, g_in, g_bt, g_ot, vec)
def small_parts(b_qv, b_in, ln_gains, row_biases, count):
    dp, dpi = lax.axis_size("dp"), lax.axis_index("dp")
    t = lax.axis_index("tensor")
    y, c = t // 2, t % 2

    def at(i, size):
        return (jnp.arange(size) == i).astype(F32)

    heads, hd = b_qv.shape[1:]
    units = at(t, 4)[:, None, None, None] * b_in.astype(F32)[None, :, None, :] * at(dpi, dp)[None, None, :, None]
    rows = jnp.concatenate([ln_gains, row_biases]).astype(F32)
    rows = rows[:, None, :] * at(dpi, dp)[None, :, None] * (t == 0).astype(F32)
    total = count * at(0, D)
    bias = b_qv.astype(F32)[:, None, :, None, None, :] * at(c, 2)[None, :, None, None, None, None]
    bias = bias * at(y, 2)[None, None, None, :, None, None] * at(dpi, dp)[None, None, None, None, :, None]
    out = jnp.concatenate([units.reshape(4, D), rows.reshape(6, D), total.reshape(1, D), bias.reshape(2, D)])
    return jnp.pad(out, ((0, SMALL_ROWS - out.shape[0]), (0, 0)))


def finish(vector, par, encoded, grad_in, s_qkv, s_out, s_in, s_back, b_in, pairs, hd):
    dp, tensor = lax.axis_size("dp"), lax.axis_size("tensor")
    dpi, ti = lax.axis_index("dp"), lax.axis_index("tensor")
    part = dpi * tensor + ti
    cols = D // (dp * tensor)
    gains_biases = lax.dynamic_slice_in_dim(vector[:6], part * cols, cols, 1)
    grad_b_in = lax.dynamic_index_in_dim(vector[6:10].reshape(tensor, b_in.shape[0], dp, hd), ti, 0, False)
    grad_b_in = lax.dynamic_index_in_dim(grad_b_in, dpi, 1, False)
    grad_qv = lax.dynamic_index_in_dim(vector[11:13].reshape(2, 2, pairs, 2, dp, hd), ti % 2, 1, False)
    grad_qv = lax.dynamic_index_in_dim(grad_qv, ti // 2, 2, False)
    grad_qv = lax.dynamic_index_in_dim(grad_qv, dpi, 2, False)
    loss = jnp.sum(vector[10]) / (D * par[10, 0])
    return (
        loss,
        encoded,
        grad_in,
        s_qkv,
        grad_qv,
        s_out,
        s_in,
        grad_b_in,
        s_back,
        gains_biases[:2],
        gains_biases[2:],
    )


def per_device(
    hidden_in, teacher, valid_mask, random_blocks, w_qkv, b_qv, w_out, w_in, b_in, w_back, ln_gains, row_biases
):
    local = hidden_in.shape[0]
    dp, tensor = lax.axis_size("dp"), lax.axis_size("tensor")
    zn = dp // 2
    tokens_total = local * tensor * dp
    c = lax.axis_index("tensor") % 2
    share = ln_gains.shape[1]
    pairs = b_qv.shape[1]
    hd = b_qv.shape[2]
    mask = valid_mask.astype(F32)
    small = small_parts(b_qv, b_in, ln_gains, row_biases, jnp.sum(mask))
    tables = block_tables(random_blocks, c)
    half = share // 2
    wq = jnp.concatenate([w_qkv[k, h * half : (h + 1) * half] for h in range(2) for k in range(3)], axis=1)
    q, k, v, ctx, lse, ctx_rows, hid, w, full_in, full_bt, full_ot, par = gather_attend(
        tables[0], wq, hidden_in, small, w_in, w_back, w_out, pairs, zn, 0
    )
    units = (tensor, D, w_in.shape[1])
    encoded, gmix, gctx, g_in, g_bt, g_ot, vec = row_pass(
        tokens_total, ctx_rows, hidden_in, teacher, mask[:, None], full_in.reshape(units), full_bt.reshape(units),
        full_ot, par, 256,
    )
    grad_in, s_in, s_bt, s_ot, s_q, vector = attend_sum(
        tables, q, k, v, ctx, lse, gctx, hid, w, gmix, g_in.reshape(full_in.shape), g_bt.reshape(full_in.shape),
        g_ot, vec, zn, 1,
    )
    s_qkv = s_q.reshape(pairs, half, 2, 3, HD).transpose(3, 2, 1, 0, 4).reshape(w_qkv.shape)
    s_ot = s_ot.reshape(half, 2, -1).transpose(2, 1, 0).reshape(w_out.shape)
    return finish(vector, par, encoded, grad_in, s_qkv, s_ot, s_in, s_bt.T, b_in, pairs, hd)


def project_attend_kernel(idx_ref, hid_ref, w_ref, b_ref, q_ref, k_ref, v_ref, ctx_ref, lse_ref, lse_t):
    chunk = hid_ref.shape[1] // 2

    def project(i, carry):
        project_rows(i, chunk, hid_ref, w_ref, b_ref[...], q_ref, k_ref, v_ref)
        return carry

    lax.fori_loop(0, 4, project, 0)
    Forward(idx_ref, q_ref, k_ref, v_ref, ctx_ref, lse_ref, lse_t).run(q_ref.shape[0])


def project_attend(idx, hid, w, bias, pairs):
    n = 2 * hid.shape[1]
    heads = SDS((pairs, n, 128), BF)
    blocks = SDS((pairs, n // BLK, BLK, 128), BF)
    return pl.pallas_call(
        project_attend_kernel,
        out_shape=(heads, blocks, blocks, heads, SDS((pairs, n // BLK, 128), F32)),
        in_specs=[SM, VM, VM, VM],
        out_specs=(VM,) * 5,
        scratch_shapes=[pltpu.VMEM((128, 128), F32)],
        compiler_params=params(56),
        name="project_attend",
    )(idx, hid, w, bias)


def attend_back_kernel(
    idx_ref, prev_ref, last_ref, q_ref, k_ref, v_ref, ctx_ref, lse_ref, do_ref, hid_ref, w_ref, gw_ref, gh_ref, gb_ref,
    dq, dk, dv, dk_acc, dv_acc, dk_run, dv_run, hid_t,
):
    pairs = q_ref.shape[0]
    local = hid_ref.shape[1]
    for i in range(2):
        hid_t[:, i * local : (i + 1) * local] = hid_ref[i].T
    attend = Backward(
        idx_ref, prev_ref, last_ref, q_ref, k_ref, v_ref, ctx_ref, do_ref, lse_ref, dq, dk, dv,
        dk_acc, dv_acc, dk_run, dv_run,
    )

    def done(p):
        gw_ref[p] = weight_grad(p, hid_t, dq, dk, dv)
        for n, g in enumerate((dq, dv)):
            gb_ref[p, n : n + 1, :] = jnp.sum(g[p].astype(F32), axis=0, keepdims=True)

    attend.run(pairs, None, done)
    size = local // 4

    def some(i, carry):
        rows = pl.ds(pl.multiple_of(i * size, size), size)
        gh_ref[rows, :] = hidden_grad(dq, dk, dv, w_ref, rows)
        return carry

    lax.fori_loop(0, 8, some, 0)


def attend_back(tables, q, k, v, ctx, lse, do, hid, w):
    pairs, n, _ = q.shape
    slots = 3 * (n // BLK - 2) + 1
    heads = pltpu.VMEM((pairs, n, 128), BF)
    return pl.pallas_call(
        attend_back_kernel,
        out_shape=(SDS((pairs, D, 3 * 128), F32), SDS((n, D), F32), SDS((pairs, 2, 128), F32)),
        in_specs=[SM] * 3 + [VM] * 8,
        out_specs=(VM,) * 3,
        scratch_shapes=[heads] * 3
        + [pltpu.VMEM((n, 128), F32)] * 2
        + [pltpu.VMEM((slots, BLK, 128), F32)] * 2
        + [pltpu.VMEM((D, n), BF)],
        compiler_params=params(60),
        name="attend_back",
    )(*tables, q, k, v, ctx, lse, do, hid, w)


def plain_device(
    hidden_in, teacher, valid_mask, random_blocks, w_qkv, b_qv, w_out, w_in, b_in, w_back, ln_gains, row_biases
):
    local = hidden_in.shape[0]
    dp, tensor = lax.axis_size("dp"), lax.axis_size("tensor")
    tokens_total = local * tensor * dp
    dpi, ti = lax.axis_index("dp"), lax.axis_index("tensor")
    y, c = ti // 2, ti % 2
    pairs, hd = b_qv.shape[1:]
    everyone = ("dp", "tensor")
    mask = valid_mask.astype(F32)
    par = lax.psum(small_parts(b_qv, b_in, ln_gains, row_biases, jnp.sum(mask)), everyone)
    tables = block_tables(random_blocks, c)

    def swap(x):
        there = lax.ppermute(x[1 - c], "tensor", [(i, i ^ 1) for i in range(tensor)])
        here = x[c]
        return jnp.stack([jnp.where(c == 0, here, there), jnp.where(c == 0, there, here)])

    hid = swap(jnp.stack([hidden_in, hidden_in]))
    w = lax.all_gather(lax.all_gather(w_qkv, "dp", axis=1, tiled=True), "tensor", axis=0)
    w = w.reshape(2, 2, 3, D, pairs, HD)[:, c].transpose(2, 1, 3, 0, 4).reshape(D, -1)
    w_o = lax.all_gather(lax.all_gather(w_out, "dp", axis=1, tiled=True), "tensor", axis=0)
    w_o = w_o.reshape(2, 2, pairs, HD, D).transpose(4, 1, 2, 0, 3).reshape(D, D)
    full_in = lax.all_gather(lax.all_gather(w_in, "dp", axis=0, tiled=True), "tensor", axis=0)
    full_bt = lax.all_gather(lax.all_gather(w_back.T, "dp", axis=0, tiled=True), "tensor", axis=0)
    bias = lax.dynamic_index_in_dim(par[11:13].reshape(2, 2, -1), c, 1, False)
    q, k, v, ctx, lse = project_attend(tables[0], hid, w, bias, pairs)
    ctx_rows = swap(ctx.reshape(pairs, 2, local, 128).swapaxes(0, 1))
    encoded, gmix, gctx, g_in, g_bt, g_ot, vec = row_pass(
        tokens_total, ctx_rows, hidden_in, teacher, mask[:, None], full_in, full_bt, w_o, par, 256
    )
    gw, gh, gb = attend_back(tables, q, k, v, ctx, lse, swap(gctx), hid, w)
    there = lax.ppermute(gh.reshape(2, local, D)[1 - c].astype(BF), "tensor", [(i, i ^ 1) for i in range(tensor)])
    grad_in = gmix + gh.reshape(2, local, D)[c] + there.astype(F32)

    def spread(g):
        g = lax.psum_scatter(g, "tensor", scatter_dimension=0, tiled=False)
        return lax.psum_scatter(g, "dp", scatter_dimension=0, tiled=True)

    s_in, s_bt = spread(g_in.astype(F32)), spread(g_bt.astype(F32))
    s_ot = spread(g_ot.astype(F32).reshape(D, 2, pairs, 2, HD).transpose(3, 1, 0, 2, 4).reshape(tensor, D, -1))
    own = (jnp.arange(2) == c).astype(F32)
    gw = gw.reshape(pairs, D, 3, 2, HD).transpose(3, 1, 2, 0, 4).reshape(2, 1, D, -1) * own[None, :, None, None]
    s_qkv = spread(gw.reshape(tensor, D, -1)).reshape(-1, 3, pairs * HD).swapaxes(0, 1)
    gb = gb.swapaxes(0, 1).reshape(2, 1, -1) * own[None, :, None]
    vector = lax.psum(vec.at[11:13].set(gb.reshape(2, D)), everyone)
    return finish(vector, par, encoded, grad_in, s_qkv, s_ot.T, s_in, s_bt.T, b_in, pairs, hd)


def solution(mesh):
    rows = P(("dp", "tensor"), None)
    in_specs = (
        rows,
        rows,
        P(("dp", "tensor")),
        P(),
        P(None, "dp", "tensor"),
        P(None, "tensor", "dp"),
        P("tensor", "dp"),
        P("dp", "tensor"),
        P("tensor", "dp"),
        P("tensor", "dp"),
        P(None, "dp"),
        P(None, "dp"),
    )
    out_specs = (
        P(),
        rows,
        rows,
        P(None, "dp", "tensor"),
        P(None, "tensor", "dp"),
        P("tensor", "dp"),
        P("dp", "tensor"),
        P("tensor", "dp"),
        P("tensor", "dp"),
        P(None, ("dp", "tensor")),
        P(None, ("dp", "tensor")),
    )
    fills_tiles = (D // mesh.shape["dp"]) % 32 == 0
    step = per_device if fills_tiles else plain_device
    return jax.shard_map(step, mesh=mesh, in_specs=in_specs, out_specs=out_specs, check_vma=False)
```

time: 451 us -> 326 us (0.72); the launches traced: 443 us -> 325 us
  Pallas kernels: 387 us -> 292 us
  local copies, waits for them, and re-layouts: 42 us -> 23.3 us
    pallas_call x9 -> x3, Pallas kernels: 387 us -> 292 us  [the longest x1 126 us: attend_sum(): pl.pallas_call(attend_sum_kernel, out_shape=(SDS((local, D), F32), SDS((s...]
    unnamed x54 -> x18, local copies, waits for them, and re-layouts: 24.7 us -> 6.17 us
where the time goes in v2:
time: 326 us; the launch traced here: 325 us
  Pallas kernels  292 us (90%)
  local copies, waits for them, and re-layouts  23.3 us (7%)
  other arithmetic  6.43 us (2%)
  between operations  3.4 us (1%)
    pallas_call x1, Pallas kernels, attend_sum(): pl.pallas_call(attend_sum_kernel, out_shape=(SDS((local, D), F32), SDS((s...  126 us
    pallas_call x1, Pallas kernels, gather_attend(): pl.pallas_call(functools.partial(gather_attend_kernel, cuts), out_shape=(...  110 us
    pallas_call x1, Pallas kernels, row_pass(): pl.pallas_call(functools.partial(rows_kernel, float(tokens_total), len(w_...  55.9 us

profile of v2, /device:TPU:0, one launch (start us, length us, event | category | flops | bytes accessed | tf_op | source)
XLA Modules:
  0.0 325.3 jit_solution(4448335494993533633)
XLA Ops:
  0.7 0.7 copy.51
  1.9 0.8 copy.50
  3.2 0.7 maximum_convert_fusion
  4.0 1.3 convert_reduce_fusion
  6.6 1.4 select_reduce_fusion
  8.1 0.7 reduce_sum.30.idx_ref
  8.8 0.8 slice_bitcast_fusion
  9.6 0.8 concatenate.13.wq_ref
  10.4 1.7 copy.52.wb_ref
  12.1 110.5 %gather_attend.1 = (bf16[3,2048,128]{2,1,0:T(8,128)(2,1)}, bf16[3,32,64,128]{3,2,1,0:T(8,128)(2,1)}, bf16[3,32,64,128]{3,2,1,0:T(8,128)(2,1)}, bf16[3,2048,128]{...) custom-call(s32[6,96]{1,0:T(8,128)} %reduce_sum.30.idx_ref, ...), custom_call_target="tpu_custom_call" | custom-call | tf_op jit(solution)/shard_map/gather_attend/pallas_call | solution.py:765
  122.6 1.0 copy.53.m_ref
  123.7 55.9 %row_pass.1 = (f32[1024,768]{1,0:T(8,128)}, f32[1024,768]{1,0:T(8,128)}, bf16[2,3,1024,128]{3,2,1,0:T(8,128)(2,1)}, bf16[4,768,768]{2,1,0:T(8,128)(2,1)}, bf16[4...) custom-call(bf16[2,3,1024,128]{3,2,1,0:T(8,128)(2,1)} %get-tuple-element.41.ctx_ref, ...), custom_call_target="tpu_custom_call" | custom-call | tf_op jit(solution)/shard_map/row_pass/pallas_call | solution.py:971
  179.6 0.9 select_reduce_fusion.1.prev_ref
  181.1 125.8 %attend_sum.1 = (f32[1024,768]{1,0:T(8,128)}, f32[96,768]{1,0:T(8,128)}, f32[96,768]{1,0:T(8,128)}, f32[48,384]{1,0:T(8,128)}, f32[3,48,384]{2,1,0:T(8,128)}, /*index=5*/f32[16,768]{1,0:T(8,128)}) custom-call(s32[6,96]{1,0:T(8,128)} %reduce_sum.30.idx_ref, s32[6,96]{1,0:T(8,128)} %select_reduce_fusion.1.prev_ref, s32[6,32]{1,0:T(8,128)} %reduce_max.22.last_ref, ...), custom_call_target="tpu_custom_call" | custom-call | tf_op jit(solution)/shard_map/attend_sum/pallas_call | solution.py:1207
  306.9 2.2 reshape.204
  309.0 2.2 copy.54
  311.2 2.1 reshape.205
  313.4 1.0 reshape.207
  314.4 0.7 copy.58
  315.3 0.7 copy.57
  318.5 1.2 slice.46
  321.1 1.7 copy.65
  322.7 0.7 copy.66
  323.4 0.7 copy.67
  (55 shorter events, 5.8 us)
Async XLA Ops:
  0.6 122.0 %copy-start.5 = (s32[1024]{0:T(1024)S(1)}, s32[1024]{0:T(1024)}, u32[]{:S(2)}) copy-start(s32[1024]{0:T(1024)} %param.14) | copy-start | bytes 12292
  123.7 55.9 %copy-start.3 = (s32[6,96]{1,0:T(8,128)S(1)}, s32[6,96]{1,0:T(8,128)}, u32[]{:S(2)}) copy-start(s32[6,96]{1,0:T(8,128)} %reduce_sum.30.idx_ref) | copy-start | bytes 6916
  306.9 8.3 %copy-start.4 = (f32[16,768]{1,0:T(8,128)S(1)}, f32[16,768]{1,0:T(8,128)}, u32[]{:S(2)}) copy-start(f32[16,768]{1,0:T(8,128)} %get-tuple-element.54) | copy-start | bytes 147460
  306.9 14.2 %copy-start = (f32[1024,768]{1,0:T(8,128)S(1)}, f32[1024,768]{1,0:T(8,128)}, u32[]{:S(2)}) copy-start(f32[1024,768]{1,0:T(8,128)} %get-tuple-element.115) | copy-start | bytes 9437188
  321.0 1.7 copy-start.2
  321.0 2.4 copy-start.1

commit v3 on v2

--- a/solution.py
+++ b/solution.py
@@ -104,7 +104,7 @@
 class Gather:
     def __init__(self, place, sems, shard, out, spec):
         self.place, self.shard, self.out = place, shard, out
-        self.order, self.pre, self.axes, self.lanes = spec
+        self.order, self.pre, self.axes, self.cut = spec
         self.sems = sems
         self.base = sems.take(copies_of(self.order, place.zn))
 
@@ -113,15 +113,10 @@
         own = {"y": p.y, "c": p.c, "z": p.z, "x": p.x}
         idx = (slice(None),) * self.pre
         idx += tuple(slice(None) if a in whole else own[a] for a in self.axes)
-        if self.lanes is not None:
-            idx += (slice(None),) * (len(self.out.shape) - len(idx) - 1) + (self.lanes,)
-        return self.out.at[idx]
+        return self.out.at[idx + self.cut]
 
     def mine(self):
-        ref = self.shard
-        if self.lanes is None:
-            return ref
-        return ref.at[(slice(None),) * (len(ref.shape) - 1) + (self.lanes,)]
+        return self.shard.at[(slice(None),) * self.pre + self.cut] if self.cut else self.shard
 
     def local(self, sem):
         return pltpu.make_async_copy(self.mine(), self.piece(""), sem)
@@ -150,7 +145,7 @@
 class Scatter:
     def __init__(self, place, sems, grad, out, spec, bufs):
         self.place, self.sems, self.grad, self.out = place, sems, grad, out
-        self.order, self.pre, self.axes, self.lanes = spec
+        self.order, self.pre, self.axes, self.cut = spec
         self.base = sems.take(copies_of(self.order, place.zn))
         self.keep, self.recv, self.send = bufs[0], [bufs[1]] + list(bufs[2::2]), [None] + list(bufs[3::2])
         self.own = {"y": place.y, "c": place.c, "z": place.z, "x": place.x}
@@ -158,11 +153,10 @@
 
     @staticmethod
     def buffers(a, spec, zn):
-        order, pre, axes, lanes = spec
+        order, pre, axes, cut = spec
         size = {"y": 2, "c": 2, "z": zn, "x": 2}
         lead, tail = a.shape[:pre], a.shape[pre + len(axes) :]
-        if lanes is not None:
-            tail = tail[:-1] + (lanes.stop - lanes.start,)
+        tail = tuple(len(range(*s.indices(d))) for s, d in zip(cut, tail)) + tail[len(cut) :]
         out = []
         for n, axis in enumerate(order):
             after = tuple(size[s] for s in axes if s not in order[: n + 1])
@@ -186,10 +180,9 @@
         return [self.sems.copy(at, self.half(1 - self.own[axis]) if stage == 0 else send, recv, p.peer(axis))]
 
     def half(self, i):
-        idx = (slice(None),) * (self.pre + self.axes.index(self.order[0])) + (i,)
-        if self.lanes is not None:
-            idx += (slice(None),) * (len(self.grad.shape) - len(idx) - 1) + (self.lanes,)
-        return self.grad.at[idx]
+        first = self.order[0]
+        idx = (slice(None),) * self.pre + tuple(i if a == first else slice(None) for a in self.axes)
+        return self.grad.at[idx + self.cut]
 
     def kept(self, here):
         return pltpu.make_async_copy(self.half(self.own[self.order[0]]), self.keep, here)
@@ -241,10 +234,7 @@
         if n == len(self.order) - 1:
 
             def last(lead, coords):
-                if self.lanes is None:
-                    self.out[lead] = self.total(n, lead, coords)
-                else:
-                    self.out[lead + (slice(None), self.lanes)] = self.total(n, lead, coords)
+                self.out[lead + self.cut] = self.total(n, lead, coords)
 
             self.each("", last)
             return
@@ -271,15 +261,15 @@
 
 
 class SumAll:
-    order = "cyxz"
-
-    def __init__(self, place, sems, value, out, recv, held):
+    def __init__(self, place, sems, value, out, order, recv, held):
+        self.order = order
         self.place, self.sems, self.value, self.out, self.recv, self.held = place, sems, value, out, recv, held
         self.base = sems.take(copies_of(self.order, place.zn))
 
     @staticmethod
-    def buffers(a, zn):
-        return [pltpu.VMEM((2 + zn,) + a.shape, F32), pltpu.VMEM((3,) + a.shape, F32)]
+    def buffers(a, order, zn):
+        hops = len(order)
+        return [pltpu.VMEM((hops - 2 + zn,) + a.shape, F32), pltpu.VMEM((hops - 1,) + a.shape, F32)]
 
     def copies(self, n):
         p = self.place
@@ -291,16 +281,16 @@
             for k in range(1, p.zn if axis == "z" else 2)
         ]
 
-    def begin(self):
+    def begin(self, here=None):
         self.copies(0)[0].start()
 
-    def wait(self, n):
+    def wait(self, n, here=None):
         for copy in self.copies(n):
             copy.wait()
 
     def add(self, n):
         mine = self.value[...] if n == 0 else self.held[n - 1]
-        if n == 3:
+        if n == len(self.order) - 1:
             for k in range(self.place.zn - 1):
                 mine = mine + self.recv[n + k]
             self.out[...] = mine
@@ -308,6 +298,44 @@
         self.held[n] = mine + self.recv[n]
         for copy in self.copies(n + 1):
             copy.start()
+
+
+AFTER = 90
+
+
+class Due:
+    def __init__(self):
+        self.todo = {}
+
+    def add(self, step, fn):
+        self.todo.setdefault(step, []).append(fn)
+
+    def now(self, step):
+        for fn in self.todo.get(step, []):
+            fn()
+
+    def __call__(self, g, first=0, last=AFTER):
+        for step, fns in sorted(self.todo.items()):
+            if first <= step < last:
+
+                @pl.when(g == step - first)
+                def _(fns=fns):
+                    for fn in fns:
+                        fn()
+
+
+def relay(table, jobs, waves, window, finish):
+    due, stage, behind = Due(), {}, list(waves[window:])
+    for step, name in table:
+        n = stage.get(name, 0)
+        stage[name] = n + 1
+        wave = [w for w in waves if name in w]
+        begin = []
+        if n == 0 and behind and wave and all(stage.get(other) for other in wave[0]):
+            begin = behind.pop(0)
+        due.add(step, functools.partial(finish, name, n, begin))
+    assert not behind and all(stage.get(name) == len(job.order) for name, job in jobs.items())
+    return due
 
 
 UNROLL = 5
@@ -545,70 +573,128 @@
 SMALL_ROWS = 16
 
 
-class Due:
-    def __init__(self):
-        self.todo = {}
-
-    def add(self, step, fn):
-        self.todo.setdefault(step, []).append(fn)
-
-    def __call__(self, g):
-        for step, fns in self.todo.items():
-
-            @pl.when(g == step)
-            def _(fns=fns):
-                for fn in fns:
-                    fn()
-
-
-def assemble_qkv(parts, w, pairs):
-    zn, half = parts.shape[1], parts.shape[3]
-    wide = parts.shape[4] // 2
+FORWARD_TABLE = (
+    (-1000, "q0b"),
+    (-999, "q1b"),
+    (-998, "q0a"),
+    (-997, "q1a"),
+    (-996, "q0b"),
+    (-995, "q1b"),
+    (-994, "q0a"),
+    (-993, "q1a"),
+    (-992, "q2b"),
+    (-991, "q0b"),
+    (-990, "q1b"),
+    (-989, "q2a"),
+    (-988, "a0"),
+    (-987, "b0"),
+    (-986, "q2b"),
+    (-985, "q1a"),
+    (-984, "q0a"),
+    (-983, "q2a"),
+    (-982, "q2b"),
+    (-981, "b0"),
+    (-980, "a0"),
+    (-979, "a1"),
+    (-978, "b1"),
+    (-977, "q2a"),
+    (0, "o"),
+    (1, "a2"),
+    (1, "b2"),
+    (5, "a1"),
+    (6, "b0"),
+    (6, "a2"),
+    (7, "o"),
+    (7, "b1"),
+    (9, "b0"),
+    (9, "b2"),
+    (11, "a0"),
+    (14, "a0"),
+    (16, "a1"),
+    (17, "a2"),
+    (17, "o"),
+    (18, "a1"),
+    (19, "b1"),
+    (20, "b2"),
+    (20, "o"),
+    (20, "a2"),
+    (AFTER, "b1"),
+    (AFTER, "b2"),
+)
+FORWARD_WINDOW = 2
+
+
+def assemble_qkv(p, parts, w):
+    zn, half = parts.shape[2], parts.shape[4]
 
     def body(n, carry):
         z, x = n // 2, n % 2
         for h in range(2):
             rows = pl.ds(pl.multiple_of(n * 2 * half + h * half, half), half)
-            src = [parts[y, z, x, :, h * wide : (h + 1) * wide] for y in range(2)]
-            for kp in range(3 * pairs):
-                w[rows, kp * 128 : (kp + 1) * 128] = jnp.concatenate(
-                    [s[:, kp * HD : (kp + 1) * HD] for s in src], axis=1
-                )
+            src = [parts[p, y, z, x, :, h * 3 * HD : (h + 1) * 3 * HD] for y in range(2)]
+            for k in range(3):
+                w[p, rows, k * 128 : (k + 1) * 128] = concat_lanes([s[:, k * HD : (k + 1) * HD] for s in src])
         return carry
 
     lax.fori_loop(0, zn * 2, body, 0)
 
 
-def project_rows(i, chunk, hid, w, bias, q, k, v):
-    pairs = q.shape[0]
-    e = pairs * 128
+def project_rows(p, i, chunk, hid, w, bias, q, k, v):
     per = hid.shape[1] // chunk
     src = hid[i // per, pl.ds(pl.multiple_of(i % per * chunk, chunk), chunk), :]
-    rows = pl.ds(pl.multiple_of(i * chunk, chunk), chunk)
-    t = dot(src, w[...], NN)
-    for n, out in enumerate((q, k, v)):
-        part = t[:, n * e : (n + 1) * e]
-        if n == 0:
-            part = (part + bias[0:1, :]).astype(BF).astype(F32) * 0.125
-        if n == 2:
-            part = part + bias[1:2, :]
-        part = part.astype(BF)
-        for p in range(pairs):
-            one = part[:, p * 128 : (p + 1) * 128]
-            if n == 0:
-                out[p, rows, :] = one
-            else:
-                out[p, pl.ds(i * (chunk // BLK), chunk // BLK)] = one.reshape(chunk // BLK, BLK, 128)
+    t = dot(src, w[p], NN)
+    part = (t[:, :128] + bias[0:1, :]).astype(BF).astype(F32) * 0.125
+    q[p, pl.ds(pl.multiple_of(i * chunk, chunk), chunk), :] = part.astype(BF)
+    rows = pl.ds(i * (chunk // BLK), chunk // BLK)
+    k[p, rows] = t[:, 128:256].astype(BF).reshape(chunk // BLK, BLK, 128)
+    v[p, rows] = (t[:, 256:] + bias[1:2, :]).astype(BF).reshape(chunk // BLK, BLK, 128)
+
+
+def place_small(place, out, b_qv, b_in, ln_gains, row_biases, mask):
+    def lane(rows):
+        return lax.broadcasted_iota(jnp.int32, (rows, D), 1)
+
+    def row(rows):
+        return lax.broadcasted_iota(jnp.int32, (rows, D), 0)
+
+    def ones(where):
+        return where.astype(F32).astype(BF)
+
+    dp = place.z * 2 + place.x
+    t = place.y * 2 + place.c
+    pairs, _, n = b_qv.shape
+    units = b_in.shape[1]
+    share = ln_gains.shape[1]
+    out[...] = jnp.zeros_like(out)
+    wide = dot(b_in[...], ones(lane(units) // HD == row(units)), NN)
+    own = jnp.sum(jnp.where(lane(n) % HD == dp * n + row(n), wide, 0.0), axis=0, keepdims=True)
+    for i in range(4):
+        out[i : i + 1, :] = jnp.where(t == i, own, 0.0)
+    at = ones(lane(share) == dp * share + row(share))
+    one = jnp.where(t == 0, 1.0, 0.0)
+    out[4:6, :] = dot(ln_gains[...], at, NN) * one
+    out[6:10, :] = dot(row_biases[...], at, NN) * one
+    count = jnp.sum(mask[...].astype(F32))
+    out[10:11, :] = jnp.where(lane(1) == 0, count, 0.0)
+    at = ones(lane(n) % HD == dp * n + row(n))
+    total = jnp.zeros((2, D), F32)
+    for p in range(pairs):
+        here = (lane(2) // 128 == place.c * pairs + p) & (lane(2) % 128 // HD == place.y)
+        total = total + jnp.where(here, dot(b_qv[p], at, NN), 0.0)
+    out[11:13, :] = total
 
 
 def gather_attend_kernel(
-    cuts,
     idx_ref,
-    wq_ref,
+    wqkv_ref,
     h_ref,
-    small_ref,
+    bqv_ref,
+    bin_ref,
+    gain_ref,
+    rowb_ref,
+    mask_ref,
     win_ref,
-    wb_ref,
+    wbt,
     wo_ref,
     q_ref,
     k_ref,
@@ -616,7 +702,7 @@
     ctx_ref,
     lse_ref,
     rows_ref,
-    hid_ref,
+    hidt_ref,
     w_ref,
     fin_ref,
     fbt_ref,
@@ -625,8 +711,10 @@
     send,
     recv,
     here,
+    hid_ref,
+    wq,
     parts,
-    wbt,
+    small_ref,
     wot,
     s_recv,
     s_held,
@@ -636,134 +724,114 @@
     c = place.c
     local = h_ref.shape[0]
     pairs = q_ref.shape[0]
+    share = win_ref.shape[0]
+    half = share // 2
+    for p in range(pairs):
+        cols = slice(p * HD, (p + 1) * HD)
+        wq[p] = concat_lanes([wqkv_ref[k, h * half : (h + 1) * half, cols] for h in range(2) for k in range(3)])
     greet(place, "zxyc")
     sems = Sems(send, recv)
-    qkv = [
-        Gather(place, sems, wq_ref, parts, ("zxy" if n % 2 == 0 else "zyx", 0, "yzx", slice(a, b)))
-        for n, (a, b) in enumerate(cuts)
-    ]
-    hid = Gather(place, sems, h_ref, hid_ref, ("c", 0, "c", None))
-    small = SumAll(place, sems, small_ref, par_ref, s_recv, s_held)
-    half = win_ref.shape[1] // 2
-    lo, hi = slice(0, half), slice(half, 2 * half)
-    ffn = [
-        Gather(place, sems, win_ref, fin_ref, ("zxyc", 0, "yczx", lo)),
-        Gather(place, sems, wbt, fbt_ref, ("zyxc", 0, "yczx", lo)),
-        Gather(place, sems, win_ref, fin_ref, ("zxyc", 0, "yczx", hi)),
-        Gather(place, sems, wbt, fbt_ref, ("zyxc", 0, "yczx", hi)),
-        Gather(place, sems, wot, fot_ref, ("zyxc", 0, "yczx", None)),
-    ]
+    jobs, waves = {}, []
+    for p in range(pairs):
+        orders = ("zxy", "zyx") if p % 2 == 0 else ("zyx", "zxy")
+        lanes = (slice(0, 2 * 128), slice(2 * 128, 3 * 128))
+        for name, order, lane in zip("ab", orders, lanes):
+            spec = (order, 0, "yzx", (slice(None), lane))
+            jobs[f"q{p}{name}"] = Gather(place, sems, wq.at[p], parts.at[p], spec)
+        waves.append([f"q{p}a", f"q{p}b"])
+    count = 3
+    size = share // count
+    for n in range(count):
+        rows = (slice(n * size, (n + 1) * size),)
+        jobs[f"a{n}"] = Gather(place, sems, win_ref, fin_ref, ("zxyc", 0, "yczx", rows))
+        jobs[f"b{n}"] = Gather(place, sems, wbt, fbt_ref, ("zyxc", 0, "yczx", rows))
+        waves.append([f"a{n}", f"b{n}"])
+    jobs["o"] = Gather(place, sems, wot, fot_ref, ("zyxc", 0, "yczx", ()))
+    waves[-1].append("o")
+    hid = Gather(place, sems, h_ref, hid_ref, ("c", 0, "c", ()))
+    small = SumAll(place, sems, small_ref, par_ref, "cyxz", s_recv, s_held)
     swap_at = sems.take(pairs)
-    for chunk in qkv:
-        chunk.start(0)
+    for wave in waves[:FORWARD_WINDOW]:
+        for name in wave:
+            jobs[name].start(0)
     hid.start(0)
-    small.begin()
-    own = [pltpu.make_async_copy(wq_ref, parts.at[place.y, place.z, place.x], here.at[0]), hid.local(here.at[1])]
+    own = [pltpu.make_async_copy(wq.at[p], parts.at[p, place.y, place.z, place.x], here.at[p]) for p in range(pairs)]
+    own.append(hid.local(here.at[pairs]))
     for copy in own:
         copy.start()
-    wbt[...] = wb_ref[...].T
+    place_small(place, small_ref, bqv_ref, bin_ref, gain_ref, rowb_ref, mask_ref)
+    small.begin()
     t = wo_ref[...].T
-    hr = wot.shape[0]
-    wot[...] = concat_lanes([t[:hr], t[hr:]])
+    wot[...] = concat_lanes([t[:half], t[half:]])
     late = [
-        pltpu.make_async_copy(src, out.at[place.y, c, place.z, place.x], here.at[2 + n])
+        pltpu.make_async_copy(src, out.at[place.y, c, place.z, place.x], here.at[pairs + 1 + n])
         for n, (src, out) in enumerate(((win_ref, fin_ref), (wbt, fbt_ref), (wot, fot_ref)))
     ]
     for copy in late:
         copy.start()
-    for copy in own:
+    for copy in own + late:
         copy.wait()
-    small.wait(0)
-    small.add(0)
-    for chunk in qkv:
-        chunk.wait(0)
-        chunk.start(1)
-    small.wait(1)
-    small.add(1)
-    for chunk in ffn:
-        chunk.start(0)
-    for chunk in qkv:
-        chunk.wait(1)
-        chunk.start(2)
-    small.wait(2)
-    small.add(2)
-    for copy in late:
-        copy.wait()
-    hid.wait(0)
-    small.wait(3)
-    small.add(3)
-    for chunk in qkv:
-        chunk.wait(2)
-    assemble_qkv(parts, w_ref, pairs)
-
-    def pass_on(n, stage):
-        def fn():
-            ffn[n].wait(stage)
-            ffn[n].start(stage + 1)
-
-        return fn
-
-    early, due = Due(), Due()
-    for step, n, stage in ((0, 0, 0), (0, 1, 0), (1, 2, 0), (3, 3, 0)):
-        early.add(step, pass_on(n, stage))
-    for step, n, stage in (
-        (0, 4, 0),
-        (0, 0, 1),
-        (1, 1, 1),
-        (3, 2, 1),
-        (4, 3, 1),
-        (6, 4, 1),
-        (6, 0, 2),
-        (8, 1, 2),
-        (12, 2, 2),
-        (15, 3, 2),
-        (17, 4, 2),
-    ):
-        due.add(step, pass_on(n, stage))
-    e = pairs * 128
-    bias = jnp.where(c == 0, par_ref[11:13, :e], par_ref[11:13, e:])
-    chunk_rows = local // 2
-
-    def project(i, carry):
-        early(i)
-        project_rows(i, chunk_rows, hid_ref, w_ref, bias, q_ref, k_ref, v_ref)
-        return carry
-
-    lax.fori_loop(0, 4, project, 0)
+
+    def pass_on(name, stage, begin):
+        jobs[name].wait(stage)
+        if stage + 1 < len(jobs[name].order):
+            jobs[name].start(stage + 1)
+        for other in begin:
+            jobs[other].start(0)
+
+    due = relay(FORWARD_TABLE, jobs, waves, FORWARD_WINDOW, pass_on)
+    early = sorted(step for step in due.todo if step < 0)
+    for n, step in enumerate(early):
+        due.now(step)
+        if n == 1:
+            hid.wait(0)
+            for i in range(2):
+                hidt_ref[:, i * local : (i + 1) * local] = hid_ref[i].T
+        if n < 4:
+            small.wait(n)
+            small.add(n)
+    chunk = local // 2
     attend = Forward(idx_ref, q_ref, k_ref, v_ref, ctx_ref, lse_ref, lse_t)
-    attend.run(pairs, due)
 
     def there(p):
         rows = pl.ds(pl.multiple_of((1 - c) * local, local), local)
         return sems.copy(swap_at + p, ctx_ref.at[p, rows, :], rows_ref.at[c, p], place.peer("c"))
 
+    bias = jnp.where(c == 0, par_ref[11:13, : pairs * 128], par_ref[11:13, pairs * 128 :])
+    for p in range(pairs):
+        assemble_qkv(p, parts, w_ref)
+
+    def project(i, carry):
+        due(i, 0, 4)
+        for p in range(pairs):
+            project_rows(p, i, chunk, hid_ref, w_ref, bias[:, p * 128 : (p + 1) * 128], q_ref, k_ref, v_ref)
+        return carry
+
+    lax.fori_loop(0, 4, project, 0)
+    attend.run(pairs, lambda g: due(g, 4))
     for p in range(pairs):
         there(p).start()
     mine = pltpu.make_async_copy(
         ctx_ref.at[:, pl.ds(pl.multiple_of(c * local, local), local), :], rows_ref.at[c], here.at[0]
     )
     mine.start()
-    for chunk in ffn:
-        chunk.wait(3)
+    due.now(AFTER)
     mine.wait()
     for p in range(pairs):
         there(p).wait()
 
 
-def gather_attend(idx, wq, hidden, small, w_in, w_back, w_out, pairs, zn, cid):
+def gather_attend(idx, w_qkv, hidden, smalls, w_in, w_bt, w_out, pairs, zn, cid):
     local = hidden.shape[0]
     n = 2 * local
-    e = pairs * 128
     share, wide = w_in.shape
-    width = wq.shape[1]
-    step = width // 128 // 4 * 128
-    cuts = [(i * step, (i + 1) * step if i < 3 else width) for i in range(4)]
     heads_shape = SDS((pairs, n, 128), BF)
     blocks_shape = SDS((pairs, n // BLK, BLK, 128), BF)
-    wot = (share // 2, 2 * w_out.shape[0])
-    copies = 4 * copies_of("zxy", zn) + 1 + copies_of("cyxz", zn) + 5 * copies_of("zxyc", zn) + pairs
+    packed = (share // 2, 6 * HD)
+    small = SDS((SMALL_ROWS, D), F32)
+    copies = 2 * pairs * copies_of("zxy", zn) + 1 + copies_of("cyxz", zn) + 7 * copies_of("zxyc", zn) + pairs
     return pl.pallas_call(
-        functools.partial(gather_attend_kernel, cuts),
+        gather_attend_kernel,
         out_shape=(
             heads_shape,
             blocks_shape,
@@ -771,28 +839,30 @@
             heads_shape,
             SDS((pairs, n // BLK, 128), F32),
             SDS((2, pairs, local, 128), BF),
-            SDS((2, local, D), BF),
-            SDS((D, 3 * e), BF),
+            SDS((D, n), BF),
+            SDS((pairs, D, 3 * 128), BF),
             SDS((2, 2, zn, 2, share, wide), BF),
             SDS((2, 2, zn, 2, share, wide), BF),
-            SDS((2, 2, zn, 2) + wot, BF),
+            SDS((2, 2, zn, 2) + packed, BF),
             SDS(small.shape, F32),
         ),
-        in_specs=[SM, ANY, ANY, VM, ANY, VM, VM],
+        in_specs=[SM, VM, ANY] + [VM] * len(smalls) + [ANY, ANY, VM],
         out_specs=(VM,) * 5 + (ANY, VM, VM, ANY, ANY, ANY, VM),
         scratch_shapes=[
             pltpu.SemaphoreType.DMA((copies,)),
             pltpu.SemaphoreType.DMA((copies,)),
-            pltpu.SemaphoreType.DMA((5,)),
-            pltpu.VMEM((2, zn, 2) + wq.shape, BF),
-            pltpu.VMEM((share, wide), BF),
-            pltpu.VMEM(wot, BF),
+            pltpu.SemaphoreType.DMA((pairs + 4,)),
+            pltpu.VMEM((2, local, D), BF),
+            pltpu.VMEM((pairs,) + packed, BF),
+            pltpu.VMEM((pairs, 2, zn, 2) + packed, BF),
+            pltpu.VMEM(small.shape, F32),
+            pltpu.VMEM(packed, BF),
         ]
-        + SumAll.buffers(small, zn)
+        + SumAll.buffers(small, "cyxz", zn)
         + [pltpu.VMEM((128, 128), F32)],
         compiler_params=params(56, cid),
         name="gather_attend",
-    )(idx, wq, hidden, small, w_in, w_back, w_out)
+    )(idx, w_qkv, hidden, *smalls, w_in, w_bt, w_out)
 def norm(v):
     centred = v - jnp.mean(v, axis=-1, keepdims=True)
     rs = lax.rsqrt(jnp.mean(centred * centred, axis=-1, keepdims=True) + epsilon)
@@ -848,6 +918,16 @@
         return carry
 
     lax.fori_loop(0, zn * 2, body, 0)
+
+
+def mask_rows(m_ref, step, tile):
+    columns = m_ref[...].astype(F32).T
+    at = lax.broadcasted_iota(jnp.int32, columns.shape, 1)
+    per = tile // 128
+    parts = [
+        jnp.sum(jnp.where(at == step * per + i, columns, 0.0), axis=1, keepdims=True) for i in range(per)
+    ]
+    return jnp.concatenate(parts, axis=0)
 
 
 def rows_kernel(
@@ -911,7 +991,7 @@
     encoded = xhat2 * gains[1:2, :] + biases[3:4, :]
     enc_ref[...] = encoded
     error = encoded - t_ref[...]
-    merr = m_ref[...] * error
+    merr = mask_rows(m_ref, step, tile) * error
     genc = merr * scale
     gsec = norm_back(genc, gains[1:2, :], xhat2, rs2)
     slow = gsec.astype(BF)
@@ -972,7 +1052,7 @@
         functools.partial(rows_kernel, float(tokens_total), len(w_ot.shape) > 2),
         grid=(n // tile,),
         out_shape=outs,
-        in_specs=[heads, rows(D), rows(D), rows(1)] + [whole(a) for a in (w_in, w_bt, w_ot, par)],
+        in_specs=[heads, rows(D), rows(D)] + [whole(a) for a in (mask, w_in, w_bt, w_ot, par)],
         out_specs=(rows(D), rows(D), heads) + tuple(whole(a) for a in outs[3:]),
         scratch_shapes=[
             pltpu.VMEM((units, tile, wide), F32),
@@ -986,9 +1066,79 @@
         compiler_params=params(62),
         name="row_pass",
     )(ctx, hidden, teacher, mask, w_in, w_bt, w_ot, par)
-QKV_ORDERS = ("yxz", "xyz", "yxz")
-FFN_ORDERS = ("cyxz", "cxyz", "cyxz", "cxyz")
-OUT_ORDER = "cxyz"
+BACKWARD_TABLE = (
+    (0, "a0"),
+    (0, "b0"),
+    (2, "a1"),
+    (2, "b1"),
+    (4, "v"),
+    (5, "a0"),
+    (5, "o"),
+    (5, "b0"),
+    (6, "a2"),
+    (6, "b2"),
+    (6, "v"),
+    (7, "a1"),
+    (8, "v"),
+    (8, "b0"),
+    (9, "b1"),
+    (10, "v"),
+    (11, "q0a"),
+    (11, "a0"),
+    (11, "q0b"),
+    (12, "b0"),
+    (13, "a0"),
+    (13, "q0b"),
+    (13, "o"),
+    (13, "b1"),
+    (13, "a2"),
+    (13, "a1"),
+    (14, "q0a"),
+    (14, "q1b"),
+    (15, "q0b"),
+    (16, "o"),
+    (17, "b2"),
+    (AFTER, "q1b"),
+    (AFTER, "q1a"),
+    (AFTER, "q0a"),
+    (AFTER, "b1"),
+    (AFTER, "a2"),
+    (AFTER, "a1"),
+    (AFTER, "o"),
+    (AFTER, "b2"),
+    (AFTER + 1, "s"),
+    (AFTER + 1, "q1b"),
+    (AFTER + 1, "q2b"),
+    (AFTER + 3, "s"),
+    (AFTER + 3, "q1a"),
+    (AFTER + 3, "a2"),
+    (AFTER + 3, "q2a"),
+    (AFTER + 3, "b2"),
+    (AFTER + 3, "q2b"),
+    (AFTER + 3, "s"),
+    (AFTER + 3, "q1a"),
+    (AFTER + 3, "q2b"),
+    (AFTER + 3, "q2a"),
+    (AFTER + 3, "q2a"),
+)
+BACKWARD_WINDOW = 1
+CHUNKS = 3
+
+
+def sum_specs(share, pairs):
+    size = share // CHUNKS
+    specs = []
+    for n in range(CHUNKS):
+        rows = (slice(n * size, (n + 1) * size),)
+        specs.append((f"a{n}", "in", ("cyxz", 0, "yczx", rows)))
+        specs.append((f"b{n}", "back", ("cxyz", 0, "yczx", rows)))
+    specs.append(("o", "out", ("cxyz", 0, "yczx", ())))
+    for p in range(pairs):
+        orders = ("yxz", "xyz") if p % 2 == 0 else ("xyz", "yxz")
+        lanes = (slice(0, 2 * 128), slice(2 * 128, 3 * 128))
+        for name, order, lane in zip("ab", orders, lanes):
+            specs.append((f"q{p}{name}", p, (order, 0, "yzx", (slice(None), lane))))
+    return specs
 
 
 def weight_grad(p, hid_t, dq, dk, dv):
@@ -997,7 +1147,8 @@
 
 def hidden_grad(dq, dk, dv, w, rows):
     pairs = dq.shape[0]
-    return dot(concat_lanes([g[p, rows, :] for g in (dq, dk, dv) for p in range(pairs)]), w[...], NT)
+    grads = concat_lanes([g[p, rows, :] for p in range(pairs) for g in (dq, dk, dv)])
+    return dot(grads, concat_lanes([w[p] for p in range(pairs)]), NT)
 
 
 def attend_sum_kernel(
@@ -1010,7 +1161,7 @@
     ctx_ref,
     lse_ref,
     gctx_ref,
-    hid_ref,
+    hid_t,
     w_ref,
     gmix_ref,
     gin_ref,
@@ -1018,11 +1169,13 @@
     got_ref,
     vec_ref,
     out_ref,
+    gh_recv,
     sin_ref,
-    sbt_ref,
+    sbt,
     sot_ref,
     sq_ref,
     vsum_ref,
+    bsum_ref,
     send,
     recv,
     here,
@@ -1034,90 +1187,62 @@
     dv_acc,
     dk_run,
     dv_run,
-    hid_t,
     gq,
     gh_send,
-    gh_recv,
+    bias,
+    sot,
+    sq,
     v_recv,
     v_held,
+    b_recv,
+    b_held,
     *bufs,
 ):
     place = Place()
     c = place.c
     pairs = q_ref.shape[0]
     local = gmix_ref.shape[0]
+    share = gin_ref.shape[-2]
     greet(place, "zxyc")
     sems = Sems(send, recv)
-    wide = gin_ref.shape[-1]
-    halves = (slice(0, wide // 2), slice(wide // 2, wide))
-    jobs = []
-    rest = list(bufs)
-    for grad, out, order, lanes in (
-        (gin_ref, sin_ref, FFN_ORDERS[0], halves[0]),
-        (gbt_ref, sbt_ref, FFN_ORDERS[1], halves[0]),
-        (gin_ref, sin_ref, FFN_ORDERS[2], halves[1]),
-        (gbt_ref, sbt_ref, FFN_ORDERS[3], halves[1]),
-        (got_ref, sot_ref, OUT_ORDER, None),
-    ):
-        spec = (order, 0, "yczx", lanes)
+    grads = {"in": (gin_ref, sin_ref), "back": (gbt_ref, sbt), "out": (got_ref, sot)}
+    for p in range(pairs):
+        grads[p] = (gq.at[p], sq.at[p])
+    jobs, spot, rest = {}, {}, list(bufs)
+    for name, which, spec in sum_specs(share, pairs):
+        grad, out = grads[which]
         count = len(Scatter.buffers(grad, spec, place.zn))
-        jobs.append(Scatter(place, sems, grad, out, spec, rest[:count]))
+        spot[name] = here.at[len(jobs)]
+        jobs[name] = Scatter(place, sems, grad, out, spec, rest[:count])
         rest = rest[count:]
-    for p in range(pairs):
-        spec = (QKV_ORDERS[p % 3], 0, "yzx", None)
-        count = len(Scatter.buffers(gq.at[p], spec, place.zn))
-        jobs.append(Scatter(place, sems, gq.at[p], sq_ref.at[p], spec, rest[:count]))
-        rest = rest[count:]
-    small = SumAll(place, sems, vec_ref, vsum_ref, v_recv, v_held)
+    jobs["v"] = SumAll(place, sems, vec_ref, vsum_ref, "cyxz", v_recv, v_held)
+    jobs["s"] = SumAll(place, sems, bias, bsum_ref, "yxz", b_recv, b_held)
+    spot["v"] = spot["s"] = None
+    waves = [[f"a{n}", f"b{n}"] for n in range(CHUNKS)]
+    waves[-1] += ["o", "v"]
     swaps = sems.take(2)
     first = sems.copy(swaps, gctx_ref.at[1 - c], do_ref.at[c], place.peer("c"))
     first.start()
     mine = pltpu.make_async_copy(gctx_ref.at[c], do_ref.at[c], here.at[len(jobs)])
     mine.start()
+    for wave in waves[:BACKWARD_WINDOW]:
+        for name in wave:
+            jobs[name].begin(spot[name])
     start_out = pltpu.make_async_copy(gmix_ref, out_ref, here.at[len(jobs) + 1])
     start_out.start()
-    for n in range(5):
-        jobs[n].begin(here.at[n])
-    for i in range(2):
-        hid_t[:, i * local : (i + 1) * local] = hid_ref[i].T
+    bias[...] = jnp.zeros_like(bias)
+
+    def advance(name, stage, begin):
+        jobs[name].wait(stage, spot[name])
+        jobs[name].add(stage)
+        for other in begin:
+            jobs[other].begin(spot[other])
+
+    due = relay(BACKWARD_TABLE, jobs, waves, BACKWARD_WINDOW, advance)
+    for step in sorted(step for step in due.todo if step < 0):
+        due.now(step)
     mine.wait()
     first.wait()
-
-    def advance(n, stage):
-        def fn():
-            jobs[n].wait(stage, here.at[n])
-            jobs[n].add(stage)
-
-        return fn
-
-    due = Due()
-    for step, n, stage in (
-        (0, 0, 0),
-        (1, 1, 0),
-        (2, 2, 0),
-        (3, 3, 0),
-        (4, 4, 0),
-        (6, 0, 1),
-        (6, 1, 1),
-        (9, 0, 2),
-        (9, 1, 2),
-        (10, 2, 1),
-        (10, 3, 1),
-        (11, 4, 1),
-        (12, 0, 3),
-        (12, 1, 3),
-        (12, 5, 0),
-        (14, 2, 2),
-        (14, 3, 2),
-        (14, 5, 1),
-        (15, 4, 2),
-        (15, 6, 0),
-        (16, 5, 2),
-        (17, 2, 3),
-        (17, 3, 3),
-        (17, 6, 1),
-    ):
-        due.add(step, advance(n, stage))
     attend = Backward(
         idx_ref, prev_ref, last_ref, q_ref, k_ref, v_ref, ctx_ref, do_ref, lse_ref, dq, dk, dv,
         dk_acc, dv_acc, dk_run, dv_run,
@@ -1134,31 +1259,31 @@
                     gq[p, y, z, x] = concat_lanes(
                         [s[:, k * 128 + y * HD : k * 128 + (y + 1) * HD] for s in src for k in range(3)]
                     )
-        lanes = pl.ds(pl.multiple_of((c * pairs + p) * 128, 128), 128)
-        for row, g in ((11, dq), (12, dv)):
-            vec_ref[row : row + 1, lanes] = jnp.sum(g[p].astype(F32), axis=0, keepdims=True)
+        lanes = pl.ds(pl.multiple_of(p * 128, 128), 128)
+        for row, g in enumerate((dq, dv)):
+            bias[row : row + 1, lanes] = jnp.sum(g[p].astype(F32), axis=0, keepdims=True)
         for n in range(pairs):
 
             @pl.when(p == n)
             def _(n=n):
-                jobs[5 + n].begin(here.at[5 + n])
+                for name in (f"q{n}a", f"q{n}b"):
+                    jobs[name].begin(spot[name])
 
     attend.run(pairs, due, done)
-    small.begin()
-    size = local // 4
+    jobs["s"].begin()
+    size = local // 2
 
     def other(i, carry):
         t = hidden_grad(dq, dk, dv, w_ref, pl.ds(pl.multiple_of((1 - c) * local + i * size, size), size))
         gh_send[pl.ds(pl.multiple_of(i * size, size), size), :] = t.astype(BF)
         return carry
 
-    lax.fori_loop(0, 4, other, 0)
+    due.now(AFTER)
+    lax.fori_loop(0, 2, other, 0)
     swap = sems.copy(swaps + 1, gh_send, gh_recv, place.peer("c"))
     swap.start()
     start_out.wait()
-    small.wait(0)
-    small.add(0)
-    advance(7, 0)()
+    due.now(AFTER + 1)
 
     def own(i, carry):
         rows = pl.ds(pl.multiple_of(i * size, size), size)
@@ -1166,28 +1291,20 @@
         out_ref[rows, :] += t
         return carry
 
-    lax.fori_loop(0, 4, own, 0)
-    for n, stage in ((4, 3), (6, 2)):
-        advance(n, stage)()
-    small.wait(1)
-    small.add(1)
-    advance(7, 1)()
+    lax.fori_loop(0, 2, own, 0)
+    due.now(AFTER + 2)
+    due.now(AFTER + 3)
     swap.wait()
-
-    def last(i, carry):
-        rows = pl.ds(pl.multiple_of(i * size, size), size)
-        out_ref[rows, :] += gh_recv[rows, :].astype(F32)
-        return carry
-
-    lax.fori_loop(0, 4, last, 0)
-    small.wait(2)
-    small.add(2)
-    advance(7, 2)()
-    small.wait(3)
-    small.add(3)
-
-
-def attend_sum(tables, q, k, v, ctx, lse, gctx, hid, w, gmix, g_in, g_bt, g_ot, vec, zn, cid):
+    t = sot[...]
+    wide = pairs * HD
+    sot_ref[...] = jnp.concatenate([t[:, :wide], t[:, wide:]], axis=0).T
+    for h in range(2):
+        for k in range(3):
+            at = (h * 3 + k) * HD
+            sq_ref[k, h * half : (h + 1) * half, :] = concat_lanes([sq[p, :, at : at + HD] for p in range(pairs)])
+
+
+def attend_sum(tables, q, k, v, ctx, lse, gctx, hid_t, w, gmix, g_in, g_bt, g_ot, vec, zn, cid):
     pairs, n, _ = q.shape
     local = gmix.shape[0]
     share, wide = g_in.shape[-2:]
@@ -1195,31 +1312,32 @@
     packed = g_ot.shape[-2:]
     gq = (pairs, 2, zn, 2) + packed
     heads = pltpu.VMEM((pairs, n, 128), BF)
-    half = slice(0, wide // 2)
+    bias = SDS((8, pairs * 128), F32)
+    shapes = {"in": g_in, "back": g_bt, "out": g_ot}
     bufs = []
-    copies = copies_of("cyxz", zn) + 2
-    big = [(g_in, order, "yczx", half) for order in FFN_ORDERS]
-    for a, order, axes, lanes in big + [(g_ot, OUT_ORDER, "yczx", None)] + [
-        (SDS(gq[1:], BF), QKV_ORDERS[p % 3], "yzx", None) for p in range(pairs)
-    ]:
-        bufs += Scatter.buffers(a, (order, 0, axes, lanes), zn)
-        copies += copies_of(order, zn)
+    copies = copies_of("cyxz", zn) + copies_of("yxz", zn) + 2
+    specs = sum_specs(share, pairs)
+    for _, which, spec in specs:
+        bufs += Scatter.buffers(shapes.get(which, SDS(gq[1:], BF)), spec, zn)
+        copies += copies_of(spec[0], zn)
     return pl.pallas_call(
         attend_sum_kernel,
         out_shape=(
             SDS((local, D), F32),
+            SDS((local, D), BF),
             SDS((share, wide), F32),
             SDS((share, wide), F32),
-            SDS(packed, F32),
-            SDS((pairs,) + packed, F32),
+            SDS((pairs * HD, share), F32),
+            SDS((3, share, pairs * HD), F32),
             SDS(vec.shape, F32),
+            bias,
         ),
         in_specs=[SM] * 3 + [VM] * 5 + [ANY, VM, VM, ANY, ANY, ANY, ANY, VM],
-        out_specs=(VM,) * 6,
+        out_specs=(VM,) * 8,
         scratch_shapes=[
             pltpu.SemaphoreType.DMA((copies,)),
             pltpu.SemaphoreType.DMA((copies,)),
-            pltpu.SemaphoreType.DMA((7 + pairs,)),
+            pltpu.SemaphoreType.DMA((len(specs) + 4,)),
             pltpu.VMEM(gctx.shape, BF),
             heads,
             heads,
@@ -1228,16 +1346,104 @@
             pltpu.VMEM((n, 128), F32),
             pltpu.VMEM((3 * (blocks - 2) + 1, BLK, 128), F32),
             pltpu.VMEM((3 * (blocks - 2) + 1, BLK, 128), F32),
-            pltpu.VMEM((D, n), BF),
             pltpu.VMEM(gq, BF),
             pltpu.VMEM((local, D), BF),
-            pltpu.VMEM((local, D), BF),
+            pltpu.VMEM(bias.shape, F32),
+            pltpu.VMEM(packed, F32),
+            pltpu.VMEM((pairs,) + packed, F32),
         ]
-        + SumAll.buffers(vec, zn)
+        + SumAll.buffers(vec, "cyxz", zn)
+        + SumAll.buffers(bias, "yxz", zn)
         + bufs,
-        compiler_params=params(62, cid),
+        compiler_params=params(63, cid),
         name="attend_sum",
-    )(*tables, q, k, v, ctx, lse, gctx, hid, w, gmix, g_in, g_bt, g_ot, vec)
+    )(*tables, q, k, v, ctx, lse, gctx, hid_t, w, gmix, g_in, g_bt, g_ot, vec)
+
+
+def take_kernel(
+    par_ref,
+    vec_ref,
+    bias_ref,
+    part_ref,
+    recv_ref,
+    sin_ref,
+    sbt_ref,
+    sot_ref,
+    sq_ref,
+    loss_ref,
+    out_ref,
+    oq_ref,
+    ob_ref,
+    oo_ref,
+    oi_ref,
+    obin_ref,
+    obt_ref,
+    og_ref,
+    orow_ref,
+):
+    place = Place()
+    dp = place.z * 2 + place.x
+    t = place.y * 2 + place.c
+    out_ref[...] = part_ref[...] + recv_ref[...].astype(F32)
+    oq_ref[...] = sq_ref[...]
+    oo_ref[...] = sot_ref[...]
+    oi_ref[...] = sin_ref[...]
+    obt_ref[...] = sbt_ref[...]
+    loss_ref[...] = jnp.sum(vec_ref[10:11, :], axis=1, keepdims=True) / (float(D) * par_ref[10:11, 0:1])
+
+    def exact(a, b):
+        return lax.dot_general(a, b, NN, precision=lax.Precision.HIGHEST, preferred_element_type=F32)
+
+    cols = og_ref.shape[1]
+    part = dp * 4 + t
+    l = lax.broadcasted_iota(jnp.int32, (D, cols), 0)
+    i = lax.broadcasted_iota(jnp.int32, (D, cols), 1)
+    both = exact(vec_ref[0:8, :], (l == part * cols + i).astype(F32))
+    og_ref[...] = both[:2]
+    orow_ref[...] = both[2:6]
+    n = obin_ref.shape[0]
+    units = obin_ref.shape[1]
+    row = jnp.zeros((1, D), F32)
+    for u in range(4):
+        row = row + jnp.where(t == u, 1.0, 0.0) * vec_ref[6 + u : 7 + u, :]
+    l = lax.broadcasted_iota(jnp.int32, (n, D), 1)
+    i = lax.broadcasted_iota(jnp.int32, (n, D), 0)
+    own = jnp.where(l % HD == dp * n + i, row, 0.0)
+    l = lax.broadcasted_iota(jnp.int32, (D, units), 0)
+    u = lax.broadcasted_iota(jnp.int32, (D, units), 1)
+    obin_ref[...] = exact(own, (l // HD == u).astype(F32))
+    e = bias_ref.shape[1]
+    l = lax.broadcasted_iota(jnp.int32, (e, n), 0)
+    i = lax.broadcasted_iota(jnp.int32, (e, n), 1)
+    for p in range(ob_ref.shape[0]):
+        ob_ref[p] = exact(bias_ref[...], (l == p * 128 + place.y * HD + dp * n + i).astype(F32))[:2]
+
+
+def take(par, vec, bias, part, recv, s_in, s_bt, s_ot, s_q, b_in_shape, b_qv_shape):
+    dp, tensor = lax.axis_size("dp"), lax.axis_size("tensor")
+    cols = D // (dp * tensor)
+    outs = (
+        SDS((1, 1), F32),
+        SDS(part.shape, F32),
+        SDS(s_q.shape, F32),
+        SDS((b_qv_shape[1], b_qv_shape[0], b_qv_shape[2]), F32),
+        SDS(s_ot.shape, F32),
+        SDS(s_in.shape, F32),
+        SDS((b_in_shape[1], b_in_shape[0]), F32),
+        SDS(s_bt.shape, F32),
+        SDS((2, cols), F32),
+        SDS((4, cols), F32),
+    )
+    return pl.pallas_call(
+        take_kernel,
+        out_shape=outs,
+        in_specs=[VM] * 9,
+        out_specs=(VM,) * len(outs),
+        compiler_params=params(62),
+        name="take_parts",
+    )(par, vec, bias, part, recv, s_in, s_bt, s_ot, s_q)
+
+
 def small_parts(b_qv, b_in, ln_gains, row_biases, count):
     dp, dpi = lax.axis_size("dp"), lax.axis_index("dp")
     t = lax.axis_index("tensor")
@@ -1257,7 +1463,7 @@
     return jnp.pad(out, ((0, SMALL_ROWS - out.shape[0]), (0, 0)))
 
 
-def finish(vector, par, encoded, grad_in, s_qkv, s_out, s_in, s_back, b_in, pairs, hd):
+def finish(vector, bias, par, encoded, grad_in, s_qkv, s_out, s_in, s_back, b_in, pairs, hd):
     dp, tensor = lax.axis_size("dp"), lax.axis_size("tensor")
     dpi, ti = lax.axis_index("dp"), lax.axis_index("tensor")
     part = dpi * tensor + ti
@@ -1265,8 +1471,7 @@
     gains_biases = lax.dynamic_slice_in_dim(vector[:6], part * cols, cols, 1)
     grad_b_in = lax.dynamic_index_in_dim(vector[6:10].reshape(tensor, b_in.shape[0], dp, hd), ti, 0, False)
     grad_b_in = lax.dynamic_index_in_dim(grad_b_in, dpi, 1, False)
-    grad_qv = lax.dynamic_index_in_dim(vector[11:13].reshape(2, 2, pairs, 2, dp, hd), ti % 2, 1, False)
-    grad_qv = lax.dynamic_index_in_dim(grad_qv, ti // 2, 2, False)
+    grad_qv = lax.dynamic_index_in_dim(bias.reshape(2, pairs, 2, dp, hd), ti // 2, 2, False)
     grad_qv = lax.dynamic_index_in_dim(grad_qv, dpi, 2, False)
     loss = jnp.sum(vector[10]) / (D * par[10, 0])
     return (
@@ -1291,40 +1496,40 @@
     dp, tensor = lax.axis_size("dp"), lax.axis_size("tensor")
     zn = dp // 2
     tokens_total = local * tensor * dp
-    c = lax.axis_index("tensor") % 2
-    share = ln_gains.shape[1]
     pairs = b_qv.shape[1]
-    hd = b_qv.shape[2]
-    mask = valid_mask.astype(F32)
-    small = small_parts(b_qv, b_in, ln_gains, row_biases, jnp.sum(mask))
-    tables = block_tables(random_blocks, c)
-    half = share // 2
-    wq = jnp.concatenate([w_qkv[k, h * half : (h + 1) * half] for h in range(2) for k in range(3)], axis=1)
-    q, k, v, ctx, lse, ctx_rows, hid, w, full_in, full_bt, full_ot, par = gather_attend(
-        tables[0], wq, hidden_in, small, w_in, w_back, w_out, pairs, zn, 0
+    mask = valid_mask.reshape(-1, 128)
+    tables = block_tables(random_blocks, lax.axis_index("tensor") % 2)
+    q, k, v, ctx, lse, ctx_rows, hid_t, w, full_in, full_bt, full_ot, par = gather_attend(
+        tables[0], w_qkv, hidden_in, (b_qv.transpose(1, 0, 2), b_in.T, ln_gains, row_biases, mask), w_in, w_back.T,
+        w_out, pairs, zn, 0,
     )
     units = (tensor, D, w_in.shape[1])
     encoded, gmix, gctx, g_in, g_bt, g_ot, vec = row_pass(
-        tokens_total, ctx_rows, hidden_in, teacher, mask[:, None], full_in.reshape(units), full_bt.reshape(units),
-        full_ot, par, 256,
+        tokens_total, ctx_rows, hidden_in, teacher, mask, full_in.reshape(units), full_bt.reshape(units), full_ot,
+        par, 256,
     )
-    grad_in, s_in, s_bt, s_ot, s_q, vector = attend_sum(
-        tables, q, k, v, ctx, lse, gctx, hid, w, gmix, g_in.reshape(full_in.shape), g_bt.reshape(full_in.shape),
+    part, there, s_in, s_bt, s_ot, s_qkv, vector, bias = attend_sum(
+        tables, q, k, v, ctx, lse, gctx, hid_t, w, gmix, g_in.reshape(full_in.shape), g_bt.reshape(full_in.shape),
         g_ot, vec, zn, 1,
     )
-    s_qkv = s_q.reshape(pairs, half, 2, 3, HD).transpose(3, 2, 1, 0, 4).reshape(w_qkv.shape)
-    s_ot = s_ot.reshape(half, 2, -1).transpose(2, 1, 0).reshape(w_out.shape)
-    return finish(vector, par, encoded, grad_in, s_qkv, s_ot, s_in, s_bt.T, b_in, pairs, hd)
+    loss, grad_in, g_qkv, g_bias, g_out, g_w_in, g_b_in, g_back, g_gains, g_rows = take(
+        par, vector, bias, part, there, s_in, s_bt, s_ot, s_qkv, b_in.shape, b_qv.shape
+    )
+    return (
+        loss.reshape(()), encoded, grad_in, g_qkv, g_bias.transpose(1, 0, 2), g_out, g_w_in, g_b_in.T, g_back.T,
+        g_gains, g_rows,
+    )
 
 
 def project_attend_kernel(idx_ref, hid_ref, w_ref, b_ref, q_ref, k_ref, v_ref, ctx_ref, lse_ref, lse_t):
     chunk = hid_ref.shape[1] // 2
-
-    def project(i, carry):
-        project_rows(i, chunk, hid_ref, w_ref, b_ref[...], q_ref, k_ref, v_ref)
-        return carry
-
-    lax.fori_loop(0, 4, project, 0)
+    for p in range(q_ref.shape[0]):
+
+        def project(i, carry, p=p):
+            project_rows(p, i, chunk, hid_ref, w_ref, b_ref[:, p * 128 : (p + 1) * 128], q_ref, k_ref, v_ref)
+            return carry
+
+        lax.fori_loop(0, 4, project, 0)
     Forward(idx_ref, q_ref, k_ref, v_ref, ctx_ref, lse_ref, lse_t).run(q_ref.shape[0])
 
 
@@ -1411,7 +1616,7 @@
 
     hid = swap(jnp.stack([hidden_in, hidden_in]))
     w = lax.all_gather(lax.all_gather(w_qkv, "dp", axis=1, tiled=True), "tensor", axis=0)
-    w = w.reshape(2, 2, 3, D, pairs, HD)[:, c].transpose(2, 1, 3, 0, 4).reshape(D, -1)
+    w = w.reshape(2, 2, 3, D, pairs, HD)[:, c].transpose(3, 2, 1, 0, 4).reshape(pairs, D, -1)
     w_o = lax.all_gather(lax.all_gather(w_out, "dp", axis=1, tiled=True), "tensor", axis=0)
     w_o = w_o.reshape(2, 2, pairs, HD, D).transpose(4, 1, 2, 0, 3).reshape(D, D)
     full_in = lax.all_gather(lax.all_gather(w_in, "dp", axis=0, tiled=True), "tensor", axis=0)
@@ -1420,7 +1625,7 @@
     q, k, v, ctx, lse = project_attend(tables[0], hid, w, bias, pairs)
     ctx_rows = swap(ctx.reshape(pairs, 2, local, 128).swapaxes(0, 1))
     encoded, gmix, gctx, g_in, g_bt, g_ot, vec = row_pass(
-        tokens_total, ctx_rows, hidden_in, teacher, mask[:, None], full_in, full_bt, w_o, par, 256
+        tokens_total, ctx_rows, hidden_in, teacher, valid_mask.reshape(-1, 128), full_in, full_bt, w_o, par, 256
     )
     gw, gh, gb = attend_back(tables, q, k, v, ctx, lse, swap(gctx), hid, w)
     there = lax.ppermute(gh.reshape(2, local, D)[1 - c].astype(BF), "tensor", [(i, i ^ 1) for i in range(tensor)])
@@ -1435,9 +1640,11 @@
     own = (jnp.arange(2) == c).astype(F32)
     gw = gw.reshape(pairs, D, 3, 2, HD).transpose(3, 1, 2, 0, 4).reshape(2, 1, D, -1) * own[None, :, None, None]
     s_qkv = spread(gw.reshape(tensor, D, -1)).reshape(-1, 3, pairs * HD).swapaxes(0, 1)
-    gb = gb.swapaxes(0, 1).reshape(2, 1, -1) * own[None, :, None]
-    vector = lax.psum(vec.at[11:13].set(gb.reshape(2, D)), everyone)
-    return finish(vector, par, encoded, grad_in, s_qkv, s_ot.T, s_in, s_bt.T, b_in, pairs, hd)
+    bias = gb.swapaxes(0, 1).reshape(2, -1)
+    bias = lax.psum(bias[:, None, :] * own[None, :, None], everyone)
+    bias = lax.dynamic_index_in_dim(bias, c, 1, False)
+    vector = lax.psum(vec, everyone)
+    return finish(vector, bias, par, encoded, grad_in, s_qkv, s_ot.T, s_in, s_bt.T, b_in, pairs, hd)
 
 
 def solution(mesh):

time: 326 us -> 280 us (0.86)
  local copies, waits for them, and re-layouts: 23.3 us -> 1.43 us
  Pallas kernels: 292 us -> 275 us
  other arithmetic: 6.43 us -> 2.3 us
    pallas_call x2 -> x3, Pallas kernels: 236 us -> 219 us  [the longest x1 109 us: attend_sum(): pl.pallas_call(attend_sum_kernel, out_shape=(SDS((local, D), F32), SDS((l...]
    unnamed x18 -> x2, local copies, waits for them, and re-layouts: 6.17 us -> 0.01 us
    reshape x6 -> x0, local copies, waits for them, and re-layouts: 5.54 us -> none  [the longest x2 4.3 us: per_device(): s_q.reshape(pairs, half, 2, 3, HD).transpose(3, 2, 1, 0, 4)]
where the time goes in v3:
time: 280 us; the launch traced here: 279 us
  Pallas kernels  275 us (98%)
    pallas_call x1, Pallas kernels, attend_sum(): pl.pallas_call(attend_sum_kernel, out_shape=(SDS((local, D), F32), SDS((l...  109 us
    pallas_call x1, Pallas kernels, gather_attend(): pl.pallas_call(gather_attend_kernel, out_shape=(heads_shape, blocks_shape...  104 us
    pallas_call x1, Pallas kernels, row_pass(): pl.pallas_call(functools.partial(rows_kernel, float(tokens_total), len(w_...  55.9 us
    pallas_call x1, Pallas kernels, take(): pl.pallas_call(take_kernel, out_shape=outs, in_specs=[VM] * 9, out_specs=...  5.62 us

profile of v3, /device:TPU:0, one launch (start us, length us, event | category | flops | bytes accessed | tf_op | source)
XLA Modules:
  0.0 279.4 jit_solution(5697353400682156832)
XLA Ops:
  0.7 1.4 select_reduce_fusion
  2.1 0.1 copy.24
  2.2 0.7 reduce_sum.12.idx_ref
  2.9 104.3 %gather_attend.1 = (bf16[3,2048,128]{2,1,0:T(8,128)(2,1)}, bf16[3,32,64,128]{3,2,1,0:T(8,128)(2,1)}, bf16[3,32,64,128]{3,2,1,0:T(8,128)(2,1)}, bf16[3,2048,128]{...) custom-call(s32[6,96]{1,0:T(8,128)} %reduce_sum.12.idx_ref, ...), custom_call_target="tpu_custom_call" | custom-call | tf_op jit(solution)/shard_map/gather_attend/pallas_call | solution.py:833
  107.2 0.0 copy-start
  107.2 55.9 %row_pass.1 = (f32[1024,768]{1,0:T(8,128)}, f32[1024,768]{1,0:T(8,128)}, bf16[2,3,1024,128]{3,2,1,0:T(8,128)(2,1)}, bf16[4,768,768]{2,1,0:T(8,128)(2,1)}, bf16[4...) custom-call(bf16[2,3,1024,128]{3,2,1,0:T(8,128)(2,1)} %get-tuple-element.54.ctx_ref, ...), custom_call_target="tpu_custom_call" | custom-call | tf_op jit(solution)/shard_map/row_pass/pallas_call | solution.py:1051
  163.2 0.0 copy-done
  163.2 0.9 select_reduce_fusion.1.prev_ref
  164.1 0.6 reduce_max.22.last_ref
  164.6 109.0 %attend_sum.1 = (f32[1024,768]{1,0:T(8,128)}, bf16[1024,768]{1,0:T(8,128)(2,1)}, f32[96,768]{1,0:T(8,128)}, f32[96,768]{1,0:T(8,128)}, f32[192,96]{1,0:T(8,128)}...) custom-call(s32[6,96]{1,0:T(8,128)} %reduce_sum.12.idx_ref, s32[6,96]{1,0:T(8,128)} %select_reduce_fusion.1.prev_ref, ...), custom_call_target="tpu_custom_call" | custom-call | tf_op jit(solution)/shard_map/attend_sum/pallas_call | solution.py:1323
  273.6 5.6 %take_parts.1 = (f32[1,1]{1,0:T(1,128)}, f32[1024,768]{1,0:T(8,128)}, f32[3,96,192]{2,1,0:T(8,128)}, f32[3,2,8]{2,1,0:T(2,128)}, f32[192,96]{1,0:T(8,128)}, /*in...) custom-call(f32[16,768]{1,0:T(8,128)} %get-tuple-element.48.par.par_ref, ...), custom_call_target="tpu_custom_call" | custom-call | tf_op jit(solution)/shard_map/take_parts/pallas_call | solution.py:1437
  (3 shorter events, 0.0 us)
Async XLA Ops:
  107.2 55.9 %copy-start = (s32[6,96]{1,0:T(8,128)S(1)}, s32[6,96]{1,0:T(8,128)}, u32[]{:S(2)}) copy-start(s32[6,96]{1,0:T(8,128)} %reduce_sum.12.idx_ref) | copy-start | bytes 6916

commit v4 on v3

--- a/solution.py
+++ b/solution.py
@@ -696,14 +696,14 @@
     win_ref,
     wbt,
     wo_ref,
-    q_ref,
-    k_ref,
-    v_ref,
-    ctx_ref,
+    q_out,
+    k_out,
+    v_out,
+    ctx_out,
     lse_ref,
     rows_ref,
-    hidt_ref,
-    w_ref,
+    hidt_out,
+    w_out,
     fin_ref,
     fbt_ref,
     fot_ref,
@@ -711,6 +711,12 @@
     send,
     recv,
     here,
+    q_ref,
+    k_ref,
+    v_ref,
+    ctx_ref,
+    hidt_ref,
+    w_ref,
     hid_ref,
     wq,
     parts,
@@ -769,10 +775,13 @@
     ]
     for copy in late:
         copy.start()
-    for copy in own + late:
+    for copy in own:
         copy.wait()
+    in_flight = dict(zip("abo", late))
 
     def pass_on(name, stage, begin):
+        if name[0] in in_flight:
+            in_flight.pop(name[0]).wait()
         jobs[name].wait(stage)
         if stage + 1 < len(jobs[name].order):
             jobs[name].start(stage + 1)
@@ -808,6 +817,14 @@
         return carry
 
     lax.fori_loop(0, 4, project, 0)
+    stores = [
+        pltpu.make_async_copy(src, dst, here.at[pairs + 4 + n])
+        for n, (src, dst) in enumerate(
+            ((q_ref, q_out), (k_ref, k_out), (v_ref, v_out), (hidt_ref, hidt_out), (w_ref, w_out), (ctx_ref, ctx_out))
+        )
+    ]
+    for copy in stores[:5]:
+        copy.start()
     attend.run(pairs, lambda g: due(g, 4))
     for p in range(pairs):
         there(p).start()
@@ -815,7 +832,10 @@
         ctx_ref.at[:, pl.ds(pl.multiple_of(c * local, local), local), :], rows_ref.at[c], here.at[0]
     )
     mine.start()
+    stores[5].start()
     due.now(AFTER)
+    for copy in stores:
+        copy.wait()
     mine.wait()
     for p in range(pairs):
         there(p).wait()
@@ -847,11 +867,17 @@
             SDS(small.shape, F32),
         ),
         in_specs=[SM, VM, ANY] + [VM] * len(smalls) + [ANY, ANY, VM],
-        out_specs=(VM,) * 5 + (ANY, VM, VM, ANY, ANY, ANY, VM),
+        out_specs=(ANY,) * 4 + (VM,) + (ANY,) * 6 + (VM,),
         scratch_shapes=[
             pltpu.SemaphoreType.DMA((copies,)),
             pltpu.SemaphoreType.DMA((copies,)),
-            pltpu.SemaphoreType.DMA((pairs + 4,)),
+            pltpu.SemaphoreType.DMA((pairs + 10,)),
+            pltpu.VMEM(heads_shape.shape, BF),
+            pltpu.VMEM(blocks_shape.shape, BF),
+            pltpu.VMEM(blocks_shape.shape, BF),
+            pltpu.VMEM(heads_shape.shape, BF),
+            pltpu.VMEM((D, n), BF),
+            pltpu.VMEM((pairs, D, 3 * 128), BF),
             pltpu.VMEM((2, local, D), BF),
             pltpu.VMEM((pairs,) + packed, BF),
             pltpu.VMEM((pairs, 2, zn, 2) + packed, BF),
@@ -1155,14 +1181,14 @@
     idx_ref,
     prev_ref,
     last_ref,
-    q_ref,
-    k_ref,
-    v_ref,
-    ctx_ref,
+    q_in,
+    k_in,
+    v_in,
+    ctx_in,
     lse_ref,
     gctx_ref,
-    hid_t,
-    w_ref,
+    hid_in,
+    w_in,
     gmix_ref,
     gin_ref,
     gbt_ref,
@@ -1179,6 +1205,12 @@
     send,
     recv,
     here,
+    q_ref,
+    k_ref,
+    v_ref,
+    ctx_ref,
+    hid_t,
+    w_ref,
     do_ref,
     dq,
     dk,
@@ -1228,6 +1260,14 @@
     for wave in waves[:BACKWARD_WINDOW]:
         for name in wave:
             jobs[name].begin(spot[name])
+    loads = [
+        pltpu.make_async_copy(src, dst, here.at[len(jobs) + 2 + n])
+        for n, (src, dst) in enumerate(
+            ((q_in, q_ref), (k_in, k_ref), (v_in, v_ref), (ctx_in, ctx_ref), (hid_in, hid_t), (w_in, w_ref))
+        )
+    ]
+    for copy in loads:
+        copy.start()
     start_out = pltpu.make_async_copy(gmix_ref, out_ref, here.at[len(jobs) + 1])
     start_out.start()
     bias[...] = jnp.zeros_like(bias)
@@ -1243,6 +1283,8 @@
         due.now(step)
     mine.wait()
     first.wait()
+    for copy in loads:
+        copy.wait()
     attend = Backward(
         idx_ref, prev_ref, last_ref, q_ref, k_ref, v_ref, ctx_ref, do_ref, lse_ref, dq, dk, dv,
         dk_acc, dv_acc, dk_run, dv_run,
@@ -1332,12 +1374,18 @@
             SDS(vec.shape, F32),
             bias,
         ),
-        in_specs=[SM] * 3 + [VM] * 5 + [ANY, VM, VM, ANY, ANY, ANY, ANY, VM],
+        in_specs=[SM] * 3 + [ANY] * 4 + [VM] + [ANY] * 7 + [VM],
         out_specs=(VM,) * 8,
         scratch_shapes=[
             pltpu.SemaphoreType.DMA((copies,)),
             pltpu.SemaphoreType.DMA((copies,)),
-            pltpu.SemaphoreType.DMA((len(specs) + 4,)),
+            pltpu.SemaphoreType.DMA((len(specs) + 10,)),
+            pltpu.VMEM(q.shape, BF),
+            pltpu.VMEM(k.shape, BF),
+            pltpu.VMEM(v.shape, BF),
+            pltpu.VMEM(ctx.shape, BF),
+            pltpu.VMEM(hid_t.shape, BF),
+            pltpu.VMEM(w.shape, BF),
             pltpu.VMEM(gctx.shape, BF),
             heads,
             heads,
@@ -1355,7 +1403,7 @@
         + SumAll.buffers(vec, "cyxz", zn)
         + SumAll.buffers(bias, "yxz", zn)
         + bufs,
-        compiler_params=params(63, cid),
+        compiler_params=params(62, cid),
         name="attend_sum",
     )(*tables, q, k, v, ctx, lse, gctx, hid_t, w, gmix, g_in, g_bt, g_ot, vec)
 

time: 280 us -> 269 us (0.961)
  Pallas kernels: 275 us -> 264 us
    pallas_call x1, Pallas kernels: 104 us -> 95 us  [gather_attend(): pl.pallas_call(gather_attend_kernel, out_shape=(heads_shape, blocks_shape...]
where the time goes in v4:
time: 269 us; the launch traced here: 268 us
  Pallas kernels  264 us (98%)
    pallas_call x1, Pallas kernels, attend_sum(): pl.pallas_call(attend_sum_kernel, out_shape=(SDS((local, D), F32), SDS((l...  107 us
    pallas_call x1, Pallas kernels, gather_attend(): pl.pallas_call(gather_attend_kernel, out_shape=(heads_shape, blocks_shape...  95 us
    pallas_call x1, Pallas kernels, row_pass(): pl.pallas_call(functools.partial(rows_kernel, float(tokens_total), len(w_...  55.9 us
    pallas_call x1, Pallas kernels, take(): pl.pallas_call(take_kernel, out_shape=outs, in_specs=[VM] * 9, out_specs=...  5.62 us

profile of v4, /device:TPU:0, one launch (start us, length us, event | category | flops | bytes accessed | tf_op | source)
XLA Modules:
  0.0 268.5 jit_solution(1796447810815703987)
XLA Ops:
  0.7 1.4 select_reduce_fusion
  2.1 0.1 copy.24
  2.2 0.7 reduce_sum.12.idx_ref
  2.9 95.0 %gather_attend.1 = (bf16[3,2048,128]{2,1,0:T(8,128)(2,1)}, bf16[3,32,64,128]{3,2,1,0:T(8,128)(2,1)}, bf16[3,32,64,128]{3,2,1,0:T(8,128)(2,1)}, bf16[3,2048,128]{...) custom-call(s32[6,96]{1,0:T(8,128)} %reduce_sum.12.idx_ref, ...), custom_call_target="tpu_custom_call" | custom-call | tf_op jit(solution)/shard_map/gather_attend/pallas_call | solution.py:853
  97.9 0.0 copy-start
  97.9 55.9 %row_pass.1 = (f32[1024,768]{1,0:T(8,128)}, f32[1024,768]{1,0:T(8,128)}, bf16[2,3,1024,128]{3,2,1,0:T(8,128)(2,1)}, bf16[4,768,768]{2,1,0:T(8,128)(2,1)}, bf16[4...) custom-call(bf16[2,3,1024,128]{3,2,1,0:T(8,128)(2,1)} %get-tuple-element.54.ctx_ref, ...), custom_call_target="tpu_custom_call" | custom-call | tf_op jit(solution)/shard_map/row_pass/pallas_call | solution.py:1077
  153.8 0.0 copy-done
  153.8 0.9 select_reduce_fusion.1.prev_ref
  154.7 0.6 reduce_max.22.last_ref
  155.3 107.4 %attend_sum.1 = (f32[1024,768]{1,0:T(8,128)}, bf16[1024,768]{1,0:T(8,128)(2,1)}, f32[96,768]{1,0:T(8,128)}, f32[96,768]{1,0:T(8,128)}, f32[192,96]{1,0:T(8,128)}...) custom-call(s32[6,96]{1,0:T(8,128)} %reduce_sum.12.idx_ref, s32[6,96]{1,0:T(8,128)} %select_reduce_fusion.1.prev_ref, ...), custom_call_target="tpu_custom_call" | custom-call | tf_op jit(solution)/shard_map/attend_sum/pallas_call | solution.py:1365
  262.7 5.6 %take_parts.1 = (f32[1,1]{1,0:T(1,128)}, f32[1024,768]{1,0:T(8,128)}, f32[3,96,192]{2,1,0:T(8,128)}, f32[3,2,8]{2,1,0:T(2,128)}, f32[192,96]{1,0:T(8,128)}, /*in...) custom-call(f32[16,768]{1,0:T(8,128)} %get-tuple-element.48.par.par_ref, ...), custom_call_target="tpu_custom_call" | custom-call | tf_op jit(solution)/shard_map/take_parts/pallas_call | solution.py:1485
  (3 shorter events, 0.0 us)
Async XLA Ops:
  97.9 55.9 %copy-start = (s32[6,96]{1,0:T(8,128)S(1)}, s32[6,96]{1,0:T(8,128)}, u32[]{:S(2)}) copy-start(s32[6,96]{1,0:T(8,128)} %reduce_sum.12.idx_ref) | copy-start | bytes 6916

commit v5 on v4

--- a/solution.py
+++ b/solution.py
@@ -583,17 +583,17 @@
     (-994, "q0a"),
     (-993, "q1a"),
     (-992, "q2b"),
-    (-991, "q0b"),
-    (-990, "q1b"),
-    (-989, "q2a"),
+    (-991, "q2a"),
+    (-990, "q0b"),
+    (-989, "q1b"),
     (-988, "a0"),
     (-987, "b0"),
     (-986, "q2b"),
     (-985, "q1a"),
     (-984, "q0a"),
     (-983, "q2a"),
-    (-982, "q2b"),
-    (-981, "b0"),
+    (-982, "b0"),
+    (-981, "q2b"),
     (-980, "a0"),
     (-979, "a1"),
     (-978, "b1"),
@@ -604,20 +604,20 @@
     (5, "a1"),
     (6, "b0"),
     (6, "a2"),
+    (7, "b1"),
     (7, "o"),
-    (7, "b1"),
     (9, "b0"),
-    (9, "b2"),
+    (10, "b2"),
     (11, "a0"),
     (14, "a0"),
-    (16, "a1"),
+    (17, "a1"),
     (17, "a2"),
     (17, "o"),
-    (18, "a1"),
     (19, "b1"),
     (20, "b2"),
-    (20, "o"),
-    (20, "a2"),
+    (21, "o"),
+    (AFTER, "a1"),
+    (AFTER, "a2"),
     (AFTER, "b1"),
     (AFTER, "b2"),
 )
@@ -1093,58 +1093,58 @@
         name="row_pass",
     )(ctx, hidden, teacher, mask, w_in, w_bt, w_ot, par)
 BACKWARD_TABLE = (
-    (0, "a0"),
-    (0, "b0"),
-    (2, "a1"),
-    (2, "b1"),
-    (4, "v"),
-    (5, "a0"),
-    (5, "o"),
-    (5, "b0"),
-    (6, "a2"),
-    (6, "b2"),
+    (1, "a0"),
+    (1, "b0"),
+    (5, "a1"),
+    (5, "b1"),
+    (6, "a0"),
+    (6, "b0"),
     (6, "v"),
-    (7, "a1"),
+    (7, "o"),
+    (7, "a2"),
+    (7, "b2"),
     (8, "v"),
-    (8, "b0"),
-    (9, "b1"),
-    (10, "v"),
-    (11, "q0a"),
-    (11, "a0"),
-    (11, "q0b"),
+    (10, "q0b"),
+    (11, "a1"),
+    (11, "v"),
+    (11, "b1"),
+    (12, "q0a"),
+    (12, "a0"),
     (12, "b0"),
-    (13, "a0"),
-    (13, "q0b"),
-    (13, "o"),
-    (13, "b1"),
-    (13, "a2"),
-    (13, "a1"),
-    (14, "q0a"),
-    (14, "q1b"),
+    (12, "v"),
+    (12, "q0b"),
     (15, "q0b"),
-    (16, "o"),
-    (17, "b2"),
+    (15, "b1"),
+    (16, "q1b"),
+    (16, "a2"),
+    (17, "o"),
+    (17, "a0"),
+    (17, "b0"),
+    (AFTER, "q0a"),
+    (AFTER, "a1"),
+    (AFTER, "b1"),
+    (AFTER, "b2"),
     (AFTER, "q1b"),
     (AFTER, "q1a"),
-    (AFTER, "q0a"),
-    (AFTER, "b1"),
-    (AFTER, "a2"),
-    (AFTER, "a1"),
     (AFTER, "o"),
-    (AFTER, "b2"),
+    (AFTER + 1, "a2"),
     (AFTER + 1, "s"),
-    (AFTER + 1, "q1b"),
-    (AFTER + 1, "q2b"),
+    (AFTER + 3, "q2b"),
+    (AFTER + 3, "q0a"),
+    (AFTER + 3, "q1b"),
     (AFTER + 3, "s"),
+    (AFTER + 3, "a1"),
     (AFTER + 3, "q1a"),
+    (AFTER + 3, "o"),
     (AFTER + 3, "a2"),
+    (AFTER + 3, "s"),
     (AFTER + 3, "q2a"),
+    (AFTER + 3, "q2b"),
     (AFTER + 3, "b2"),
-    (AFTER + 3, "q2b"),
-    (AFTER + 3, "s"),
     (AFTER + 3, "q1a"),
     (AFTER + 3, "q2b"),
     (AFTER + 3, "q2a"),
+    (AFTER + 3, "b2"),
     (AFTER + 3, "q2a"),
 )
 BACKWARD_WINDOW = 1

time: 269 us -> 274 us (1.019)
  Pallas kernels: 264 us -> 269 us
    pallas_call x1, Pallas kernels: 107 us -> 112 us  [attend_sum(): pl.pallas_call(attend_sum_kernel, out_shape=(SDS((local, D), F32), SDS((l...]
where the time goes in v5:
time: 274 us; the launch traced here: 273 us
  Pallas kernels  269 us (98%)
    pallas_call x1, Pallas kernels, attend_sum(): pl.pallas_call(attend_sum_kernel, out_shape=(SDS((local, D), F32), SDS((l...  112 us
    pallas_call x1, Pallas kernels, gather_attend(): pl.pallas_call(gather_attend_kernel, out_shape=(heads_shape, blocks_shape...  95 us
    pallas_call x1, Pallas kernels, row_pass(): pl.pallas_call(functools.partial(rows_kernel, float(tokens_total), len(w_...  55.9 us
    pallas_call x1, Pallas kernels, take(): pl.pallas_call(take_kernel, out_shape=outs, in_specs=[VM] * 9, out_specs=...  5.62 us

profile of v5, /device:TPU:0, one launch (start us, length us, event | category | flops | bytes accessed | tf_op | source)
XLA Modules:
  0.0 273.4 jit_solution(8197653684799436057)
XLA Ops:
  0.7 1.4 select_reduce_fusion
  2.1 0.1 copy.24
  2.2 0.7 reduce_sum.12.idx_ref
  2.9 95.0 %gather_attend.1 = (bf16[3,2048,128]{2,1,0:T(8,128)(2,1)}, bf16[3,32,64,128]{3,2,1,0:T(8,128)(2,1)}, bf16[3,32,64,128]{3,2,1,0:T(8,128)(2,1)}, bf16[3,2048,128]{...) custom-call(s32[6,96]{1,0:T(8,128)} %reduce_sum.12.idx_ref, ...), custom_call_target="tpu_custom_call" | custom-call | tf_op jit(solution)/shard_map/gather_attend/pallas_call | solution.py:853
  97.9 0.0 copy-start
  97.9 55.9 %row_pass.1 = (f32[1024,768]{1,0:T(8,128)}, f32[1024,768]{1,0:T(8,128)}, bf16[2,3,1024,128]{3,2,1,0:T(8,128)(2,1)}, bf16[4,768,768]{2,1,0:T(8,128)(2,1)}, bf16[4...) custom-call(bf16[2,3,1024,128]{3,2,1,0:T(8,128)(2,1)} %get-tuple-element.54.ctx_ref, ...), custom_call_target="tpu_custom_call" | custom-call | tf_op jit(solution)/shard_map/row_pass/pallas_call | solution.py:1077
  153.8 0.0 copy-done
  153.9 0.9 select_reduce_fusion.1.prev_ref
  154.7 0.6 reduce_max.22.last_ref
  155.3 112.2 %attend_sum.1 = (f32[1024,768]{1,0:T(8,128)}, bf16[1024,768]{1,0:T(8,128)(2,1)}, f32[96,768]{1,0:T(8,128)}, f32[96,768]{1,0:T(8,128)}, f32[192,96]{1,0:T(8,128)}...) custom-call(s32[6,96]{1,0:T(8,128)} %reduce_sum.12.idx_ref, s32[6,96]{1,0:T(8,128)} %select_reduce_fusion.1.prev_ref, ...), custom_call_target="tpu_custom_call" | custom-call | tf_op jit(solution)/shard_map/attend_sum/pallas_call | solution.py:1365
  267.6 5.6 %take_parts.1 = (f32[1,1]{1,0:T(1,128)}, f32[1024,768]{1,0:T(8,128)}, f32[3,96,192]{2,1,0:T(8,128)}, f32[3,2,8]{2,1,0:T(2,128)}, f32[192,96]{1,0:T(8,128)}, /*in...) custom-call(f32[16,768]{1,0:T(8,128)} %get-tuple-element.48.par.par_ref, ...), custom_call_target="tpu_custom_call" | custom-call | tf_op jit(solution)/shard_map/take_parts/pallas_call | solution.py:1485
  (3 shorter events, 0.0 us)
Async XLA Ops:
  97.9 55.9 %copy-start = (s32[6,96]{1,0:T(8,128)S(1)}, s32[6,96]{1,0:T(8,128)}, u32[]{:S(2)}) copy-start(s32[6,96]{1,0:T(8,128)} %reduce_sum.12.idx_ref) | copy-start | bytes 6916
